TPU v7x, 32 devices: a whole 2x2x4 slice. The times are simulated.
32 devices in a mesh: tile: 2 (over core), level: 2 (over x), member: 8 (over z, y).
Axes of the slice: x: 2, y: 2, z: 4, core: 2. Of those that a mesh axis runs over, the one named last changes fastest.
Arguments:
- temp_salt: float32 [16, 2, 2, 128, 1024], P('member', None, 'level', None, 'tile'), may hold values from -6 to 6
- diffusivity: float32 [3, 128, 1024], P(None, None, 'tile'), may hold values from -0.1 to 0.2, as said below
- wet_rank: int32 [8], P('tile'), may hold values from -1 to 3, as said below
- land_rows: int32 [1024], P('tile'), may hold values from 0 to 42
- obs_cell: int32 [1024], P(('tile', 'level')), may hold values from 0 to 65022
- obs_frac: float32 [2, 1024], P(None, ('tile', 'level')), may hold values from 0 to 1
Outputs:
- final_field: float32 [16, 2, 2, 128, 1024], P('member', None, 'level', None, 'tile')
- obs_anomaly: float32 [16, 2, 1024], P('member', None, ('tile', 'level'))
- obs_variance: float32 [2, 1024], P(None, ('tile', 'level'))
Inputs may be any that keep to these rules, and one draw needn't show every extreme that they name: `wet_rank`: -1 marks a land tile; the wet tiles carry the ranks 0 to 3 in increasing order of tile index, so exactly half of the tiles are wet. `diffusivity`: kxx and kyy positive, kxy at most half of sqrt(kxx kyy) in magnitude.
All inputs are finite; a program needn't handle non-finite values.
Results may differ from a plain program's by a relative error of at most 0.00002.
Values sent between devices are 32-bit elements; how exact they have to be, the bound alone decides.
No kernel may reach another device: no remote copies, remote signals or barrier semaphores. Data moves between devices by JAX's collectives and lax.ppermute only.
A program may use at most 192 MiB of HBM per device.

v0:
```python
import functools

import jax
import jax.numpy as jnp
from jax import lax
from jax.experimental import pallas as pl
from jax.experimental.pallas import tpu as pltpu
from jax.sharding import PartitionSpec as P


STEPS = 6
LANES = 128
PAD = 8
ALL_AXES = ("tile", "level", "member")
VMEM = pl.BlockSpec(memory_space=pltpu.VMEM)
SMEM = pl.BlockSpec(memory_space=pltpu.SMEM)
HIGHEST = lax.Precision.HIGHEST
PARAMS = pltpu.CompilerParams(vmem_limit_bytes=20 << 20)


def chunk_number():
    member = lax.axis_index("member")
    core = lax.axis_index("tile")
    low = lax.rem(member, 2)
    high = lax.rem(member // 2, 2)
    mine = jnp.where(core == 0, 2 * high + low, 2 * low + high)
    other = jnp.where(core == 0, 2 * low + high, 2 * high + low)
    return core, mine, other


def wet_mask(land_ref, rank_ref, tile, rows):
    row = lax.broadcasted_iota(jnp.int32, (rows, LANES), 0)
    land = land_ref[pl.ds(tile, 1), :]
    dry = jnp.where(rank_ref[tile] >= 0, 0, rows)
    return (row >= jnp.maximum(land, dry)).astype(jnp.float32)


def edge_block(first, last):
    lane = lax.broadcasted_iota(jnp.int32, first.shape, len(first.shape) - 1)
    return jnp.where(lane < LANES // 2, first, last)


def sums_kernel(sizes, rank_ref, temp_ref, land_ref, send_ref, keep_ref):
    members, fields, rows, tiles = sizes
    core, mine, other = chunk_number()
    send_ref[...] = jnp.zeros_like(send_ref)
    keep_ref[...] = jnp.zeros_like(keep_ref)
    for tile in range(tiles):
        lanes = slice(tile * LANES, (tile + 1) * LANES)

        @pl.when(rank_ref[tile] >= 0)
        def _():
            rank = rank_ref[tile]
            wet = wet_mask(land_ref, rank_ref, tile, rows)
            for ref, slot, field in ((keep_ref, mine, core), (send_ref, other, 1 - core)):
                total = temp_ref[field, :, lanes] * wet
                for member in range(1, members):
                    total = total + temp_ref[member * fields + field, :, lanes] * wet
                ref[jnp.bitwise_xor(slot, rank)] = total


def edges_kernel(sizes, rank_ref, temp_ref, kappa_ref, land_ref, edge_ref):
    members, fields, rows, tiles = sizes
    planes = members * fields
    wet_first = wet_mask(land_ref, rank_ref, 0, rows)
    wet_last = wet_mask(land_ref, rank_ref, tiles - 1, rows)
    last = (tiles - 1) * LANES
    for plane in range(planes):
        edge_ref[plane] = edge_block(
            temp_ref[plane, :, :LANES] * wet_first, temp_ref[plane, :, last:] * wet_last
        )
    for part in range(3):
        edge_ref[planes + part] = edge_block(kappa_ref[part, :, :LANES], kappa_ref[part, :, last:])
    edge_ref[planes + 3] = edge_block(wet_first, wet_last)


def weights_kernel(sizes, rank_ref, kappa_ref, edge_ref, land_ref, weight_ref, pad_ref):
    members, fields, rows, tiles = sizes
    base = members * fields
    ring = tiles + 1
    zeros = jnp.zeros((PAD, LANES), jnp.float32)
    inside = slice(PAD, PAD + rows)
    for part in range(4):
        for tile in range(ring):
            pad_ref[part, tile, :PAD, :] = zeros
            pad_ref[part, tile, PAD + rows :, :] = zeros
            if tile == tiles:
                pad_ref[part, tile, inside, :] = edge_ref[base + part]
            elif part == 3:
                pad_ref[part, tile, inside, :] = wet_mask(land_ref, rank_ref, tile, rows)
            else:
                pad_ref[part, tile, inside, :] = kappa_ref[part, :, tile * LANES : (tile + 1) * LANES]
    lane = lax.broadcasted_iota(jnp.int32, (8, LANES), 1)
    is_first, is_last = lane == 0, lane == LANES - 1

    def east(values):
        rolled = [pltpu.roll(x, LANES - 1, axis=1) for x in values]
        return [jnp.where(is_last, rolled[(t + 1) % ring], rolled[t]) for t in range(ring)]

    def west(values):
        rolled = [pltpu.roll(x, 1, axis=1) for x in values]
        return [jnp.where(is_first, rolled[t - 1], rolled[t]) for t in range(ring)]

    def same(values):
        return values

    def each(f, *lists):
        return [f(*values) for values in zip(*lists, strict=True)]

    def block_rows(block, carry):
        start = pl.multiple_of(PAD + 8 * block, 8)
        row0 = pl.multiple_of(8 * block, 8)

        def load(part, shift):
            return [pad_ref[part, tile, pl.ds(start + shift, 8), :] for tile in range(ring)]

        kxx, kyy, kxy, wet = (load(part, 0) for part in range(4))
        kyy_n, kxy_n, wet_n = (load(part, 1) for part in (1, 2, 3))
        kyy_s, kxy_s, wet_s = (load(part, -1) for part in (1, 2, 3))
        x_gate = each(lambda w, e: w * e, wet, east(wet))
        y_gate = each(lambda w, n: w * n, wet, wet_n)
        s_gate = each(lambda w, n: w * n, wet_s, wet)
        ax = each(lambda k, e, g: 0.5 * (k + e) * g, kxx, east(kxx), x_gate)
        cx = each(lambda k, e, g: 0.125 * (k + e) * g, kxy, east(kxy), x_gate)
        ay = each(lambda k, n, g: 0.5 * (k + n) * g, kyy, kyy_n, y_gate)
        cy = each(lambda k, n, g: 0.125 * (k + n) * g, kxy, kxy_n, y_gate)
        ays = each(lambda k, n, g: 0.5 * (k + n) * g, kyy_s, kyy, s_gate)
        cys = each(lambda k, n, g: 0.125 * (k + n) * g, kxy_s, kxy, s_gate)
        axw, cxw = west(ax), west(cx)
        groups = (
            (same, each(lambda w, a, b, c, d: 1.0 - w * (a + b + c + d), wet, ax, axw, ay, ays)),
            (same, each(lambda w, a, b, c: w * (a + b - c), wet, ay, cx, cxw)),
            (same, each(lambda w, a, b, c: w * (a - b + c), wet, ays, cx, cxw)),
            (west, each(lambda w, a, b, c: w * (a + b - c), wet, ax, cy, cys)),
            (west, each(lambda w, a, b: w * (a + b), wet, cx, cy)),
            (west, each(lambda w, a, b: w * (-a - b), wet, cx, cys)),
            (east, each(lambda w, a, b, c: w * (a - b + c), wet, axw, cy, cys)),
            (east, each(lambda w, a, b: w * (-a - b), wet, cxw, cy)),
            (east, each(lambda w, a, b: w * (a + b), wet, cxw, cys)),
        )
        for number, (move, terms) in enumerate(groups):
            for tile, term in enumerate(move(terms)):
                weight_ref[number, tile, pl.ds(row0, 8), :] = term
        return carry

    lax.fori_loop(0, rows // 8, block_rows, 0)


def run_steps(planes, rows, tiles, rank_ref, weight_ref, u_ref, part_ref):
    lane = lax.broadcasted_iota(jnp.int32, (8, LANES), 1)
    is_first, is_last = lane == 0, lane == LANES - 1
    ring = tiles + 1
    part_ref[...] = jnp.zeros_like(part_ref)

    def on_wet(tile, work):
        if tile == tiles:
            work()
        else:
            pl.when(rank_ref[tile] >= 0)(work)

    def one_step(source, target):
        for tile in range(ring):

            def spread(tile=tile):
                for block in range(rows // 8):
                    base, row0 = PAD + 8 * block, 8 * block
                    weights = [weight_ref[k, tile, row0 : row0 + 8, :] for k in range(9)]
                    for plane in range(planes):
                        here = u_ref[source, plane, tile, base : base + 8, :]
                        up = u_ref[source, plane, tile, base + 1 : base + 9, :]
                        down = u_ref[source, plane, tile, base - 1 : base + 7, :]
                        centre, to_west, to_east = (
                            weights[3 * g] * here + weights[3 * g + 1] * up + weights[3 * g + 2] * down
                            for g in range(3)
                        )
                        u_ref[target, plane, tile, base : base + 8, :] = centre
                        part_ref[0, plane, tile, row0 : row0 + 8, :] = pltpu.roll(to_west, LANES - 1, axis=1)
                        part_ref[1, plane, tile, row0 : row0 + 8, :] = pltpu.roll(to_east, 1, axis=1)

            on_wet(tile, spread)
        for tile in range(ring):

            def collect(tile=tile):
                for block in range(rows // 8):
                    base, row0 = PAD + 8 * block, 8 * block
                    at = slice(row0, row0 + 8)
                    for plane in range(planes):
                        from_east = jnp.where(
                            is_last, part_ref[0, plane, (tile + 1) % ring, at, :], part_ref[0, plane, tile, at, :]
                        )
                        from_west = jnp.where(
                            is_first, part_ref[1, plane, (tile - 1) % ring, at, :], part_ref[1, plane, tile, at, :]
                        )
                        u_ref[target, plane, tile, base : base + 8, :] = (
                            u_ref[target, plane, tile, base : base + 8, :] + from_east + from_west
                        )

            on_wet(tile, collect)

    def two_steps(_, carry):
        one_step(0, 1)
        one_step(1, 0)
        return carry

    lax.fori_loop(0, STEPS // 2, two_steps, 0)


def step_scratch(planes, rows, tiles):
    return [
        pltpu.VMEM((2, planes, tiles + 1, rows + 2 * PAD, LANES), jnp.float32),
        pltpu.VMEM((2, planes, tiles + 1, rows, LANES), jnp.float32),
    ]


def clear_pads(planes, rows, tiles, u_ref):
    zeros = jnp.zeros((PAD, LANES), jnp.float32)
    for slot in range(2):
        for plane in range(planes):
            for tile in range(tiles + 1):
                u_ref[slot, plane, tile, :PAD, :] = zeros
                u_ref[slot, plane, tile, PAD + rows :, :] = zeros


def member_kernel(sizes, first, count, rank_ref, temp_ref, edge_ref, land_ref, weight_ref, stepped_ref, u_ref, part_ref):
    _, _, rows, tiles = sizes
    clear_pads(count, rows, tiles, u_ref)
    inside = slice(PAD, PAD + rows)
    for tile in range(tiles):
        wet = wet_mask(land_ref, rank_ref, tile, rows)
        for plane in range(count):
            u_ref[0, plane, tile, inside, :] = temp_ref[first + plane, :, tile * LANES : (tile + 1) * LANES] * wet
    for plane in range(count):
        u_ref[0, plane, tiles, inside, :] = edge_ref[first + plane]
    run_steps(count, rows, tiles, rank_ref, weight_ref, u_ref, part_ref)
    for plane in range(count):
        for tile in range(tiles):
            stepped_ref[plane, :, tile * LANES : (tile + 1) * LANES] = u_ref[0, plane, tile, inside, :]


def observe_planes(fields, cell, frac):
    rows, columns = fields[0].shape
    count = cell.shape[1]
    frac_east, frac_north = frac[0:1, :], frac[1:2, :]
    column, row = lax.rem(cell, columns), lax.rem(cell // columns, rows)
    at = lax.broadcasted_iota(jnp.int32, (columns, count), 0) - column
    pick = jnp.where(at == 0, 1.0 - frac_east, jnp.where(at == 1, frac_east, 0.0))
    values = jnp.concatenate(fields, axis=0)
    picked = jnp.dot(values, pick, precision=HIGHEST, preferred_element_type=jnp.float32)
    at = lax.broadcasted_iota(jnp.int32, (rows, count), 0) - row
    pick = jnp.where(at == 0, 1.0 - frac_north, jnp.where(at == 1, frac_north, 0.0))
    return [
        jnp.sum(picked[number * rows : (number + 1) * rows] * pick, axis=0, keepdims=True)
        for number in range(len(fields))
    ]


def observe_kernel(cell_ref, frac_ref, *refs):
    stepped_refs, seen_ref = refs[:-1], refs[-1]
    fields = [ref[plane] for ref in stepped_refs for plane in range(ref.shape[0])]
    halves = cell_ref.shape[1] // LANES
    for plane, seen in enumerate(observe_planes(fields, cell_ref[...], frac_ref[...])):
        for half in range(halves):
            at = plane * halves + half
            seen_ref[at : at + 1, :] = seen[:, half * LANES : (half + 1) * LANES]


def final_kernel(
    sizes, samples, ensemble, slots,
    rank_ref, mine_ref, other_ref, edge_ref, land_ref, weight_ref, cell_ref, frac_ref, seen_ref, stepped_refs,
    field_ref, anomaly_ref, variance_ref, u_ref, part_ref, mean_ref,
):
    members, fields, rows, tiles = sizes
    core, mine, other = chunk_number()
    owned = jnp.int32(0)
    for tile in range(tiles):
        owned = owned + (rank_ref[tile] >= 0).astype(jnp.int32)
    first_rank = jnp.clip(jnp.where(core == 0, owned, 0), 0, slots - 1)
    last_rank = jnp.clip(jnp.where(core == 0, slots - 1, slots - owned - 1), 0, slots - 1)
    clear_pads(fields, rows, tiles, u_ref)
    wet_edge = edge_ref[members * fields + 3]
    scale = 1.0 / samples

    def total(field, rank):
        own = mine_ref[jnp.bitwise_xor(mine, rank)]
        theirs = other_ref[jnp.bitwise_xor(other, rank)]
        return jnp.where(core == field, own, theirs) * scale

    inside = slice(PAD, PAD + rows)
    for tile in range(tiles):
        rank = rank_ref[tile]
        wet = wet_mask(land_ref, rank_ref, tile, rows)
        for field in range(fields):
            u_ref[0, field, tile, inside, :] = total(field, jnp.maximum(rank, 0)) * wet
    for field in range(fields):
        u_ref[0, field, tiles, inside, :] = (
            edge_block(total(field, first_rank), total(field, last_rank)) * wet_edge
        )
    run_steps(fields, rows, tiles, rank_ref, weight_ref, u_ref, part_ref)
    per_ref = field_ref.shape[0] // len(stepped_refs)
    for field in range(fields):
        for tile in range(tiles):
            lanes = slice(tile * LANES, (tile + 1) * LANES)
            mean = u_ref[0, field, tile, inside, :]
            mean_ref[field, :, lanes] = mean
            for member in range(members):
                plane = member * fields + field
                field_ref[plane, :, lanes] = stepped_refs[plane // per_ref][plane % per_ref, :, lanes] - mean
    mean_seen = observe_planes([mean_ref[field] for field in range(fields)], cell_ref[...], frac_ref[...])
    halves = cell_ref.shape[1] // LANES
    stride = members * fields * halves
    sets = seen_ref.shape[0] // stride

    def tree(values):
        while len(values) > 1:
            values = [a + b for a, b in zip(values[0::2], values[1::2], strict=True)]
        return values[0]

    for field in range(fields):
        for half in range(halves):
            lanes = slice(half * LANES, (half + 1) * LANES)
            mean = mean_seen[field][:, lanes]
            observed = []
            for part in range(sets):
                for member in range(members):
                    at = part * stride + (member * fields + field) * halves + half
                    observed.append(seen_ref[at : at + 1, :] - mean)
            centre = tree(observed) / ensemble
            anomaly = [value - centre for value in observed]
            variance_ref[field : field + 1, lanes] = tree([value * value for value in anomaly]) / ensemble
            for member in range(members):
                anomaly_ref[member, field : field + 1, lanes] = anomaly[member]


def local(temp_salt, diffusivity, wet_rank, land_rows, obs_cell, obs_frac):
    members, fields, levels, rows, columns = temp_salt.shape
    tiles = wet_rank.shape[0]
    cores, level_count, member_count = (lax.axis_size(axis) for axis in ALL_AXES)
    slots = tiles * cores // 2
    chips = level_count * member_count
    bits = chips.bit_length() - 1
    assert cores == 2 and fields == 2 and levels == 1 and slots == 4
    assert columns == tiles * LANES and chips == 1 << bits and bits >= 3
    count = obs_cell.shape[0]
    planes = members * fields
    sizes = (members, fields, rows, tiles)
    samples = members * levels * chips
    level_bit = bits - 1

    def device(core, chip):
        return core * chips + chip

    def exchange(value, masks):
        if masks is None:
            to = lambda core, chip: (1 - core, chip)
        else:
            to = lambda core, chip: (core, chip ^ masks[core])
        pairs = [(device(core, chip), device(*to(core, chip))) for core in range(2) for chip in range(chips)]
        return lax.ppermute(value, ALL_AXES, pairs)

    def struct(*shape):
        return jax.ShapeDtypeStruct(shape, jnp.float32)

    def call(kernel, out_shape, operands, scratch=(), cycles=1000):
        out_specs = jax.tree.map(lambda _: VMEM, out_shape)
        return pl.pallas_call(
            kernel,
            out_shape=out_shape,
            in_specs=[SMEM if x is wet_rank else VMEM for x in operands],
            out_specs=out_specs,
            scratch_shapes=list(scratch),
            compiler_params=PARAMS,
            cost_estimate=pl.CostEstimate(flops=cycles * 4096, bytes_accessed=1 << 20, transcendentals=0),
        )(*operands)

    temp = temp_salt.reshape(planes, rows, columns)
    land = land_rows.reshape(tiles, LANES)
    cell = obs_cell.reshape(1, count)
    masks = {1: (1, 2), 2: (2, 1), 3: (3, 3)}

    send, keep = call(
        functools.partial(sums_kernel, sizes),
        (struct(slots, rows, LANES), struct(slots, rows, LANES)), (wet_rank, temp, land),
    )
    arrived = exchange(send, None)
    edge = call(
        functools.partial(edges_kernel, sizes),
        struct(planes + 4, rows, LANES), (wet_rank, temp, diffusivity, land),
    )
    edges = exchange(edge, None)
    total = keep + arrived
    got = [exchange(total[k], masks[k]) for k in (1, 2, 3)]
    total = (total[0] + got[0]) + (got[1] + got[2])

    weights = call(
        functools.partial(weights_kernel, sizes),
        struct(9, tiles + 1, rows, LANES), (wet_rank, diffusivity, edges, land),
        [pltpu.VMEM((4, tiles + 1, rows + 2 * PAD, LANES), jnp.float32)],
    )
    per_call = 2
    stepped = [
        call(
            functools.partial(member_kernel, sizes, first, per_call),
            struct(per_call, rows, columns), (wet_rank, temp, edges, land, weights),
            step_scratch(per_call, rows, tiles), cycles=4000,
        )
        for first in range(0, planes, per_call)
    ]
    seen = call(
        observe_kernel,
        struct(planes * count // LANES, LANES), (cell, obs_frac, *stepped), cycles=2000,
    )

    for bit in [level_bit] + list(range(2, level_bit)):
        mask = (1 << bit, 1 << bit)
        if bit == level_bit:
            total = total + exchange(total, mask)
        else:
            got = exchange(jnp.concatenate([total, seen], axis=0), mask)
            total = total + got[:rows]
            seen = jnp.concatenate([seen, got[rows:]], axis=0)
    payload = jnp.concatenate([total, seen], axis=0)
    got = [payload] + [exchange(payload, masks[k]) for k in (1, 2, 3)]
    mine = jnp.stack([x[:rows] for x in got])
    theirs = exchange(mine, None)
    seen = jnp.concatenate([x[rows:] for x in got], axis=0)

    def last_kernel(*refs):
        fixed, rest = refs[:9], refs[9:]
        final_kernel(
            sizes, samples, members * member_count, slots, *fixed, rest[: len(stepped)], *rest[len(stepped) :]
        )

    field, anomaly, variance = call(
        last_kernel,
        (struct(planes, rows, columns), struct(members, fields, count), struct(fields, count)),
        (wet_rank, mine, theirs, edges, land, weights, cell, obs_frac, seen, *stepped),
        step_scratch(fields, rows, tiles) + [pltpu.VMEM((fields, rows, columns), jnp.float32)],
    )
    return field.reshape(members, fields, levels, rows, columns), anomaly, variance


def solution(mesh):
    placed = (
        P("member", None, "level", None, "tile"),
        P(None, None, "tile"),
        P("tile"),
        P("tile"),
        P(("tile", "level")),
        P(None, ("tile", "level")),
    )

    return jax.shard_map(
        local,
        mesh=mesh,
        in_specs=placed,
        out_specs=(
            P("member", None, "level", None, "tile"),
            P("member", None, ("tile", "level")),
            P(None, ("tile", "level")),
        ),
        check_vma=False,
    )
```

profile of v0, /device:TPU:0, one launch (start us, length us, event | category | flops | bytes accessed | tf_op | source)
XLA Modules:
  0.0 53.2 jit_solution(550310117614945363)
XLA Ops:
  0.6 0.0 copy-start.6
  0.6 0.0 copy-start
  0.7 1.2 %copy-done = f32[2,2,1,128,512]{4,3,2,1,0:T(8,128)S(1)} copy-done((f32[2,2,1,128,512]{4,3,2,1,0:T(8,128)S(1)}, f32[2,2,1,128,512]{4,3,2,1,0:T(8,128)}, u32[]{:S(2)}) %copy-start) | copy-done | bytes 1048600
  1.9 0.0 copy-start.4
  1.9 0.7 %copy-done.4 = s32[512]{0:T(512)S(1)} copy-done((s32[512]{0:T(512)S(1)}, s32[512]{0:T(512)}, u32[]{:S(2)}) %copy-start.4) | copy-done | bytes 2072
  2.6 0.0 copy-start.7
  2.6 0.7 %copy-done.7 = s32[4]{0:T(128)S(1)} copy-done((s32[4]{0:T(128)S(1)}, s32[4]{0:T(128)}, u32[]{:S(2)}) %copy-start.7) | copy-done | bytes 40
  3.2 0.0 copy-start.3
  3.2 0.7 %shard_map.85 = (f32[4,128,128]{2,1,0:T(8,128)S(1)}, f32[4,128,128]{2,1,0:T(8,128)S(1)}) custom-call(s32[4]{0:T(128)S(1)} %copy-done.7, f32[4,128,512]{2,1,0:T(8,128)S(1)} %bitcast.25, s32[4,128]{1,0:T(4,128)S(1)} %bitcast.29), custom_call_target="tpu_custom_call" | custom-call | flops 4096000 | bytes 1048576 | tf_op jit(solution)/shard_map/pallas_call | solution.py:365
  3.9 0.6 %collective-permute-start = (f32[4,128,128]{2,1,0:T(8,128)S(1)}, f32[4,128,128]{2,1,0:T(8,128)S(1)}, u32[]{:S(2)}, u32[]{:S(2)}) collective-permute-start(f32[4,128,128]{2,1,0:T(8,128)S(1)} %get-tuple-element.9), channel_id=1, source_target_pairs={{0,16},{1,17},{2,18},{3,19},{4,20},{5,21},{6,22},{7,23},{8,24},{9,... | collective-permute-start | bytes 786440 | tf_op jit(solution)/shard_map/ppermute | solution.py:358
  4.4 1.1 %copy-done.2 = f32[3,128,512]{2,1,0:T(8,128)S(1)} copy-done((f32[3,128,512]{2,1,0:T(8,128)S(1)}, f32[3,128,512]{2,1,0:T(8,128)}, u32[]{:S(2)}) %copy-start.2) | copy-done | bytes 786456
  5.6 0.0 copy-start.5
  5.6 0.7 %copy-done.5 = s32[512]{0:T(512)S(1)} copy-done((s32[512]{0:T(512)S(1)}, s32[512]{0:T(512)}, u32[]{:S(2)}) %copy-start.5) | copy-done | bytes 2072
  6.3 0.6 %shard_map.86 = f32[8,128,128]{2,1,0:T(8,128)S(1)} custom-call(s32[4]{0:T(128)S(1)} %copy-done.7, f32[4,128,512]{2,1,0:T(8,128)S(1)} %bitcast.26, f32[3,128,512]{2,1,0:T(8,128)S(1)} %copy-done.2, s32[4,128]{1,0:T(4,128)S(1)} %bitcast.30), custom_call_target="tpu_custom_call" | custom-call | flops 4096000 | bytes 1048576 | tf_op jit(solution)/shard_map/pallas_call | solution.py:365
  6.9 0.1 collective-permute-start.5
  7.0 0.0 collective-permute-done
  7.0 0.0 copy-start.1
  7.0 4.1 %collective-permute-start.3 = (f32[128,128]{1,0:T(8,128)S(1)}, f32[128,128]{1,0:T(8,128)S(1)}, u32[]{:S(2)}, u32[]{:S(2)}) collective-permute-start(f32[128,128]{1,0:T(8,128)S(1)} %get-tuple-element.16), channel_id=1, source_target_pairs={{0,3},{1,2},{2,1},{3,0},{4,7},{5,6},{6,5},{7,4},{8,11},{9,10},{10,... | collective-permute-start | bytes 196616 | tf_op jit(solution)/shard_map/ppermute | solution.py:358
  11.1 0.4 collective-permute-start.2
  11.6 0.2 collective-permute-start.1
  11.7 1.6 %collective-permute-done.3 = f32[128,128]{1,0:T(8,128)S(1)} collective-permute-done((f32[128,128]{1,0:T(8,128)S(1)}, f32[128,128]{1,0:T(8,128)S(1)}, u32[]{:S(2)}, u32[]{:S(2)}) %collective-permute-start.3) | collective-permute-done | bytes 65568 | tf_op jit(solution)/shard_map/ppermute | solution.py:358
  13.4 2.0 %collective-permute-done.2 = f32[128,128]{1,0:T(8,128)S(1)} collective-permute-done((f32[128,128]{1,0:T(8,128)S(1)}, f32[128,128]{1,0:T(8,128)S(1)}, u32[]{:S(2)}, u32[]{:S(2)}) %collective-permute-start.2) | collective-permute-done | bytes 65568 | tf_op jit(solution)/shard_map/ppermute | solution.py:358
  15.4 0.4 collective-permute-done.1
  15.8 1.6 %collective-permute-start.4 = (f32[128,128]{1,0:T(8,128)S(1)}, f32[128,128]{1,0:T(8,128)S(1)}, u32[]{:S(2)}, u32[]{:S(2)}) collective-permute-start(f32[128,128]{1,0:T(8,128)S(1)} %fusion.1), channel_id=1, source_target_pairs={{0,8},{1,9},{2,10},{3,11},{4,12},{5,13},{6,14},{7,15},{8,0},{9,1},... | collective-permute-start | bytes 196616 | tf_op jit(solution)/shard_map/ppermute | solution.py:358
  17.4 2.8 %collective-permute-done.4 = f32[128,128]{1,0:T(8,128)S(1)} collective-permute-done((f32[128,128]{1,0:T(8,128)S(1)}, f32[128,128]{1,0:T(8,128)S(1)}, u32[]{:S(2)}, u32[]{:S(2)}) %collective-permute-start.4) | collective-permute-done | bytes 65568 | tf_op jit(solution)/shard_map/ppermute | solution.py:358
  20.2 0.0 collective-permute-done.5.edge_ref.refs_3_
  20.2 0.0 copy-done.6
  20.2 0.0 copy-done.3
  20.2 4.6 %shard_map.87.weight_ref.refs_5_ = f32[9,5,128,128]{3,2,1,0:T(8,128)S(1)} custom-call(s32[4]{0:T(128)S(1)} %copy-done.7, f32[3,128,512]{2,1,0:T(8,128)S(1)} %copy-done.3, f32[8,128,128]{2,1,0:T(8,128)S(1)} %collective-permute-done.5.edge_ref.refs_3_, s32[4,128]{1,0:T(4,128)S(1)} %bitcast.31), custom_call_target="tpu_custom_call" | custom-call | flops 4096000 | bytes 1048576 | tf_op jit(solution)/shard_map/pallas_call | solution.py:365
  24.8 0.0 copy-done.1
  24.8 3.9 %shard_map.89.refs_1_.refs_10_ = f32[2,128,512]{2,1,0:T(8,128)S(1)} custom-call(s32[4]{0:T(128)S(1)} %copy-done.7, f32[4,128,512]{2,1,0:T(8,128)S(1)} %bitcast.27, f32[8,128,128]{2,1,0:T(8,128)S(1)} %collective-permute-done.5.edge_ref.refs_3_, s32[4,128]{1,0:T(4,128)S(1)} %bitcast.32, f32[9,5,128,128]{3,2,1,0:T(8,128)S(1)} %shard_map.87.weight_ref.refs_5_), custom_call_target="tpu_custom_call" | custom-call | flops 16384000 | bytes 1048576 | tf_op jit(solution)/shard_map/pallas_call | solution.py:365
  28.8 0.0 copy-start.8
  28.8 0.0 copy-start.9
  28.8 3.9 %shard_map.88.refs_0_.refs_9_ = f32[2,128,512]{2,1,0:T(8,128)S(1)} custom-call(s32[4]{0:T(128)S(1)} %copy-done.7, f32[4,128,512]{2,1,0:T(8,128)S(1)} %bitcast.28, f32[8,128,128]{2,1,0:T(8,128)S(1)} %collective-permute-done.5.edge_ref.refs_3_, s32[4,128]{1,0:T(4,128)S(1)} %bitcast.33, f32[9,5,128,128]{3,2,1,0:T(8,128)S(1)} %shard_map.87.weight_ref.refs_5_), custom_call_target="tpu_custom_call" | custom-call | flops 16384000 | bytes 1048576 | tf_op jit(solution)/shard_map/pallas_call | solution.py:365
  32.7 0.0 copy-done.8
  32.7 0.0 copy-done.9
  32.8 1.2 %shard_map.90 = f32[8,128]{1,0:T(8,128)S(1)} custom-call(s32[1,256]{1,0:T(1,128)S(1)} %bitcast.35, f32[2,256]{1,0:T(2,128)S(1)} %copy-done.8, f32[2,128,512]{2,1,0:T(8,128)S(1)} %shard_map.88.refs_0_.refs_9_, f32[2,128,512]{2,1,0:T(8,128)S(1)} %shard_map.89.refs_1_.refs_10_), custom_call_target="tpu_custom_call" | custom-call | flops 8192000 | bytes 1048576 | tf_op jit(solution)/shard_map/pallas_call | solution.py:365
  34.0 2.7 %collective-permute-start.6 = (f32[136,128]{1,0:T(8,128)S(1)}, f32[136,128]{1,0:T(8,128)S(1)}, u32[]{:S(2)}, u32[]{:S(2)}) collective-permute-start(f32[136,128]{1,0:T(8,128)S(1)} %pad_maximum_fusion.2), channel_id=1, source_target_pairs={{0,4},{1,5},{2,6},{3,7},{4,0},{5,1},{6,2},{7,3},{8,12},{9,13},{10,... | collective-permute-start | bytes 208904 | tf_op jit(solution)/shard_map/ppermute | solution.py:358
  36.6 2.6 %collective-permute-done.6 = f32[136,128]{1,0:T(8,128)S(1)} collective-permute-done((f32[136,128]{1,0:T(8,128)S(1)}, f32[136,128]{1,0:T(8,128)S(1)}, u32[]{:S(2)}, u32[]{:S(2)}) %collective-permute-start.6) | collective-permute-done | bytes 69664 | tf_op jit(solution)/shard_map/ppermute | solution.py:358
  39.3 1.7 %collective-permute-start.9 = (f32[144,128]{1,0:T(8,128)S(1)}, f32[144,128]{1,0:T(8,128)S(1)}, u32[]{:S(2)}, u32[]{:S(2)}) collective-permute-start(f32[144,128]{1,0:T(8,128)S(1)} %pad_maximum_fusion.1), channel_id=1, source_target_pairs={{0,3},{1,2},{2,1},{3,0},{4,7},{5,6},{6,5},{7,4},{8,11},{9,10},{10,... | collective-permute-start | bytes 221192 | tf_op jit(solution)/shard_map/ppermute | solution.py:358
  41.0 0.6 %collective-permute-start.8 = (f32[144,128]{1,0:T(8,128)S(1)}, f32[144,128]{1,0:T(8,128)S(1)}, u32[]{:S(2)}, u32[]{:S(2)}) collective-permute-start(f32[144,128]{1,0:T(8,128)S(1)} %pad_maximum_fusion.1), channel_id=1, source_target_pairs={{0,2},{1,3},{2,0},{3,1},{4,6},{5,7},{6,4},{7,5},{8,10},{9,11},{10,... | collective-permute-start | bytes 221192 | tf_op jit(solution)/shard_map/ppermute | solution.py:358
  41.6 1.3 %collective-permute-start.7 = (f32[144,128]{1,0:T(8,128)S(1)}, f32[144,128]{1,0:T(8,128)S(1)}, u32[]{:S(2)}, u32[]{:S(2)}) collective-permute-start(f32[144,128]{1,0:T(8,128)S(1)} %pad_maximum_fusion.1), channel_id=1, source_target_pairs={{0,1},{1,0},{2,3},{3,2},{4,5},{5,4},{6,7},{7,6},{8,9},{9,8},{10,11... | collective-permute-start | bytes 221192 | tf_op jit(solution)/shard_map/ppermute | solution.py:358
  42.8 1.8 %collective-permute-done.9 = f32[144,128]{1,0:T(8,128)S(1)} collective-permute-done((f32[144,128]{1,0:T(8,128)S(1)}, f32[144,128]{1,0:T(8,128)S(1)}, u32[]{:S(2)}, u32[]{:S(2)}) %collective-permute-start.9) | collective-permute-done | bytes 73760 | tf_op jit(solution)/shard_map/ppermute | solution.py:358
  44.6 0.7 %collective-permute-done.8 = f32[144,128]{1,0:T(8,128)S(1)} collective-permute-done((f32[144,128]{1,0:T(8,128)S(1)}, f32[144,128]{1,0:T(8,128)S(1)}, u32[]{:S(2)}, u32[]{:S(2)}) %collective-permute-start.8) | collective-permute-done | bytes 73760 | tf_op jit(solution)/shard_map/ppermute | solution.py:358
  45.3 0.6 %collective-permute-done.7 = f32[144,128]{1,0:T(8,128)S(1)} collective-permute-done((f32[144,128]{1,0:T(8,128)S(1)}, f32[144,128]{1,0:T(8,128)S(1)}, u32[]{:S(2)}, u32[]{:S(2)}) %collective-permute-start.7) | collective-permute-done | bytes 73760 | tf_op jit(solution)/shard_map/ppermute | solution.py:358
  46.0 0.1 collective-permute-start.10
  46.1 1.5 %collective-permute-done.10.refs_2_ = f32[4,128,128]{2,1,0:T(8,128)S(1)} collective-permute-done((f32[4,128,128]{2,1,0:T(8,128)S(1)}, f32[4,128,128]{2,1,0:T(8,128)S(1)}, u32[]{:S(2)}, u32[]{:S(2)}) %collective-permute-start.10) | collective-permute-done | bytes 262176 | tf_op jit(solution)/shard_map/ppermute | solution.py:358
  47.6 5.6 %shard_map.91 = (f32[4,128,512]{2,1,0:T(8,128)}, f32[2,2,256]{2,1,0:T(2,128)}, f32[2,256]{1,0:T(2,128)}) custom-call(s32[4]{0:T(128)S(1)} %copy-done.7, f32[4,128,128]{2,1,0:T(8,128)S(1)} %pad_maximum_fusion.refs_1_, f32[4,128,128]{2,1,0:T(8,128)S(1)} %collective-permute-done.10.refs_2_, f32[8,128,128]{2,1,0:T(8,128)S(1)} %collective-permute-done.5.edge_ref.refs_3_, ...), custom_call_target="tpu_custom_call" | custom-call | flops 4096000 | bytes 1048576 | tf_op jit(solution)/shard_map/pallas_call | solution.py:365
  (17 shorter events, 0.2 us)
Async XLA Ops:
  0.6 19.6 %copy-start.6 = (s32[512]{0:T(512)S(1)}, s32[512]{0:T(512)}, u32[]{:S(2)}) copy-start(s32[512]{0:T(512)} %param.9) | copy-start | bytes 6148
  0.6 1.2 %copy-start = (f32[2,2,1,128,512]{4,3,2,1,0:T(8,128)S(1)}, f32[2,2,1,128,512]{4,3,2,1,0:T(8,128)}, u32[]{:S(2)}) copy-start(f32[2,2,1,128,512]{4,3,2,1,0:T(8,128)} %param.6) | copy-start | bytes 3145732
  1.9 0.7 %copy-start.4 = (s32[512]{0:T(512)S(1)}, s32[512]{0:T(512)}, u32[]{:S(2)}) copy-start(s32[512]{0:T(512)} %param.9) | copy-start | bytes 6148
  2.6 0.7 %copy-start.7 = (s32[4]{0:T(128)S(1)}, s32[4]{0:T(128)}, u32[]{:S(2)}) copy-start(s32[4]{0:T(128)} %refs_0_.1) | copy-start | bytes 52
  3.2 17.0 %copy-start.3 = (f32[3,128,512]{2,1,0:T(8,128)S(1)}, f32[3,128,512]{2,1,0:T(8,128)}, u32[]{:S(2)}) copy-start(f32[3,128,512]{2,1,0:T(8,128)} %kappa_ref.3) | copy-start | bytes 2359300
  3.9 3.1 %collective-permute-start = (f32[4,128,128]{2,1,0:T(8,128)S(1)}, f32[4,128,128]{2,1,0:T(8,128)S(1)}, u32[]{:S(2)}, u32[]{:S(2)}) collective-permute-start(f32[4,128,128]{2,1,0:T(8,128)S(1)} %get-tuple-element.9), channel_id=1, source_target_pairs={{0,16},{1,17},{2,18},{3,19},{4,20},{5,21},{6,22},{7,23},{8,24},{9,... | collective-permute-start | bytes 786440 | tf_op jit(solution)/shard_map/ppermute | solution.py:358
  4.4 1.1 %copy-start.2 = (f32[3,128,512]{2,1,0:T(8,128)S(1)}, f32[3,128,512]{2,1,0:T(8,128)}, u32[]{:S(2)}) copy-start(f32[3,128,512]{2,1,0:T(8,128)} %kappa_ref.3) | copy-start | bytes 2359300
  5.6 0.7 %copy-start.5 = (s32[512]{0:T(512)S(1)}, s32[512]{0:T(512)}, u32[]{:S(2)}) copy-start(s32[512]{0:T(512)} %param.9) | copy-start | bytes 6148
  6.9 13.3 %collective-permute-start.5 = (f32[8,128,128]{2,1,0:T(8,128)S(1)}, f32[8,128,128]{2,1,0:T(8,128)S(1)}, u32[]{:S(2)}, u32[]{:S(2)}) collective-permute-start(f32[8,128,128]{2,1,0:T(8,128)S(1)} %shard_map.86), channel_id=1, source_target_pairs={{0,16},{1,17},{2,18},{3,19},{4,20},{5,21},{6,22},{7,23},{8,24},{9,... | collective-permute-start | bytes 1572872 | tf_op jit(solution)/shard_map/ppermute | solution.py:358
  7.0 17.9 %copy-start.1 = (f32[2,2,1,128,512]{4,3,2,1,0:T(8,128)S(1)}, f32[2,2,1,128,512]{4,3,2,1,0:T(8,128)}, u32[]{:S(2)}) copy-start(f32[2,2,1,128,512]{4,3,2,1,0:T(8,128)} %param.6) | copy-start | bytes 3145732
  7.0 6.3 %collective-permute-start.3 = (f32[128,128]{1,0:T(8,128)S(1)}, f32[128,128]{1,0:T(8,128)S(1)}, u32[]{:S(2)}, u32[]{:S(2)}) collective-permute-start(f32[128,128]{1,0:T(8,128)S(1)} %get-tuple-element.16), channel_id=1, source_target_pairs={{0,3},{1,2},{2,1},{3,0},{4,7},{5,6},{6,5},{7,4},{8,11},{9,10},{10,... | collective-permute-start | bytes 196616 | tf_op jit(solution)/shard_map/ppermute | solution.py:358
  11.1 4.3 %collective-permute-start.2 = (f32[128,128]{1,0:T(8,128)S(1)}, f32[128,128]{1,0:T(8,128)S(1)}, u32[]{:S(2)}, u32[]{:S(2)}) collective-permute-start(f32[128,128]{1,0:T(8,128)S(1)} %get-tuple-element.17), channel_id=1, source_target_pairs={{0,2},{1,3},{2,0},{3,1},{4,6},{5,7},{6,4},{7,5},{8,10},{9,11},{10,... | collective-permute-start | bytes 196616 | tf_op jit(solution)/shard_map/ppermute | solution.py:358
  11.6 4.3 %collective-permute-start.1 = (f32[128,128]{1,0:T(8,128)S(1)}, f32[128,128]{1,0:T(8,128)S(1)}, u32[]{:S(2)}, u32[]{:S(2)}) collective-permute-start(f32[128,128]{1,0:T(8,128)S(1)} %get-tuple-element.18), channel_id=1, source_target_pairs={{0,1},{1,0},{2,3},{3,2},{4,5},{5,4},{6,7},{7,6},{8,9},{9,8},{10,11... | collective-permute-start | bytes 196616 | tf_op jit(solution)/shard_map/ppermute | solution.py:358
  15.8 4.3 %collective-permute-start.4 = (f32[128,128]{1,0:T(8,128)S(1)}, f32[128,128]{1,0:T(8,128)S(1)}, u32[]{:S(2)}, u32[]{:S(2)}) collective-permute-start(f32[128,128]{1,0:T(8,128)S(1)} %fusion.1), channel_id=1, source_target_pairs={{0,8},{1,9},{2,10},{3,11},{4,12},{5,13},{6,14},{7,15},{8,0},{9,1},... | collective-permute-start | bytes 196616 | tf_op jit(solution)/shard_map/ppermute | solution.py:358
  28.8 4.0 %copy-start.8 = (f32[2,256]{1,0:T(2,128)S(1)}, f32[2,256]{1,0:T(2,128)}, u32[]{:S(2)}) copy-start(f32[2,256]{1,0:T(2,128)} %refs_7_.1) | copy-start | bytes 6148
  28.8 4.0 %copy-start.9 = (s32[256]{0:T(256)S(1)}, s32[256]{0:T(256)}, u32[]{:S(2)}) copy-start(s32[256]{0:T(256)} %param.10) | copy-start | bytes 3076
  34.0 5.3 %collective-permute-start.6 = (f32[136,128]{1,0:T(8,128)S(1)}, f32[136,128]{1,0:T(8,128)S(1)}, u32[]{:S(2)}, u32[]{:S(2)}) collective-permute-start(f32[136,128]{1,0:T(8,128)S(1)} %pad_maximum_fusion.2), channel_id=1, source_target_pairs={{0,4},{1,5},{2,6},{3,7},{4,0},{5,1},{6,2},{7,3},{8,12},{9,13},{10,... | collective-permute-start | bytes 208904 | tf_op jit(solution)/shard_map/ppermute | solution.py:358
  39.3 5.3 %collective-permute-start.9 = (f32[144,128]{1,0:T(8,128)S(1)}, f32[144,128]{1,0:T(8,128)S(1)}, u32[]{:S(2)}, u32[]{:S(2)}) collective-permute-start(f32[144,128]{1,0:T(8,128)S(1)} %pad_maximum_fusion.1), channel_id=1, source_target_pairs={{0,3},{1,2},{2,1},{3,0},{4,7},{5,6},{6,5},{7,4},{8,11},{9,10},{10,... | collective-permute-start | bytes 221192 | tf_op jit(solution)/shard_map/ppermute | solution.py:358
  41.0 4.4 %collective-permute-start.8 = (f32[144,128]{1,0:T(8,128)S(1)}, f32[144,128]{1,0:T(8,128)S(1)}, u32[]{:S(2)}, u32[]{:S(2)}) collective-permute-start(f32[144,128]{1,0:T(8,128)S(1)} %pad_maximum_fusion.1), channel_id=1, source_target_pairs={{0,2},{1,3},{2,0},{3,1},{4,6},{5,7},{6,4},{7,5},{8,10},{9,11},{10,... | collective-permute-start | bytes 221192 | tf_op jit(solution)/shard_map/ppermute | solution.py:358
  41.6 4.4 %collective-permute-start.7 = (f32[144,128]{1,0:T(8,128)S(1)}, f32[144,128]{1,0:T(8,128)S(1)}, u32[]{:S(2)}, u32[]{:S(2)}) collective-permute-start(f32[144,128]{1,0:T(8,128)S(1)} %pad_maximum_fusion.1), channel_id=1, source_target_pairs={{0,1},{1,0},{2,3},{3,2},{4,5},{5,4},{6,7},{7,6},{8,9},{9,8},{10,11... | collective-permute-start | bytes 221192 | tf_op jit(solution)/shard_map/ppermute | solution.py:358
  46.0 1.6 %collective-permute-start.10 = (f32[4,128,128]{2,1,0:T(8,128)S(1)}, f32[4,128,128]{2,1,0:T(8,128)S(1)}, u32[]{:S(2)}, u32[]{:S(2)}) collective-permute-start(f32[4,128,128]{2,1,0:T(8,128)S(1)} %pad_maximum_fusion.refs_1_), channel_id=1, source_target_pairs={{0,16},{1,17},{2,18},{3,19},{4,20},{5,21},{6,22},{7,23},{8,24},{9,... | collective-permute-start | bytes 786440 | tf_op jit(solution)/shard_map/ppermute | solution.py:358
where the time goes:
time: 53.4 us; the launch traced here: 53.2 us
  Pallas kernels  20.5 us (38%)
  waiting for transfers between devices  14 us (26%)
  starting transfers between devices  13.2 us (25%)
  local copies, waits for them, and re-layouts  4.45 us (8%)
  between operations  0.86 us (2%)
    pallas_call x7, Pallas kernels, call(): pl.pallas_call(kernel, out_shape=out_shape, in_specs=[SMEM if x is wet_ra...  20.5 us
    ppermute x11, waiting for transfers between devices, exchange(): return lax.ppermute(value, ALL_AXES, pairs)  14 us
    ppermute x11, starting transfers between devices, exchange(): return lax.ppermute(value, ALL_AXES, pairs)  13.2 us
    unnamed x24, local copies, waits for them, and re-layouts  4.41 us
  transfers between devices with their start and end apart: 11, of which 9 were waited for; matrix products, arithmetic and copies ran while one was open for 0% of the time, Pallas kernels for 1%

commit v1 on v0

v1 whole, which is shorter than its diff:
```python
import functools

import jax
import jax.numpy as jnp
from jax import lax
from jax.experimental import pallas as pl
from jax.experimental.pallas import tpu as pltpu
from jax.sharding import PartitionSpec as P


STEPS = 6
LANES = 128
PAD = 8
ALL_AXES = ("tile", "level", "member")
VMEM = pl.BlockSpec(memory_space=pltpu.VMEM)
SMEM = pl.BlockSpec(memory_space=pltpu.SMEM)
HBM = pl.BlockSpec(memory_space=pltpu.HBM)
HIGHEST = lax.Precision.HIGHEST
PARAMS = pltpu.CompilerParams(vmem_limit_bytes=20 << 20)


def chunk_number():
    member = lax.axis_index("member")
    core = lax.axis_index("tile")
    low = lax.rem(member, 2)
    high = lax.rem(member // 2, 2)
    mine = jnp.where(core == 0, 2 * high + low, 2 * low + high)
    other = jnp.where(core == 0, 2 * low + high, 2 * high + low)
    return core, mine, other


def wet_mask(land_ref, rank_ref, tile, rows):
    row = lax.broadcasted_iota(jnp.int32, (rows, LANES), 0)
    land = land_ref[pl.ds(tile, 1), :]
    dry = jnp.where(rank_ref[tile] >= 0, 0, rows)
    return (row >= jnp.maximum(land, dry)).astype(jnp.float32)


def slot_owner(rank_ref, slot, tiles):
    tile, owned = jnp.int32(0), jnp.int32(0)
    for t in range(tiles):
        here = (rank_ref[t] == slot).astype(jnp.int32)
        owned, tile = owned + here, tile + t * here
    return owned > 0, tile


def tile_lanes(tile):
    return pl.ds(pl.multiple_of(tile * LANES, LANES), LANES)


def signed_number(land_ref, rank_ref, core, tile, rows, tiles):
    number = (core * tiles + tile + 1).astype(jnp.float32)
    return (2.0 * wet_mask(land_ref, rank_ref, tile, rows) - 1.0) * number


def sums_kernel(sizes, rank_hbm, temp_hbm, land_hbm, send_ref, keep_ref, rank_ref, temp_ref, land_ref, sem):
    members, fields, rows, tiles, _ = sizes
    core, mine, other = chunk_number()
    copies = [
        pltpu.make_async_copy(rank_hbm, rank_ref, sem.at[0]),
        pltpu.make_async_copy(land_hbm, land_ref, sem.at[1]),
        pltpu.make_async_copy(temp_hbm, temp_ref, sem.at[2]),
    ]
    for copy in copies:
        copy.start()
    send_ref[...] = jnp.zeros_like(send_ref)
    keep_ref[...] = jnp.zeros_like(keep_ref)
    for copy in copies:
        copy.wait()
    for tile in range(tiles):
        lanes = slice(tile * LANES, (tile + 1) * LANES)

        @pl.when(rank_ref[tile] >= 0)
        def _():
            rank = rank_ref[tile]
            wet = wet_mask(land_ref, rank_ref, tile, rows)
            for ref, slot, field in ((send_ref, other, 1 - core), (keep_ref, mine, core)):
                total = temp_ref[field, :, lanes] * wet
                for member in range(1, members):
                    total = total + temp_ref[member * fields + field, :, lanes] * wet
                ref[jnp.bitwise_xor(slot, rank)] = total


def pack_kernel(sizes, rank_ref, temp_ref, kappa_ref, land_ref, pack_ref):
    _, fields, rows, tiles, _ = sizes
    core, _, _ = chunk_number()
    for tile in range(tiles):
        lanes = slice(tile * LANES, (tile + 1) * LANES)

        @pl.when(rank_ref[tile] >= 0)
        def _():
            rank = rank_ref[tile]
            wet = wet_mask(land_ref, rank_ref, tile, rows)
            for field in range(fields):
                pack_ref[field, rank] = temp_ref[(1 - core) * fields + field, :, lanes] * wet
            for part in range(3):
                pack_ref[fields + part, rank] = kappa_ref[part, :, lanes]
            pack_ref[fields + 3, rank] = signed_number(land_ref, rank_ref, core, tile, rows, tiles)


def weights_kernel(sizes, rank_ref, kappa_ref, land_ref, pack_ref, weight_ref, pad_ref):
    _, fields, rows, tiles, slots = sizes
    core, _, _ = chunk_number()
    band = float(2 * tiles)
    zeros = jnp.zeros((PAD, LANES), jnp.float32)
    inside = slice(PAD, PAD + rows)
    for slot in range(slots):
        owned, tile = slot_owner(rank_ref, slot, tiles)
        for part in range(4):
            pad_ref[part, slot, :PAD, :] = zeros
            pad_ref[part, slot, PAD + rows :, :] = zeros

        @pl.when(owned)
        def _():
            for part in range(3):
                pad_ref[part, slot, inside, :] = kappa_ref[part, :, tile_lanes(tile)]
            pad_ref[3, slot, inside, :] = signed_number(land_ref, rank_ref, core, tile, rows, tiles)

        @pl.when(jnp.logical_not(owned))
        def _():
            for part in range(4):
                pad_ref[part, slot, inside, :] = pack_ref[fields + part, slot]

    lane = lax.broadcasted_iota(jnp.int32, (8, LANES), 1)
    is_first, is_last = lane == 0, lane == LANES - 1
    numbers = [jnp.abs(pad_ref[3, slot, PAD : PAD + 8, :]) for slot in range(slots)]
    joined = []
    for slot in range(slots):
        here, following = numbers[slot], numbers[(slot + 1) % slots]
        expected = jnp.where(here == band, 1.0, here + 1.0)
        joined.append((following == expected).astype(jnp.float32))

    def east(values):
        rolled = [pltpu.roll(x, LANES - 1, axis=1) for x in values]
        return [
            jnp.where(is_last, joined[t] * rolled[(t + 1) % slots], rolled[t]) for t in range(slots)
        ]

    def west(values):
        rolled = [pltpu.roll(x, 1, axis=1) for x in values]
        return [jnp.where(is_first, joined[t - 1] * rolled[t - 1], rolled[t]) for t in range(slots)]

    def same(values):
        return values

    def each(f, *lists):
        return [f(*values) for values in zip(*lists, strict=True)]

    def load(part, start):
        values = [pad_ref[part, slot, start : start + 8, :] for slot in range(slots)]
        return [(x > 0.0).astype(jnp.float32) for x in values] if part == 3 else values

    for block in range(rows // 8):
        start = PAD + 8 * block
        kxx, kyy, kxy, wet = (load(part, start) for part in range(4))
        kyy_n, kxy_n, wet_n = (load(part, start + 1) for part in (1, 2, 3))
        kyy_s, kxy_s, wet_s = (load(part, start - 1) for part in (1, 2, 3))
        x_gate = each(lambda w, e: w * e, wet, east(wet))
        y_gate = each(lambda w, n: w * n, wet, wet_n)
        s_gate = each(lambda w, n: w * n, wet_s, wet)
        ax = each(lambda k, e, g: 0.5 * (k + e) * g, kxx, east(kxx), x_gate)
        cx = each(lambda k, e, g: 0.125 * (k + e) * g, kxy, east(kxy), x_gate)
        ay = each(lambda k, n, g: 0.5 * (k + n) * g, kyy, kyy_n, y_gate)
        cy = each(lambda k, n, g: 0.125 * (k + n) * g, kxy, kxy_n, y_gate)
        ays = each(lambda k, n, g: 0.5 * (k + n) * g, kyy_s, kyy, s_gate)
        cys = each(lambda k, n, g: 0.125 * (k + n) * g, kxy_s, kxy, s_gate)
        axw, cxw = west(ax), west(cx)
        groups = (
            (same, lambda: each(lambda w, a, b, c, d: 1.0 - w * (a + b + c + d), wet, ax, axw, ay, ays)),
            (same, lambda: each(lambda w, a, b, c: w * (a + b - c), wet, ay, cx, cxw)),
            (same, lambda: each(lambda w, a, b, c: w * (a - b + c), wet, ays, cx, cxw)),
            (west, lambda: each(lambda w, a, b, c: w * (a + b - c), wet, ax, cy, cys)),
            (west, lambda: each(lambda w, a, b: w * (a + b), wet, cx, cy)),
            (west, lambda: each(lambda w, a, b: w * (-a - b), wet, cx, cys)),
            (east, lambda: each(lambda w, a, b, c: w * (a - b + c), wet, axw, cy, cys)),
            (east, lambda: each(lambda w, a, b: w * (-a - b), wet, cxw, cy)),
            (east, lambda: each(lambda w, a, b: w * (a + b), wet, cxw, cys)),
        )
        for number, (move, terms) in enumerate(groups):
            for slot, term in enumerate(move(terms())):
                weight_ref[number, slot, 8 * block : 8 * block + 8, :] = term


def run_steps(planes, rows, slots, weight_ref, u_ref):
    lane = lax.broadcasted_iota(jnp.int32, (8, LANES), 1)
    is_first, is_last = lane == 0, lane == LANES - 1

    def one_step(source, target):
        for block in range(rows // 8):
            base, row0 = PAD + 8 * block, 8 * block
            parts = [[] for _ in range(planes)]
            for slot in range(slots):
                weights = [weight_ref[k, slot, row0 : row0 + 8, :] for k in range(9)]
                for plane in range(planes):
                    here = u_ref[source, plane, slot, base : base + 8, :]
                    up = u_ref[source, plane, slot, base + 1 : base + 9, :]
                    down = u_ref[source, plane, slot, base - 1 : base + 7, :]
                    centre, to_west, to_east = (
                        weights[3 * g] * here + weights[3 * g + 1] * up + weights[3 * g + 2] * down
                        for g in range(3)
                    )
                    parts[plane].append(
                        (centre, pltpu.roll(to_west, LANES - 1, axis=1), pltpu.roll(to_east, 1, axis=1))
                    )
            for plane in range(planes):
                for slot in range(slots):
                    centre, from_east, from_west = parts[plane][slot]
                    after = parts[plane][(slot + 1) % slots][1]
                    before = parts[plane][slot - 1][2]
                    u_ref[target, plane, slot, base : base + 8, :] = (
                        centre
                        + jnp.where(is_last, after, from_east)
                        + jnp.where(is_first, before, from_west)
                    )

    def two_steps(_, carry):
        one_step(0, 1)
        one_step(1, 0)
        return carry

    lax.fori_loop(0, STEPS // 2, two_steps, 0)


def clear_pads(planes, rows, slots, u_ref):
    zeros = jnp.zeros((PAD, LANES), jnp.float32)
    for half in range(2):
        for plane in range(planes):
            for slot in range(slots):
                u_ref[half, plane, slot, :PAD, :] = zeros
                u_ref[half, plane, slot, PAD + rows :, :] = zeros


def member_kernel(sizes, rank_ref, temp_ref, land_ref, pack_ref, weight_ref, stepped_ref, u_ref):
    _, fields, rows, tiles, slots = sizes
    core, _, _ = chunk_number()
    clear_pads(fields, rows, slots, u_ref)
    inside = slice(PAD, PAD + rows)
    for slot in range(slots):
        owned, tile = slot_owner(rank_ref, slot, tiles)

        @pl.when(owned)
        def _():
            wet = wet_mask(land_ref, rank_ref, tile, rows)
            for field in range(fields):
                u_ref[0, field, slot, inside, :] = temp_ref[core * fields + field, :, tile_lanes(tile)] * wet

        @pl.when(jnp.logical_not(owned))
        def _():
            for field in range(fields):
                u_ref[0, field, slot, inside, :] = pack_ref[field, slot]

    run_steps(fields, rows, slots, weight_ref, u_ref)
    for field in range(fields):
        for slot in range(slots):
            stepped_ref[field, slot] = u_ref[0, field, slot, inside, :]


def mean_kernel(sizes, samples, gathered_ref, weight_ref, stepped_ref, u_ref):
    _, _, rows, _, slots = sizes
    _, mine, _ = chunk_number()
    clear_pads(1, rows, slots, u_ref)
    inside = slice(PAD, PAD + rows)
    for slot in range(slots):
        u_ref[0, 0, slot, inside, :] = gathered_ref[jnp.bitwise_xor(mine, slot)] * (1.0 / samples)
    run_steps(1, rows, slots, weight_ref, u_ref)
    for slot in range(slots):
        stepped_ref[slot] = u_ref[0, 0, slot, inside, :]


def observe_planes(fields, cell, frac):
    rows, columns = fields[0].shape
    count = cell.shape[1]
    frac_east, frac_north = frac[0:1, :], frac[1:2, :]
    column, row = lax.rem(cell, columns), lax.rem(cell // columns, rows)
    at = lax.broadcasted_iota(jnp.int32, (columns, count), 0) - column
    pick = jnp.where(at == 0, 1.0 - frac_east, jnp.where(at == 1, frac_east, 0.0))
    values = jnp.concatenate(fields, axis=0)
    picked = jnp.dot(values, pick, precision=HIGHEST, preferred_element_type=jnp.float32)
    at = lax.broadcasted_iota(jnp.int32, (rows, count), 0) - row
    pick = jnp.where(at == 0, 1.0 - frac_north, jnp.where(at == 1, frac_north, 0.0))
    return [
        jnp.sum(picked[number * rows : (number + 1) * rows] * pick, axis=0, keepdims=True)
        for number in range(len(fields))
    ]


def observe_kernel(sizes, rank_ref, own_ref, other_ref, cell_ref, frac_ref, stepped_ref, seen_ref):
    members, fields, rows, tiles, _ = sizes
    core, _, _ = chunk_number()
    for tile in range(tiles):
        lanes = slice(tile * LANES, (tile + 1) * LANES)
        rank = rank_ref[tile]

        @pl.when(rank >= 0)
        def _():
            for field in range(fields):
                stepped_ref[core * fields + field, :, lanes] = own_ref[field, rank]
                stepped_ref[(1 - core) * fields + field, :, lanes] = other_ref[field, rank]

        @pl.when(rank < 0)
        def _():
            for plane in range(members * fields):
                stepped_ref[plane, :, lanes] = jnp.zeros((rows, LANES), jnp.float32)

    planes = [stepped_ref[plane] for plane in range(members * fields)]
    halves = cell_ref.shape[1] // LANES
    for plane, seen in enumerate(observe_planes(planes, cell_ref[...], frac_ref[...])):
        for half in range(halves):
            at = plane * halves + half
            seen_ref[at : at + 1, :] = seen[:, half * LANES : (half + 1) * LANES]


def final_kernel(
    sizes, ensemble, rank_ref, own_ref, other_ref, cell_ref, frac_ref, seen_ref, stepped_ref,
    field_hbm, anomaly_ref, variance_ref, field_ref, mean_ref, sem,
):
    members, fields, rows, tiles, _ = sizes
    core, _, _ = chunk_number()
    for tile in range(tiles):
        lanes = slice(tile * LANES, (tile + 1) * LANES)
        rank = rank_ref[tile]

        @pl.when(rank >= 0)
        def _():
            mean_ref[core, :, lanes] = own_ref[rank]
            mean_ref[1 - core, :, lanes] = other_ref[rank]

        @pl.when(rank < 0)
        def _():
            for field in range(fields):
                mean_ref[field, :, lanes] = jnp.zeros((rows, LANES), jnp.float32)

    for member in range(members):
        for field in range(fields):
            plane = member * fields + field
            field_ref[plane] = stepped_ref[plane] - mean_ref[field]
    copy = pltpu.make_async_copy(field_ref, field_hbm, sem)
    copy.start()
    mean_seen = observe_planes([mean_ref[field] for field in range(fields)], cell_ref[...], frac_ref[...])
    halves = cell_ref.shape[1] // LANES
    stride = members * fields * halves
    sets = seen_ref.shape[0] // stride

    def tree(values):
        while len(values) > 1:
            values = [a + b for a, b in zip(values[0::2], values[1::2], strict=True)]
        return values[0]

    for field in range(fields):
        for half in range(halves):
            lanes = slice(half * LANES, (half + 1) * LANES)
            mean = mean_seen[field][:, lanes]
            observed = []
            for part in range(sets):
                for member in range(members):
                    at = part * stride + (member * fields + field) * halves + half
                    observed.append(seen_ref[at : at + 1, :] - mean)
            centre = tree(observed) / ensemble
            anomaly = [value - centre for value in observed]
            variance_ref[field : field + 1, lanes] = tree([value * value for value in anomaly]) / ensemble
            for member in range(members):
                anomaly_ref[member, field : field + 1, lanes] = anomaly[member]
    copy.wait()


def local(temp_salt, diffusivity, wet_rank, land_rows, obs_cell, obs_frac):
    members, fields, levels, rows, columns = temp_salt.shape
    tiles = wet_rank.shape[0]
    cores, level_count, member_count = (lax.axis_size(axis) for axis in ALL_AXES)
    slots = tiles * cores // 2
    chips = level_count * member_count
    bits = chips.bit_length() - 1
    assert cores == 2 and fields == 2 and members == 2 and levels == 1 and slots == 4
    assert columns == tiles * LANES and chips == 1 << bits and bits >= 3
    count = obs_cell.shape[0]
    planes = members * fields
    sizes = (members, fields, rows, tiles, slots)
    samples = members * levels * chips
    level_bit = bits - 1

    def device(core, chip):
        return core * chips + chip

    def exchange(value, masks):
        if masks is None:
            to = lambda core, chip: (1 - core, chip)
        else:
            to = lambda core, chip: (core, chip ^ masks[core])
        pairs = [(device(core, chip), device(*to(core, chip))) for core in range(2) for chip in range(chips)]
        return lax.ppermute(value, ALL_AXES, pairs)

    def struct(*shape):
        return jax.ShapeDtypeStruct(shape, jnp.float32)

    def call(kernel, out_shape, operands, scratch=(), cycles=1000, in_specs=None, out_specs=None):
        return pl.pallas_call(
            functools.partial(kernel, sizes),
            out_shape=out_shape,
            in_specs=in_specs or [SMEM if x is wet_rank else VMEM for x in operands],
            out_specs=out_specs or jax.tree.map(lambda _: VMEM, out_shape),
            scratch_shapes=list(scratch),
            compiler_params=PARAMS,
            cost_estimate=pl.CostEstimate(flops=cycles * 4096, bytes_accessed=1 << 20, transcendentals=0),
        )(*operands)

    def halo(count):
        return pltpu.VMEM((2, count, slots, rows + 2 * PAD, LANES), jnp.float32)

    temp = temp_salt.reshape(planes, rows, columns)
    land = land_rows.reshape(tiles, LANES)
    cell = obs_cell.reshape(1, count)
    masks = {1: (1, 2), 2: (2, 1), 3: (3, 3)}

    send, keep = call(
        sums_kernel, (struct(slots, rows, LANES), struct(slots, rows, LANES)), (wet_rank, temp, land),
        scratch=[
            pltpu.SMEM((tiles,), jnp.int32),
            pltpu.VMEM((planes, rows, columns), jnp.float32),
            pltpu.VMEM((tiles, LANES), jnp.int32),
            pltpu.SemaphoreType.DMA((3,)),
        ],
        in_specs=[HBM] * 3,
    )
    arrived = exchange(send, None)
    pack = call(pack_kernel, struct(fields + 4, slots, rows, LANES), (wet_rank, temp, diffusivity, land))
    packed = exchange(pack, None)
    total = keep + arrived
    got = [exchange(total[k], masks[k]) for k in (1, 2, 3)]
    total = (total[0] + got[0]) + (got[1] + got[2])

    weights = call(
        weights_kernel, struct(9, slots, rows, LANES), (wet_rank, diffusivity, land, packed),
        [pltpu.VMEM((4, slots, rows + 2 * PAD, LANES), jnp.float32)],
    )
    own = call(
        member_kernel, struct(fields, slots, rows, LANES), (wet_rank, temp, land, packed, weights),
        [halo(fields)], cycles=4000,
    )
    other = exchange(own, None)
    stepped, seen = call(
        observe_kernel, (struct(planes, rows, columns), struct(planes * count // LANES, LANES)),
        (wet_rank, own, other, cell, obs_frac), cycles=2000,
    )

    for bit in [level_bit] + list(range(2, level_bit)):
        mask = (1 << bit, 1 << bit)
        if bit == level_bit:
            total = total + exchange(total, mask)
        else:
            got = exchange(jnp.concatenate([total, seen], axis=0), mask)
            total = total + got[:rows]
            seen = jnp.concatenate([seen, got[rows:]], axis=0)
    payload = jnp.concatenate([total, seen], axis=0)
    got = [payload] + [exchange(payload, masks[k]) for k in (1, 2, 3)]
    gathered = jnp.stack([x[:rows] for x in got])
    seen = jnp.concatenate([x[rows:] for x in got], axis=0)

    def step_mean(sizes, *refs):
        mean_kernel(sizes, samples, *refs)

    own_mean = call(step_mean, struct(slots, rows, LANES), (gathered, weights), [halo(1)], cycles=2000)
    other_mean = exchange(own_mean, None)

    def last_kernel(sizes, *refs):
        final_kernel(sizes, members * member_count, *refs)

    field, anomaly, variance = call(
        last_kernel,
        (struct(planes, rows, columns), struct(members, fields, count), struct(fields, count)),
        (wet_rank, own_mean, other_mean, cell, obs_frac, seen, stepped),
        [
            pltpu.VMEM((planes, rows, columns), jnp.float32),
            pltpu.VMEM((fields, rows, columns), jnp.float32),
            pltpu.SemaphoreType.DMA,
        ],
        out_specs=(HBM, VMEM, VMEM),
    )
    return field.reshape(members, fields, levels, rows, columns), anomaly, variance


def solution(mesh):
    placed = (
        P("member", None, "level", None, "tile"),
        P(None, None, "tile"),
        P("tile"),
        P("tile"),
        P(("tile", "level")),
        P(None, ("tile", "level")),
    )

    return jax.shard_map(
        local,
        mesh=mesh,
        in_specs=placed,
        out_specs=(
            P("member", None, "level", None, "tile"),
            P("member", None, ("tile", "level")),
            P(None, ("tile", "level")),
        ),
        check_vma=False,
    )
```

time: 53.4 us -> 51.4 us (0.963)
  Pallas kernels: 20.5 us -> 15 us
  waiting for transfers between devices: 14 us -> 18.2 us
  local copies, waits for them, and re-layouts: 4.45 us -> 3.76 us
    pallas_call x7, Pallas kernels: 20.5 us -> 15 us  [call(): pl.pallas_call(functools.partial(kernel, sizes), out_shape=out_shape, in_...]
    ppermute x11 -> x12, waiting for transfers between devices: 14 us -> 18.2 us  [exchange(): return lax.ppermute(value, ALL_AXES, pairs)]
    unnamed x24 -> x22, local copies, waits for them, and re-layouts: 4.41 us -> 3.73 us
    ppermute x11 -> x12, starting transfers between devices: 13.2 us -> 13.2 us  [exchange(): return lax.ppermute(value, ALL_AXES, pairs)]
  transfers between devices with their start and end apart: 11 -> 12, of which waited for: 9 -> 9; matrix products, arithmetic and copies ran while one was open for 0% -> 0% of each run, Pallas kernels for 1% -> 1%
where the time goes in v1:
time: 51.4 us; the launch traced here: 51.2 us
  waiting for transfers between devices  18.2 us (35%)
  Pallas kernels  15 us (29%)
  starting transfers between devices  13.2 us (26%)
  local copies, waits for them, and re-layouts  3.76 us (7%)
  between operations  0.87 us (2%)
    ppermute x12, waiting for transfers between devices, exchange(): return lax.ppermute(value, ALL_AXES, pairs)  18.2 us
    pallas_call x7, Pallas kernels, call(): pl.pallas_call(functools.partial(kernel, sizes), out_shape=out_shape, in_...  15 us
    ppermute x12, starting transfers between devices, exchange(): return lax.ppermute(value, ALL_AXES, pairs)  13.2 us
    unnamed x22, local copies, waits for them, and re-layouts  3.73 us
  transfers between devices with their start and end apart: 12, of which 9 were waited for; matrix products, arithmetic and copies ran while one was open for 0% of the time, Pallas kernels for 1%

profile of v1, /device:TPU:0, one launch (start us, length us, event | category | flops | bytes accessed | tf_op | source)
XLA Modules:
  0.0 51.2 jit_solution(6446229549113903586)
XLA Ops:
  0.6 0.0 copy-start
  0.6 1.2 %copy-done = f32[2,2,1,128,512]{4,3,2,1,0:T(8,128)S(1)} copy-done((f32[2,2,1,128,512]{4,3,2,1,0:T(8,128)S(1)}, f32[2,2,1,128,512]{4,3,2,1,0:T(8,128)}, u32[]{:S(2)}) %copy-start) | copy-done | bytes 1048600
  1.9 0.0 copy-start.2
  1.9 1.1 %copy-done.2 = f32[3,128,512]{2,1,0:T(8,128)S(1)} copy-done((f32[3,128,512]{2,1,0:T(8,128)S(1)}, f32[3,128,512]{2,1,0:T(8,128)}, u32[]{:S(2)}) %copy-start.2) | copy-done | bytes 786456
  3.0 0.0 copy-start.4
  3.0 0.7 %copy-done.4 = s32[512]{0:T(512)S(1)} copy-done((s32[512]{0:T(512)S(1)}, s32[512]{0:T(512)}, u32[]{:S(2)}) %copy-start.4) | copy-done | bytes 2072
  3.7 0.0 copy-start.6
  3.7 0.7 %copy-done.6 = s32[4]{0:T(128)S(1)} copy-done((s32[4]{0:T(128)S(1)}, s32[4]{0:T(128)}, u32[]{:S(2)}) %copy-start.6) | copy-done | bytes 40
  4.3 0.7 %shard_map.86 = f32[6,4,128,128]{3,2,1,0:T(8,128)S(1)} custom-call(s32[4]{0:T(128)S(1)} %copy-done.6, f32[4,128,512]{2,1,0:T(8,128)S(1)} %bitcast.25, f32[3,128,512]{2,1,0:T(8,128)S(1)} %copy-done.2, s32[4,128]{1,0:T(4,128)S(1)} %bitcast.28), custom_call_target="tpu_custom_call" | custom-call | flops 4096000 | bytes 1048576 | tf_op jit(solution)/shard_map/pallas_call | solution.py:396
  5.0 0.0 copy-start.3
  5.0 0.6 %collective-permute-start.5 = (f32[6,4,128,128]{3,2,1,0:T(8,128)S(1)}, f32[6,4,128,128]{3,2,1,0:T(8,128)S(1)}, u32[]{:S(2)}, u32[]{:S(2)}) collective-permute-start(f32[6,4,128,128]{3,2,1,0:T(8,128)S(1)} %shard_map.86), channel_id=1, source_target_pairs={{0,16},{1,17},{2,18},{3,19},{4,20},{5,21},{6,22},{7,23},{8,24},{9,... | collective-permute-start | bytes 4718600 | tf_op jit(solution)/shard_map/ppermute | solution.py:390
  5.6 0.0 copy-done.5
  5.6 0.7 %shard_map.85 = (f32[4,128,128]{2,1,0:T(8,128)S(1)}, f32[4,128,128]{2,1,0:T(8,128)S(1)}) custom-call(s32[4]{0:T(128)S(1)} %copy-done.6, f32[4,128,512]{2,1,0:T(8,128)S(1)} %bitcast.26, s32[4,128]{1,0:T(4,128)S(1)} %bitcast.29), custom_call_target="tpu_custom_call" | custom-call | flops 4096000 | bytes 1048576 | tf_op jit(solution)/shard_map/pallas_call | solution.py:396
  6.2 0.1 collective-permute-start
  6.3 2.6 %collective-permute-done = f32[4,128,128]{2,1,0:T(8,128)S(1)} collective-permute-done((f32[4,128,128]{2,1,0:T(8,128)S(1)}, f32[4,128,128]{2,1,0:T(8,128)S(1)}, u32[]{:S(2)}, u32[]{:S(2)}) %collective-permute-start) | collective-permute-done | bytes 262176 | tf_op jit(solution)/shard_map/ppermute | solution.py:390
  9.0 0.0 copy-start.1
  9.0 0.0 collective-permute-done.5.pack_ref
  9.0 0.0 copy-done.3
  9.0 3.0 %shard_map.87.weight_ref.refs_1_ = f32[9,4,128,128]{3,2,1,0:T(8,128)S(1)} custom-call(s32[4]{0:T(128)S(1)} %copy-done.6, f32[3,128,512]{2,1,0:T(8,128)S(1)} %copy-done.3, s32[4,128]{1,0:T(4,128)S(1)} %bitcast.30, f32[6,4,128,128]{3,2,1,0:T(8,128)S(1)} %collective-permute-done.5.pack_ref), custom_call_target="tpu_custom_call" | custom-call | flops 4096000 | bytes 1048576 | tf_op jit(solution)/shard_map/pallas_call | solution.py:396
  12.0 0.0 copy-done.1
  12.0 0.0 copy-start.7
  12.0 0.0 copy-start.8
  12.0 3.7 %shard_map.88.own_ref = f32[2,4,128,128]{3,2,1,0:T(8,128)S(1)} custom-call(s32[4]{0:T(128)S(1)} %copy-done.6, f32[4,128,512]{2,1,0:T(8,128)S(1)} %bitcast.27, s32[4,128]{1,0:T(4,128)S(1)} %bitcast.31, f32[6,4,128,128]{3,2,1,0:T(8,128)S(1)} %collective-permute-done.5.pack_ref, f32[9,4,128,128]{3,2,1,0:T(8,128)S(1)} %shard_map.87.weight_ref.refs_1_), custom_call_target="tpu_custom_call" | custom-call | flops 16384000 | bytes 1048576 | tf_op jit(solution)/shard_map/pallas_call | solution.py:396
  15.8 0.4 collective-permute-start.6
  16.2 2.7 %collective-permute-start.1 = (f32[128,128]{1,0:T(8,128)S(1)}, f32[128,128]{1,0:T(8,128)S(1)}, u32[]{:S(2)}, u32[]{:S(2)}) collective-permute-start(f32[128,128]{1,0:T(8,128)S(1)} %get-tuple-element.22), channel_id=1, source_target_pairs={{0,1},{1,0},{2,3},{3,2},{4,5},{5,4},{6,7},{7,6},{8,9},{9,8},{10,11... | collective-permute-start | bytes 196616 | tf_op jit(solution)/shard_map/ppermute | solution.py:390
  18.9 1.6 %collective-permute-start.2 = (f32[128,128]{1,0:T(8,128)S(1)}, f32[128,128]{1,0:T(8,128)S(1)}, u32[]{:S(2)}, u32[]{:S(2)}) collective-permute-start(f32[128,128]{1,0:T(8,128)S(1)} %get-tuple-element.21), channel_id=1, source_target_pairs={{0,2},{1,3},{2,0},{3,1},{4,6},{5,7},{6,4},{7,5},{8,10},{9,11},{10,... | collective-permute-start | bytes 196616 | tf_op jit(solution)/shard_map/ppermute | solution.py:390
  20.5 0.0 collective-permute-start.3
  20.5 0.7 %collective-permute-done.1 = f32[128,128]{1,0:T(8,128)S(1)} collective-permute-done((f32[128,128]{1,0:T(8,128)S(1)}, f32[128,128]{1,0:T(8,128)S(1)}, u32[]{:S(2)}, u32[]{:S(2)}) %collective-permute-start.1) | collective-permute-done | bytes 65568 | tf_op jit(solution)/shard_map/ppermute | solution.py:390
  21.2 2.3 %collective-permute-done.2 = f32[128,128]{1,0:T(8,128)S(1)} collective-permute-done((f32[128,128]{1,0:T(8,128)S(1)}, f32[128,128]{1,0:T(8,128)S(1)}, u32[]{:S(2)}, u32[]{:S(2)}) %collective-permute-start.2) | collective-permute-done | bytes 65568 | tf_op jit(solution)/shard_map/ppermute | solution.py:390
  23.5 2.2 %collective-permute-done.3 = f32[128,128]{1,0:T(8,128)S(1)} collective-permute-done((f32[128,128]{1,0:T(8,128)S(1)}, f32[128,128]{1,0:T(8,128)S(1)}, u32[]{:S(2)}, u32[]{:S(2)}) %collective-permute-start.3) | collective-permute-done | bytes 65568 | tf_op jit(solution)/shard_map/ppermute | solution.py:390
  25.7 1.6 %collective-permute-start.4 = (f32[128,128]{1,0:T(8,128)S(1)}, f32[128,128]{1,0:T(8,128)S(1)}, u32[]{:S(2)}, u32[]{:S(2)}) collective-permute-start(f32[128,128]{1,0:T(8,128)S(1)} %fusion.1), channel_id=1, source_target_pairs={{0,8},{1,9},{2,10},{3,11},{4,12},{5,13},{6,14},{7,15},{8,0},{9,1},... | collective-permute-start | bytes 196616 | tf_op jit(solution)/shard_map/ppermute | solution.py:390
  27.3 2.8 %collective-permute-done.4 = f32[128,128]{1,0:T(8,128)S(1)} collective-permute-done((f32[128,128]{1,0:T(8,128)S(1)}, f32[128,128]{1,0:T(8,128)S(1)}, u32[]{:S(2)}, u32[]{:S(2)}) %collective-permute-start.4) | collective-permute-done | bytes 65568 | tf_op jit(solution)/shard_map/ppermute | solution.py:390
  30.0 0.0 collective-permute-done.6.other_ref
  30.1 0.0 copy-done.7
  30.1 0.0 copy-done.8
  30.1 1.9 %shard_map.89 = (f32[4,128,512]{2,1,0:T(8,128)S(1)}, f32[8,128]{1,0:T(8,128)S(1)}) custom-call(s32[4]{0:T(128)S(1)} %copy-done.6, f32[2,4,128,128]{3,2,1,0:T(8,128)S(1)} %shard_map.88.own_ref, f32[2,4,128,128]{3,2,1,0:T(8,128)S(1)} %collective-permute-done.6.other_ref, s32[1,256]{1,0:T(1,128)S(1)} %bitcast.32, f32[2,256]{1,0:T(2,128)S(1)} %copy-done.7), custom_call_target="tpu_custom_call" | custom-call | flops 8192000 | bytes 1048576 | tf_op jit(solution)/shard_map/pallas_call | solution.py:396
  32.0 2.7 %collective-permute-start.7 = (f32[136,128]{1,0:T(8,128)S(1)}, f32[136,128]{1,0:T(8,128)S(1)}, u32[]{:S(2)}, u32[]{:S(2)}) collective-permute-start(f32[136,128]{1,0:T(8,128)S(1)} %pad_maximum_fusion.2), channel_id=1, source_target_pairs={{0,4},{1,5},{2,6},{3,7},{4,0},{5,1},{6,2},{7,3},{8,12},{9,13},{10,... | collective-permute-start | bytes 208904 | tf_op jit(solution)/shard_map/ppermute | solution.py:390
  34.6 3.3 %collective-permute-done.7 = f32[136,128]{1,0:T(8,128)S(1)} collective-permute-done((f32[136,128]{1,0:T(8,128)S(1)}, f32[136,128]{1,0:T(8,128)S(1)}, u32[]{:S(2)}, u32[]{:S(2)}) %collective-permute-start.7) | collective-permute-done | bytes 69664 | tf_op jit(solution)/shard_map/ppermute | solution.py:390
  38.0 0.1 collective-permute-start.10
  38.1 1.9 %collective-permute-start.9 = (f32[144,128]{1,0:T(8,128)S(1)}, f32[144,128]{1,0:T(8,128)S(1)}, u32[]{:S(2)}, u32[]{:S(2)}) collective-permute-start(f32[144,128]{1,0:T(8,128)S(1)} %pad_maximum_fusion.1), channel_id=1, source_target_pairs={{0,2},{1,3},{2,0},{3,1},{4,6},{5,7},{6,4},{7,5},{8,10},{9,11},{10,... | collective-permute-start | bytes 221192 | tf_op jit(solution)/shard_map/ppermute | solution.py:390
  40.1 1.5 %collective-permute-start.8 = (f32[144,128]{1,0:T(8,128)S(1)}, f32[144,128]{1,0:T(8,128)S(1)}, u32[]{:S(2)}, u32[]{:S(2)}) collective-permute-start(f32[144,128]{1,0:T(8,128)S(1)} %pad_maximum_fusion.1), channel_id=1, source_target_pairs={{0,1},{1,0},{2,3},{3,2},{4,5},{5,4},{6,7},{7,6},{8,9},{9,8},{10,11... | collective-permute-start | bytes 221192 | tf_op jit(solution)/shard_map/ppermute | solution.py:390
  41.6 1.8 %collective-permute-done.10 = f32[144,128]{1,0:T(8,128)S(1)} collective-permute-done((f32[144,128]{1,0:T(8,128)S(1)}, f32[144,128]{1,0:T(8,128)S(1)}, u32[]{:S(2)}, u32[]{:S(2)}) %collective-permute-start.10) | collective-permute-done | bytes 73760 | tf_op jit(solution)/shard_map/ppermute | solution.py:390
  43.3 0.0 collective-permute-done.9
  43.4 1.1 %collective-permute-done.8 = f32[144,128]{1,0:T(8,128)S(1)} collective-permute-done((f32[144,128]{1,0:T(8,128)S(1)}, f32[144,128]{1,0:T(8,128)S(1)}, u32[]{:S(2)}, u32[]{:S(2)}) %collective-permute-start.8) | collective-permute-done | bytes 73760 | tf_op jit(solution)/shard_map/ppermute | solution.py:390
  44.4 2.0 %shard_map.90.refs_1_ = f32[4,128,128]{2,1,0:T(8,128)S(1)} custom-call(f32[4,128,128]{2,1,0:T(8,128)S(1)} %pad_maximum_fusion.refs_0_, f32[9,4,128,128]{3,2,1,0:T(8,128)S(1)} %shard_map.87.weight_ref.refs_1_), custom_call_target="tpu_custom_call" | custom-call | flops 8192000 | bytes 1048576 | tf_op jit(solution)/shard_map/pallas_call | solution.py:396
  46.5 0.1 collective-permute-start.11
  46.6 1.5 %collective-permute-done.11.refs_2_ = f32[4,128,128]{2,1,0:T(8,128)S(1)} collective-permute-done((f32[4,128,128]{2,1,0:T(8,128)S(1)}, f32[4,128,128]{2,1,0:T(8,128)S(1)}, u32[]{:S(2)}, u32[]{:S(2)}) %collective-permute-start.11) | collective-permute-done | bytes 262176 | tf_op jit(solution)/shard_map/ppermute | solution.py:390
  48.1 3.1 %shard_map.91 = (f32[4,128,512]{2,1,0:T(8,128)}, f32[2,2,256]{2,1,0:T(2,128)}, f32[2,256]{1,0:T(2,128)}) custom-call(s32[4]{0:T(128)S(1)} %copy-done.6, f32[4,128,128]{2,1,0:T(8,128)S(1)} %shard_map.90.refs_1_, f32[4,128,128]{2,1,0:T(8,128)S(1)} %collective-permute-done.11.refs_2_, s32[1,256]{1,0:T(1,128)S(1)} %bitcast.33, f32[2,256]{1,0:T(2,128)S(1)} %copy-done.7, ...), custom_call_target="tpu_custom_call" | custom-call | flops 4096000 | bytes 1048576 | tf_op jit(solution)/shard_map/pallas_call | solution.py:396
  (17 shorter events, 0.2 us)
Async XLA Ops:
  0.6 1.2 %copy-start = (f32[2,2,1,128,512]{4,3,2,1,0:T(8,128)S(1)}, f32[2,2,1,128,512]{4,3,2,1,0:T(8,128)}, u32[]{:S(2)}) copy-start(f32[2,2,1,128,512]{4,3,2,1,0:T(8,128)} %param.6) | copy-start | bytes 3145732
  1.9 1.1 %copy-start.2 = (f32[3,128,512]{2,1,0:T(8,128)S(1)}, f32[3,128,512]{2,1,0:T(8,128)}, u32[]{:S(2)}) copy-start(f32[3,128,512]{2,1,0:T(8,128)} %kappa_ref.3) | copy-start | bytes 2359300
  3.0 0.7 %copy-start.4 = (s32[512]{0:T(512)S(1)}, s32[512]{0:T(512)}, u32[]{:S(2)}) copy-start(s32[512]{0:T(512)} %param.9) | copy-start | bytes 6148
  3.7 0.7 %copy-start.6 = (s32[4]{0:T(128)S(1)}, s32[4]{0:T(128)}, u32[]{:S(2)}) copy-start(s32[4]{0:T(128)} %refs_0_.1) | copy-start | bytes 52
  4.3 1.2 %copy-start.5 = (s32[512]{0:T(512)S(1)}, s32[512]{0:T(512)}, u32[]{:S(2)}) copy-start(s32[512]{0:T(512)} %param.9) | copy-start | bytes 6148
  5.0 4.0 %copy-start.3 = (f32[3,128,512]{2,1,0:T(8,128)S(1)}, f32[3,128,512]{2,1,0:T(8,128)}, u32[]{:S(2)}) copy-start(f32[3,128,512]{2,1,0:T(8,128)} %kappa_ref.3) | copy-start | bytes 2359300
  5.0 4.0 %collective-permute-start.5 = (f32[6,4,128,128]{3,2,1,0:T(8,128)S(1)}, f32[6,4,128,128]{3,2,1,0:T(8,128)S(1)}, u32[]{:S(2)}, u32[]{:S(2)}) collective-permute-start(f32[6,4,128,128]{3,2,1,0:T(8,128)S(1)} %shard_map.86), channel_id=1, source_target_pairs={{0,16},{1,17},{2,18},{3,19},{4,20},{5,21},{6,22},{7,23},{8,24},{9,... | collective-permute-start | bytes 4718600 | tf_op jit(solution)/shard_map/ppermute | solution.py:390
  6.2 2.7 %collective-permute-start = (f32[4,128,128]{2,1,0:T(8,128)S(1)}, f32[4,128,128]{2,1,0:T(8,128)S(1)}, u32[]{:S(2)}, u32[]{:S(2)}) collective-permute-start(f32[4,128,128]{2,1,0:T(8,128)S(1)} %get-tuple-element.11), channel_id=1, source_target_pairs={{0,16},{1,17},{2,18},{3,19},{4,20},{5,21},{6,22},{7,23},{8,24},{9,... | collective-permute-start | bytes 786440 | tf_op jit(solution)/shard_map/ppermute | solution.py:390
  9.0 3.0 %copy-start.1 = (f32[2,2,1,128,512]{4,3,2,1,0:T(8,128)S(1)}, f32[2,2,1,128,512]{4,3,2,1,0:T(8,128)}, u32[]{:S(2)}) copy-start(f32[2,2,1,128,512]{4,3,2,1,0:T(8,128)} %param.6) | copy-start | bytes 3145732
  12.0 18.0 %copy-start.7 = (f32[2,256]{1,0:T(2,128)S(1)}, f32[2,256]{1,0:T(2,128)}, u32[]{:S(2)}) copy-start(f32[2,256]{1,0:T(2,128)} %refs_4_.1) | copy-start | bytes 6148
  12.0 18.0 %copy-start.8 = (s32[256]{0:T(256)S(1)}, s32[256]{0:T(256)}, u32[]{:S(2)}) copy-start(s32[256]{0:T(256)} %param.10) | copy-start | bytes 3076
  15.8 14.3 %collective-permute-start.6 = (f32[2,4,128,128]{3,2,1,0:T(8,128)S(1)}, f32[2,4,128,128]{3,2,1,0:T(8,128)S(1)}, u32[]{:S(2)}, u32[]{:S(2)}) collective-permute-start(f32[2,4,128,128]{3,2,1,0:T(8,128)S(1)} %shard_map.88.own_ref), channel_id=1, source_target_pairs={{0,16},{1,17},{2,18},{3,19},{4,20},{5,21},{6,22},{7,23},{8,24},{9,... | collective-permute-start | bytes 1572872 | tf_op jit(solution)/shard_map/ppermute | solution.py:390
  16.2 5.0 %collective-permute-start.1 = (f32[128,128]{1,0:T(8,128)S(1)}, f32[128,128]{1,0:T(8,128)S(1)}, u32[]{:S(2)}, u32[]{:S(2)}) collective-permute-start(f32[128,128]{1,0:T(8,128)S(1)} %get-tuple-element.22), channel_id=1, source_target_pairs={{0,1},{1,0},{2,3},{3,2},{4,5},{5,4},{6,7},{7,6},{8,9},{9,8},{10,11... | collective-permute-start | bytes 196616 | tf_op jit(solution)/shard_map/ppermute | solution.py:390
  18.9 4.6 %collective-permute-start.2 = (f32[128,128]{1,0:T(8,128)S(1)}, f32[128,128]{1,0:T(8,128)S(1)}, u32[]{:S(2)}, u32[]{:S(2)}) collective-permute-start(f32[128,128]{1,0:T(8,128)S(1)} %get-tuple-element.21), channel_id=1, source_target_pairs={{0,2},{1,3},{2,0},{3,1},{4,6},{5,7},{6,4},{7,5},{8,10},{9,11},{10,... | collective-permute-start | bytes 196616 | tf_op jit(solution)/shard_map/ppermute | solution.py:390
  20.5 5.2 %collective-permute-start.3 = (f32[128,128]{1,0:T(8,128)S(1)}, f32[128,128]{1,0:T(8,128)S(1)}, u32[]{:S(2)}, u32[]{:S(2)}) collective-permute-start(f32[128,128]{1,0:T(8,128)S(1)} %get-tuple-element.20), channel_id=1, source_target_pairs={{0,3},{1,2},{2,1},{3,0},{4,7},{5,6},{6,5},{7,4},{8,11},{9,10},{10,... | collective-permute-start | bytes 196616 | tf_op jit(solution)/shard_map/ppermute | solution.py:390
  25.7 4.3 %collective-permute-start.4 = (f32[128,128]{1,0:T(8,128)S(1)}, f32[128,128]{1,0:T(8,128)S(1)}, u32[]{:S(2)}, u32[]{:S(2)}) collective-permute-start(f32[128,128]{1,0:T(8,128)S(1)} %fusion.1), channel_id=1, source_target_pairs={{0,8},{1,9},{2,10},{3,11},{4,12},{5,13},{6,14},{7,15},{8,0},{9,1},... | collective-permute-start | bytes 196616 | tf_op jit(solution)/shard_map/ppermute | solution.py:390
  32.0 6.0 %collective-permute-start.7 = (f32[136,128]{1,0:T(8,128)S(1)}, f32[136,128]{1,0:T(8,128)S(1)}, u32[]{:S(2)}, u32[]{:S(2)}) collective-permute-start(f32[136,128]{1,0:T(8,128)S(1)} %pad_maximum_fusion.2), channel_id=1, source_target_pairs={{0,4},{1,5},{2,6},{3,7},{4,0},{5,1},{6,2},{7,3},{8,12},{9,13},{10,... | collective-permute-start | bytes 208904 | tf_op jit(solution)/shard_map/ppermute | solution.py:390
  38.0 5.3 %collective-permute-start.10 = (f32[144,128]{1,0:T(8,128)S(1)}, f32[144,128]{1,0:T(8,128)S(1)}, u32[]{:S(2)}, u32[]{:S(2)}) collective-permute-start(f32[144,128]{1,0:T(8,128)S(1)} %pad_maximum_fusion.1), channel_id=1, source_target_pairs={{0,3},{1,2},{2,1},{3,0},{4,7},{5,6},{6,5},{7,4},{8,11},{9,10},{10,... | collective-permute-start | bytes 221192 | tf_op jit(solution)/shard_map/ppermute | solution.py:390
  38.1 5.2 %collective-permute-start.9 = (f32[144,128]{1,0:T(8,128)S(1)}, f32[144,128]{1,0:T(8,128)S(1)}, u32[]{:S(2)}, u32[]{:S(2)}) collective-permute-start(f32[144,128]{1,0:T(8,128)S(1)} %pad_maximum_fusion.1), channel_id=1, source_target_pairs={{0,2},{1,3},{2,0},{3,1},{4,6},{5,7},{6,4},{7,5},{8,10},{9,11},{10,... | collective-permute-start | bytes 221192 | tf_op jit(solution)/shard_map/ppermute | solution.py:390
  40.1 4.4 %collective-permute-start.8 = (f32[144,128]{1,0:T(8,128)S(1)}, f32[144,128]{1,0:T(8,128)S(1)}, u32[]{:S(2)}, u32[]{:S(2)}) collective-permute-start(f32[144,128]{1,0:T(8,128)S(1)} %pad_maximum_fusion.1), channel_id=1, source_target_pairs={{0,1},{1,0},{2,3},{3,2},{4,5},{5,4},{6,7},{7,6},{8,9},{9,8},{10,11... | collective-permute-start | bytes 221192 | tf_op jit(solution)/shard_map/ppermute | solution.py:390
  46.5 1.6 %collective-permute-start.11 = (f32[4,128,128]{2,1,0:T(8,128)S(1)}, f32[4,128,128]{2,1,0:T(8,128)S(1)}, u32[]{:S(2)}, u32[]{:S(2)}) collective-permute-start(f32[4,128,128]{2,1,0:T(8,128)S(1)} %shard_map.90.refs_1_), channel_id=1, source_target_pairs={{0,16},{1,17},{2,18},{3,19},{4,20},{5,21},{6,22},{7,23},{8,24},{9,... | collective-permute-start | bytes 786440 | tf_op jit(solution)/shard_map/ppermute | solution.py:390

commit v2 on v1

--- a/solution.py
+++ b/solution.py
@@ -53,19 +53,18 @@
     return (2.0 * wet_mask(land_ref, rank_ref, tile, rows) - 1.0) * number
 
 
-def sums_kernel(sizes, rank_hbm, temp_hbm, land_hbm, send_ref, keep_ref, rank_ref, temp_ref, land_ref, sem):
+def sums_kernel(
+    sizes, rank_hbm, temp_hbm, kappa_hbm, land_hbm, send_ref, keep_ref, temp_ref, kappa_ref, land_ref, rank_ref, sem
+):
     members, fields, rows, tiles, _ = sizes
     core, mine, other = chunk_number()
-    copies = [
-        pltpu.make_async_copy(rank_hbm, rank_ref, sem.at[0]),
-        pltpu.make_async_copy(land_hbm, land_ref, sem.at[1]),
-        pltpu.make_async_copy(temp_hbm, temp_ref, sem.at[2]),
-    ]
+    pairs = ((rank_hbm, rank_ref), (land_hbm, land_ref), (temp_hbm, temp_ref), (kappa_hbm, kappa_ref))
+    copies = [pltpu.make_async_copy(*pair, sem.at[number]) for number, pair in enumerate(pairs)]
     for copy in copies:
         copy.start()
     send_ref[...] = jnp.zeros_like(send_ref)
     keep_ref[...] = jnp.zeros_like(keep_ref)
-    for copy in copies:
+    for copy in copies[:3]:
         copy.wait()
     for tile in range(tiles):
         lanes = slice(tile * LANES, (tile + 1) * LANES)
@@ -80,6 +79,8 @@
                     total = total + temp_ref[member * fields + field, :, lanes] * wet
                 ref[jnp.bitwise_xor(slot, rank)] = total
 
+    copies[3].wait()
+
 
 def pack_kernel(sizes, rank_ref, temp_ref, kappa_ref, land_ref, pack_ref):
     _, fields, rows, tiles, _ = sizes
@@ -98,7 +99,7 @@
             pack_ref[fields + 3, rank] = signed_number(land_ref, rank_ref, core, tile, rows, tiles)
 
 
-def weights_kernel(sizes, rank_ref, kappa_ref, land_ref, pack_ref, weight_ref, pad_ref):
+def weights_kernel(sizes, rank_ref, kappa_ref, land_ref, pack_ref, weight_ref, pad_ref, face_ref):
     _, fields, rows, tiles, slots = sizes
     core, _, _ = chunk_number()
     band = float(2 * tiles)
@@ -140,45 +141,52 @@
         rolled = [pltpu.roll(x, 1, axis=1) for x in values]
         return [jnp.where(is_first, joined[t - 1] * rolled[t - 1], rolled[t]) for t in range(slots)]
 
-    def same(values):
-        return values
-
     def each(f, *lists):
         return [f(*values) for values in zip(*lists, strict=True)]
 
-    def load(part, start):
-        values = [pad_ref[part, slot, start : start + 8, :] for slot in range(slots)]
-        return [(x > 0.0).astype(jnp.float32) for x in values] if part == 3 else values
-
+    def load(ref, part, start):
+        return [ref[part, slot, start : start + 8, :] for slot in range(slots)]
+
+    def flags(start):
+        return [(x > 0.0).astype(jnp.float32) for x in load(pad_ref, 3, start)]
+
+    for part in range(4):
+        for slot in range(slots):
+            face_ref[part, slot, :PAD, :] = zeros
     for block in range(rows // 8):
         start = PAD + 8 * block
-        kxx, kyy, kxy, wet = (load(part, start) for part in range(4))
-        kyy_n, kxy_n, wet_n = (load(part, start + 1) for part in (1, 2, 3))
-        kyy_s, kxy_s, wet_s = (load(part, start - 1) for part in (1, 2, 3))
-        x_gate = each(lambda w, e: w * e, wet, east(wet))
+        kyy, kxy, wet = load(pad_ref, 1, start), load(pad_ref, 2, start), flags(start)
+        kyy_n, kxy_n, wet_n = load(pad_ref, 1, start + 1), load(pad_ref, 2, start + 1), flags(start + 1)
         y_gate = each(lambda w, n: w * n, wet, wet_n)
-        s_gate = each(lambda w, n: w * n, wet_s, wet)
+        ay = each(lambda k, n, g: 0.5 * (k + n) * g, kyy, kyy_n, y_gate)
+        cy = each(lambda k, n, g: 0.125 * (k + n) * g, kxy, kxy_n, y_gate)
+        for part, values in enumerate((cy, west(cy), east(cy), ay)):
+            for slot in range(slots):
+                face_ref[part, slot, start : start + 8, :] = values[slot]
+    for block in range(rows // 8):
+        start = PAD + 8 * block
+        kxx, kxy, wet = load(pad_ref, 0, start), load(pad_ref, 2, start), flags(start)
+        wet_e, wet_w = east(wet), west(wet)
+        x_gate = each(lambda w, e: w * e, wet, wet_e)
         ax = each(lambda k, e, g: 0.5 * (k + e) * g, kxx, east(kxx), x_gate)
         cx = each(lambda k, e, g: 0.125 * (k + e) * g, kxy, east(kxy), x_gate)
-        ay = each(lambda k, n, g: 0.5 * (k + n) * g, kyy, kyy_n, y_gate)
-        cy = each(lambda k, n, g: 0.125 * (k + n) * g, kxy, kxy_n, y_gate)
-        ays = each(lambda k, n, g: 0.5 * (k + n) * g, kyy_s, kyy, s_gate)
-        cys = each(lambda k, n, g: 0.125 * (k + n) * g, kxy_s, kxy, s_gate)
         axw, cxw = west(ax), west(cx)
-        groups = (
-            (same, lambda: each(lambda w, a, b, c, d: 1.0 - w * (a + b + c + d), wet, ax, axw, ay, ays)),
-            (same, lambda: each(lambda w, a, b, c: w * (a + b - c), wet, ay, cx, cxw)),
-            (same, lambda: each(lambda w, a, b, c: w * (a - b + c), wet, ays, cx, cxw)),
-            (west, lambda: each(lambda w, a, b, c: w * (a + b - c), wet, ax, cy, cys)),
-            (west, lambda: each(lambda w, a, b: w * (a + b), wet, cx, cy)),
-            (west, lambda: each(lambda w, a, b: w * (-a - b), wet, cx, cys)),
-            (east, lambda: each(lambda w, a, b, c: w * (a - b + c), wet, axw, cy, cys)),
-            (east, lambda: each(lambda w, a, b: w * (-a - b), wet, cxw, cy)),
-            (east, lambda: each(lambda w, a, b: w * (a + b), wet, cxw, cys)),
+        cy, cyw, cye, ay = (load(face_ref, part, start) for part in range(4))
+        cysw, cyse, ays = (load(face_ref, part, start - 1) for part in (1, 2, 3))
+        terms = (
+            each(lambda w, a, b, c, d: 1.0 - w * (a + b + c + d), wet, ax, axw, ay, ays),
+            each(lambda w, a, b, c: w * (a + b - c), wet, ay, cx, cxw),
+            each(lambda w, a, b, c: w * (a - b + c), wet, ays, cx, cxw),
+            each(lambda w, a, b, c: w * (a + b - c), wet_w, axw, cyw, cysw),
+            each(lambda w, a, b: w * (a + b), wet_w, cxw, cyw),
+            each(lambda w, a, b: w * (-a - b), wet_w, cxw, cysw),
+            each(lambda w, a, b, c: w * (a - b + c), wet_e, ax, cye, cyse),
+            each(lambda w, a, b: w * (-a - b), wet_e, cx, cye),
+            each(lambda w, a, b: w * (a + b), wet_e, cx, cyse),
         )
-        for number, (move, terms) in enumerate(groups):
-            for slot, term in enumerate(move(terms())):
-                weight_ref[number, slot, 8 * block : 8 * block + 8, :] = term
+        for number, values in enumerate(terms):
+            for slot in range(slots):
+                weight_ref[number, slot, 8 * block : 8 * block + 8, :] = values[slot]
 
 
 def run_steps(planes, rows, slots, weight_ref, u_ref):
@@ -411,26 +419,30 @@
     cell = obs_cell.reshape(1, count)
     masks = {1: (1, 2), 2: (2, 1), 3: (3, 3)}
 
-    send, keep = call(
-        sums_kernel, (struct(slots, rows, LANES), struct(slots, rows, LANES)), (wet_rank, temp, land),
-        scratch=[
-            pltpu.SMEM((tiles,), jnp.int32),
-            pltpu.VMEM((planes, rows, columns), jnp.float32),
-            pltpu.VMEM((tiles, LANES), jnp.int32),
-            pltpu.SemaphoreType.DMA((3,)),
-        ],
-        in_specs=[HBM] * 3,
+    inputs = tuple(pltpu.with_memory_space_constraint(x, pltpu.HBM) for x in (wet_rank, temp, diffusivity, land))
+    send, keep, temp, kappa, land = call(
+        sums_kernel,
+        (
+            struct(slots, rows, LANES),
+            struct(slots, rows, LANES),
+            struct(planes, rows, columns),
+            struct(*diffusivity.shape),
+            jax.ShapeDtypeStruct((tiles, LANES), jnp.int32),
+        ),
+        inputs,
+        scratch=[pltpu.SMEM((tiles,), jnp.int32), pltpu.SemaphoreType.DMA((4,))],
+        in_specs=[HBM] * 4,
     )
     arrived = exchange(send, None)
-    pack = call(pack_kernel, struct(fields + 4, slots, rows, LANES), (wet_rank, temp, diffusivity, land))
+    pack = call(pack_kernel, struct(fields + 4, slots, rows, LANES), (wet_rank, temp, kappa, land))
     packed = exchange(pack, None)
     total = keep + arrived
     got = [exchange(total[k], masks[k]) for k in (1, 2, 3)]
     total = (total[0] + got[0]) + (got[1] + got[2])
 
     weights = call(
-        weights_kernel, struct(9, slots, rows, LANES), (wet_rank, diffusivity, land, packed),
-        [pltpu.VMEM((4, slots, rows + 2 * PAD, LANES), jnp.float32)],
+        weights_kernel, struct(9, slots, rows, LANES), (wet_rank, kappa, land, packed),
+        [pltpu.VMEM((4, slots, rows + 2 * PAD, LANES), jnp.float32)] * 2,
     )
     own = call(
         member_kernel, struct(fields, slots, rows, LANES), (wet_rank, temp, land, packed, weights),

time: 51.4 us -> 47.1 us (0.916)
  local copies, waits for them, and re-layouts: 3.76 us -> 0.06 us
  waiting for transfers between devices: 18.2 us -> 17.6 us
    unnamed x22 -> x10, local copies, waits for them, and re-layouts: 3.73 us -> 0.03 us
    ppermute x12, waiting for transfers between devices: 18.2 us -> 17.6 us  [exchange(): return lax.ppermute(value, ALL_AXES, pairs)]
  transfers between devices with their start and end apart: 12 -> 12, of which waited for: 9 -> 10; matrix products, arithmetic and copies ran while one was open for 0% -> 0% of each run, Pallas kernels for 1% -> 0%
where the time goes in v2:
time: 47.1 us; the launch traced here: 46.9 us
  waiting for transfers between devices  17.6 us (37%)
  Pallas kernels  15.1 us (32%)
  starting transfers between devices  13.3 us (28%)
  between operations  0.83 us (2%)
    ppermute x12, waiting for transfers between devices, exchange(): return lax.ppermute(value, ALL_AXES, pairs)  17.6 us
    pallas_call x7, Pallas kernels, call(): pl.pallas_call(functools.partial(kernel, sizes), out_shape=out_shape, in_...  15.1 us
    ppermute x12, starting transfers between devices, exchange(): return lax.ppermute(value, ALL_AXES, pairs)  13.3 us
  transfers between devices with their start and end apart: 12, of which 10 were waited for; matrix products, arithmetic and copies ran while one was open for 0% of the time, Pallas kernels for 0%

profile of v2, /device:TPU:0, one launch (start us, length us, event | category | flops | bytes accessed | tf_op | source)
XLA Modules:
  0.0 46.9 jit_solution(15053903222641798116)
XLA Ops:
  0.6 0.0 copy-start
  0.6 1.5 %shard_map.85 = (f32[4,128,128]{2,1,0:T(8,128)S(1)}, f32[4,128,128]{2,1,0:T(8,128)S(1)}, f32[4,128,512]{2,1,0:T(8,128)S(1)}, f32[3,128,512]{2,1,0:T(8,128)S(1)}, s32[4,128]{1,0:T(4,128)S(1)}) custom-call(s32[4]{0:T(128)} %refs_0_.1, f32[4,128,512]{2,1,0:T(8,128)} %bitcast.27, f32[3,128,512]{2,1,0:T(8,128)} %kappa_hbm.1, s32[4,128]{1,0:T(4,128)} %bitcast.29), custom_call_target="tpu_custom_call" | custom-call | flops 4096000 | bytes 1048576 | tf_op jit(solution)/shard_map/pallas_call | solution.py:404
  2.2 0.0 copy-done
  2.2 0.7 %shard_map.86 = f32[6,4,128,128]{3,2,1,0:T(8,128)S(1)} custom-call(s32[4]{0:T(128)S(1)} %copy-done, f32[4,128,512]{2,1,0:T(8,128)S(1)} %get-tuple-element.15.temp_ref, f32[3,128,512]{2,1,0:T(8,128)S(1)} %get-tuple-element.17.kappa_ref, s32[4,128]{1,0:T(4,128)S(1)} %get-tuple-element.16.land_ref), custom_call_target="tpu_custom_call" | custom-call | flops 4096000 | bytes 1048576 | tf_op jit(solution)/shard_map/pallas_call | solution.py:404
  2.8 0.6 %collective-permute-start.5 = (f32[6,4,128,128]{3,2,1,0:T(8,128)S(1)}, f32[6,4,128,128]{3,2,1,0:T(8,128)S(1)}, u32[]{:S(2)}, u32[]{:S(2)}) collective-permute-start(f32[6,4,128,128]{3,2,1,0:T(8,128)S(1)} %shard_map.86), channel_id=1, source_target_pairs={{0,16},{1,17},{2,18},{3,19},{4,20},{5,21},{6,22},{7,23},{8,24},{9,... | collective-permute-start | bytes 4718600 | tf_op jit(solution)/shard_map/ppermute | solution.py:398
  3.4 0.1 collective-permute-start
  3.5 3.3 %collective-permute-done = f32[4,128,128]{2,1,0:T(8,128)S(1)} collective-permute-done((f32[4,128,128]{2,1,0:T(8,128)S(1)}, f32[4,128,128]{2,1,0:T(8,128)S(1)}, u32[]{:S(2)}, u32[]{:S(2)}) %collective-permute-start) | collective-permute-done | bytes 262176 | tf_op jit(solution)/shard_map/ppermute | solution.py:398
  6.8 0.0 collective-permute-done.5.pack_ref
  6.8 2.3 %shard_map.87.weight_ref.refs_1_ = f32[9,4,128,128]{3,2,1,0:T(8,128)S(1)} custom-call(s32[4]{0:T(128)S(1)} %copy-done, f32[3,128,512]{2,1,0:T(8,128)S(1)} %get-tuple-element.17.kappa_ref, s32[4,128]{1,0:T(4,128)S(1)} %get-tuple-element.16.land_ref, f32[6,4,128,128]{3,2,1,0:T(8,128)S(1)} %collective-permute-done.5.pack_ref), custom_call_target="tpu_custom_call" | custom-call | flops 4096000 | bytes 1048576 | tf_op jit(solution)/shard_map/pallas_call | solution.py:404
  9.1 0.0 copy-start.1
  9.1 0.0 copy-start.2
  9.1 3.7 %shard_map.88.own_ref = f32[2,4,128,128]{3,2,1,0:T(8,128)S(1)} custom-call(s32[4]{0:T(128)S(1)} %copy-done, f32[4,128,512]{2,1,0:T(8,128)S(1)} %get-tuple-element.15.temp_ref, s32[4,128]{1,0:T(4,128)S(1)} %get-tuple-element.16.land_ref, f32[6,4,128,128]{3,2,1,0:T(8,128)S(1)} %collective-permute-done.5.pack_ref, ...), custom_call_target="tpu_custom_call" | custom-call | flops 16384000 | bytes 1048576 | tf_op jit(solution)/shard_map/pallas_call | solution.py:404
  12.9 0.4 collective-permute-start.6
  13.3 3.7 %collective-permute-start.3 = (f32[128,128]{1,0:T(8,128)S(1)}, f32[128,128]{1,0:T(8,128)S(1)}, u32[]{:S(2)}, u32[]{:S(2)}) collective-permute-start(f32[128,128]{1,0:T(8,128)S(1)} %get-tuple-element.26), channel_id=1, source_target_pairs={{0,3},{1,2},{2,1},{3,0},{4,7},{5,6},{6,5},{7,4},{8,11},{9,10},{10,... | collective-permute-start | bytes 196616 | tf_op jit(solution)/shard_map/ppermute | solution.py:398
  17.0 0.4 collective-permute-start.2
  17.5 0.2 collective-permute-start.1
  17.7 2.0 %collective-permute-done.3 = f32[128,128]{1,0:T(8,128)S(1)} collective-permute-done((f32[128,128]{1,0:T(8,128)S(1)}, f32[128,128]{1,0:T(8,128)S(1)}, u32[]{:S(2)}, u32[]{:S(2)}) %collective-permute-start.3) | collective-permute-done | bytes 65568 | tf_op jit(solution)/shard_map/ppermute | solution.py:398
  19.7 1.7 %collective-permute-done.2 = f32[128,128]{1,0:T(8,128)S(1)} collective-permute-done((f32[128,128]{1,0:T(8,128)S(1)}, f32[128,128]{1,0:T(8,128)S(1)}, u32[]{:S(2)}, u32[]{:S(2)}) %collective-permute-start.2) | collective-permute-done | bytes 65568 | tf_op jit(solution)/shard_map/ppermute | solution.py:398
  21.4 0.4 collective-permute-done.1
  21.8 1.6 %collective-permute-start.4 = (f32[128,128]{1,0:T(8,128)S(1)}, f32[128,128]{1,0:T(8,128)S(1)}, u32[]{:S(2)}, u32[]{:S(2)}) collective-permute-start(f32[128,128]{1,0:T(8,128)S(1)} %fusion.1), channel_id=1, source_target_pairs={{0,8},{1,9},{2,10},{3,11},{4,12},{5,13},{6,14},{7,15},{8,0},{9,1},... | collective-permute-start | bytes 196616 | tf_op jit(solution)/shard_map/ppermute | solution.py:398
  23.3 2.8 %collective-permute-done.4 = f32[128,128]{1,0:T(8,128)S(1)} collective-permute-done((f32[128,128]{1,0:T(8,128)S(1)}, f32[128,128]{1,0:T(8,128)S(1)}, u32[]{:S(2)}, u32[]{:S(2)}) %collective-permute-start.4) | collective-permute-done | bytes 65568 | tf_op jit(solution)/shard_map/ppermute | solution.py:398
  26.1 0.0 collective-permute-done.6.other_ref
  26.1 0.0 copy-done.1
  26.1 0.0 copy-done.2
  26.2 1.9 %shard_map.89 = (f32[4,128,512]{2,1,0:T(8,128)S(1)}, f32[8,128]{1,0:T(8,128)S(1)}) custom-call(s32[4]{0:T(128)S(1)} %copy-done, f32[2,4,128,128]{3,2,1,0:T(8,128)S(1)} %shard_map.88.own_ref, f32[2,4,128,128]{3,2,1,0:T(8,128)S(1)} %collective-permute-done.6.other_ref, s32[1,256]{1,0:T(1,128)S(1)} %bitcast.25, f32[2,256]{1,0:T(2,128)S(1)} %copy-done.1), custom_call_target="tpu_custom_call" | custom-call | flops 8192000 | bytes 1048576 | tf_op jit(solution)/shard_map/pallas_call | solution.py:404
  28.0 2.7 %collective-permute-start.7 = (f32[136,128]{1,0:T(8,128)S(1)}, f32[136,128]{1,0:T(8,128)S(1)}, u32[]{:S(2)}, u32[]{:S(2)}) collective-permute-start(f32[136,128]{1,0:T(8,128)S(1)} %pad_maximum_fusion.2), channel_id=1, source_target_pairs={{0,4},{1,5},{2,6},{3,7},{4,0},{5,1},{6,2},{7,3},{8,12},{9,13},{10,... | collective-permute-start | bytes 208904 | tf_op jit(solution)/shard_map/ppermute | solution.py:398
  30.7 2.6 %collective-permute-done.7 = f32[136,128]{1,0:T(8,128)S(1)} collective-permute-done((f32[136,128]{1,0:T(8,128)S(1)}, f32[136,128]{1,0:T(8,128)S(1)}, u32[]{:S(2)}, u32[]{:S(2)}) %collective-permute-start.7) | collective-permute-done | bytes 69664 | tf_op jit(solution)/shard_map/ppermute | solution.py:398
  33.4 1.8 %collective-permute-start.10 = (f32[144,128]{1,0:T(8,128)S(1)}, f32[144,128]{1,0:T(8,128)S(1)}, u32[]{:S(2)}, u32[]{:S(2)}) collective-permute-start(f32[144,128]{1,0:T(8,128)S(1)} %pad_maximum_fusion.1), channel_id=1, source_target_pairs={{0,3},{1,2},{2,1},{3,0},{4,7},{5,6},{6,5},{7,4},{8,11},{9,10},{10,... | collective-permute-start | bytes 221192 | tf_op jit(solution)/shard_map/ppermute | solution.py:398
  35.1 0.7 %collective-permute-start.9 = (f32[144,128]{1,0:T(8,128)S(1)}, f32[144,128]{1,0:T(8,128)S(1)}, u32[]{:S(2)}, u32[]{:S(2)}) collective-permute-start(f32[144,128]{1,0:T(8,128)S(1)} %pad_maximum_fusion.1), channel_id=1, source_target_pairs={{0,2},{1,3},{2,0},{3,1},{4,6},{5,7},{6,4},{7,5},{8,10},{9,11},{10,... | collective-permute-start | bytes 221192 | tf_op jit(solution)/shard_map/ppermute | solution.py:398
  35.9 1.1 %collective-permute-start.8 = (f32[144,128]{1,0:T(8,128)S(1)}, f32[144,128]{1,0:T(8,128)S(1)}, u32[]{:S(2)}, u32[]{:S(2)}) collective-permute-start(f32[144,128]{1,0:T(8,128)S(1)} %pad_maximum_fusion.1), channel_id=1, source_target_pairs={{0,1},{1,0},{2,3},{3,2},{4,5},{5,4},{6,7},{7,6},{8,9},{9,8},{10,11... | collective-permute-start | bytes 221192 | tf_op jit(solution)/shard_map/ppermute | solution.py:398
  36.9 1.8 %collective-permute-done.10 = f32[144,128]{1,0:T(8,128)S(1)} collective-permute-done((f32[144,128]{1,0:T(8,128)S(1)}, f32[144,128]{1,0:T(8,128)S(1)}, u32[]{:S(2)}, u32[]{:S(2)}) %collective-permute-start.10) | collective-permute-done | bytes 73760 | tf_op jit(solution)/shard_map/ppermute | solution.py:398
  38.7 0.8 %collective-permute-done.9 = f32[144,128]{1,0:T(8,128)S(1)} collective-permute-done((f32[144,128]{1,0:T(8,128)S(1)}, f32[144,128]{1,0:T(8,128)S(1)}, u32[]{:S(2)}, u32[]{:S(2)}) %collective-permute-start.9) | collective-permute-done | bytes 73760 | tf_op jit(solution)/shard_map/ppermute | solution.py:398
  39.5 0.7 %collective-permute-done.8 = f32[144,128]{1,0:T(8,128)S(1)} collective-permute-done((f32[144,128]{1,0:T(8,128)S(1)}, f32[144,128]{1,0:T(8,128)S(1)}, u32[]{:S(2)}, u32[]{:S(2)}) %collective-permute-start.8) | collective-permute-done | bytes 73760 | tf_op jit(solution)/shard_map/ppermute | solution.py:398
  40.2 2.0 %shard_map.90.refs_1_ = f32[4,128,128]{2,1,0:T(8,128)S(1)} custom-call(f32[4,128,128]{2,1,0:T(8,128)S(1)} %pad_maximum_fusion.refs_0_, f32[9,4,128,128]{3,2,1,0:T(8,128)S(1)} %shard_map.87.weight_ref.refs_1_), custom_call_target="tpu_custom_call" | custom-call | flops 8192000 | bytes 1048576 | tf_op jit(solution)/shard_map/pallas_call | solution.py:404
  42.3 0.1 collective-permute-start.11
  42.4 1.5 %collective-permute-done.11.refs_2_ = f32[4,128,128]{2,1,0:T(8,128)S(1)} collective-permute-done((f32[4,128,128]{2,1,0:T(8,128)S(1)}, f32[4,128,128]{2,1,0:T(8,128)S(1)}, u32[]{:S(2)}, u32[]{:S(2)}) %collective-permute-start.11) | collective-permute-done | bytes 262176 | tf_op jit(solution)/shard_map/ppermute | solution.py:398
  43.9 3.1 %shard_map.91 = (f32[4,128,512]{2,1,0:T(8,128)}, f32[2,2,256]{2,1,0:T(2,128)}, f32[2,256]{1,0:T(2,128)}) custom-call(s32[4]{0:T(128)S(1)} %copy-done, f32[4,128,128]{2,1,0:T(8,128)S(1)} %shard_map.90.refs_1_, f32[4,128,128]{2,1,0:T(8,128)S(1)} %collective-permute-done.11.refs_2_, s32[1,256]{1,0:T(1,128)S(1)} %bitcast.26, f32[2,256]{1,0:T(2,128)S(1)} %copy-done.1, ...), custom_call_target="tpu_custom_call" | custom-call | flops 4096000 | bytes 1048576 | tf_op jit(solution)/shard_map/pallas_call | solution.py:404
  (16 shorter events, 0.2 us)
Async XLA Ops:
  0.6 1.5 %copy-start = (s32[4]{0:T(128)S(1)}, s32[4]{0:T(128)}, u32[]{:S(2)}) copy-start(s32[4]{0:T(128)} %refs_0_.1) | copy-start | bytes 52
  2.8 4.0 %collective-permute-start.5 = (f32[6,4,128,128]{3,2,1,0:T(8,128)S(1)}, f32[6,4,128,128]{3,2,1,0:T(8,128)S(1)}, u32[]{:S(2)}, u32[]{:S(2)}) collective-permute-start(f32[6,4,128,128]{3,2,1,0:T(8,128)S(1)} %shard_map.86), channel_id=1, source_target_pairs={{0,16},{1,17},{2,18},{3,19},{4,20},{5,21},{6,22},{7,23},{8,24},{9,... | collective-permute-start | bytes 4718600 | tf_op jit(solution)/shard_map/ppermute | solution.py:398
  3.4 3.4 %collective-permute-start = (f32[4,128,128]{2,1,0:T(8,128)S(1)}, f32[4,128,128]{2,1,0:T(8,128)S(1)}, u32[]{:S(2)}, u32[]{:S(2)}) collective-permute-start(f32[4,128,128]{2,1,0:T(8,128)S(1)} %get-tuple-element.14), channel_id=1, source_target_pairs={{0,16},{1,17},{2,18},{3,19},{4,20},{5,21},{6,22},{7,23},{8,24},{9,... | collective-permute-start | bytes 786440 | tf_op jit(solution)/shard_map/ppermute | solution.py:398
  9.1 17.0 %copy-start.1 = (f32[2,256]{1,0:T(2,128)S(1)}, f32[2,256]{1,0:T(2,128)}, u32[]{:S(2)}) copy-start(f32[2,256]{1,0:T(2,128)} %refs_4_.1) | copy-start | bytes 6148
  9.1 17.0 %copy-start.2 = (s32[256]{0:T(256)S(1)}, s32[256]{0:T(256)}, u32[]{:S(2)}) copy-start(s32[256]{0:T(256)} %param.10) | copy-start | bytes 3076
  12.9 13.2 %collective-permute-start.6 = (f32[2,4,128,128]{3,2,1,0:T(8,128)S(1)}, f32[2,4,128,128]{3,2,1,0:T(8,128)S(1)}, u32[]{:S(2)}, u32[]{:S(2)}) collective-permute-start(f32[2,4,128,128]{3,2,1,0:T(8,128)S(1)} %shard_map.88.own_ref), channel_id=1, source_target_pairs={{0,16},{1,17},{2,18},{3,19},{4,20},{5,21},{6,22},{7,23},{8,24},{9,... | collective-permute-start | bytes 1572872 | tf_op jit(solution)/shard_map/ppermute | solution.py:398
  13.3 6.4 %collective-permute-start.3 = (f32[128,128]{1,0:T(8,128)S(1)}, f32[128,128]{1,0:T(8,128)S(1)}, u32[]{:S(2)}, u32[]{:S(2)}) collective-permute-start(f32[128,128]{1,0:T(8,128)S(1)} %get-tuple-element.26), channel_id=1, source_target_pairs={{0,3},{1,2},{2,1},{3,0},{4,7},{5,6},{6,5},{7,4},{8,11},{9,10},{10,... | collective-permute-start | bytes 196616 | tf_op jit(solution)/shard_map/ppermute | solution.py:398
  17.0 4.3 %collective-permute-start.2 = (f32[128,128]{1,0:T(8,128)S(1)}, f32[128,128]{1,0:T(8,128)S(1)}, u32[]{:S(2)}, u32[]{:S(2)}) collective-permute-start(f32[128,128]{1,0:T(8,128)S(1)} %get-tuple-element.27), channel_id=1, source_target_pairs={{0,2},{1,3},{2,0},{3,1},{4,6},{5,7},{6,4},{7,5},{8,10},{9,11},{10,... | collective-permute-start | bytes 196616 | tf_op jit(solution)/shard_map/ppermute | solution.py:398
  17.5 4.3 %collective-permute-start.1 = (f32[128,128]{1,0:T(8,128)S(1)}, f32[128,128]{1,0:T(8,128)S(1)}, u32[]{:S(2)}, u32[]{:S(2)}) collective-permute-start(f32[128,128]{1,0:T(8,128)S(1)} %get-tuple-element.28), channel_id=1, source_target_pairs={{0,1},{1,0},{2,3},{3,2},{4,5},{5,4},{6,7},{7,6},{8,9},{9,8},{10,11... | collective-permute-start | bytes 196616 | tf_op jit(solution)/shard_map/ppermute | solution.py:398
  21.8 4.3 %collective-permute-start.4 = (f32[128,128]{1,0:T(8,128)S(1)}, f32[128,128]{1,0:T(8,128)S(1)}, u32[]{:S(2)}, u32[]{:S(2)}) collective-permute-start(f32[128,128]{1,0:T(8,128)S(1)} %fusion.1), channel_id=1, source_target_pairs={{0,8},{1,9},{2,10},{3,11},{4,12},{5,13},{6,14},{7,15},{8,0},{9,1},... | collective-permute-start | bytes 196616 | tf_op jit(solution)/shard_map/ppermute | solution.py:398
  28.0 5.3 %collective-permute-start.7 = (f32[136,128]{1,0:T(8,128)S(1)}, f32[136,128]{1,0:T(8,128)S(1)}, u32[]{:S(2)}, u32[]{:S(2)}) collective-permute-start(f32[136,128]{1,0:T(8,128)S(1)} %pad_maximum_fusion.2), channel_id=1, source_target_pairs={{0,4},{1,5},{2,6},{3,7},{4,0},{5,1},{6,2},{7,3},{8,12},{9,13},{10,... | collective-permute-start | bytes 208904 | tf_op jit(solution)/shard_map/ppermute | solution.py:398
  33.4 5.3 %collective-permute-start.10 = (f32[144,128]{1,0:T(8,128)S(1)}, f32[144,128]{1,0:T(8,128)S(1)}, u32[]{:S(2)}, u32[]{:S(2)}) collective-permute-start(f32[144,128]{1,0:T(8,128)S(1)} %pad_maximum_fusion.1), channel_id=1, source_target_pairs={{0,3},{1,2},{2,1},{3,0},{4,7},{5,6},{6,5},{7,4},{8,11},{9,10},{10,... | collective-permute-start | bytes 221192 | tf_op jit(solution)/shard_map/ppermute | solution.py:398
  35.1 4.4 %collective-permute-start.9 = (f32[144,128]{1,0:T(8,128)S(1)}, f32[144,128]{1,0:T(8,128)S(1)}, u32[]{:S(2)}, u32[]{:S(2)}) collective-permute-start(f32[144,128]{1,0:T(8,128)S(1)} %pad_maximum_fusion.1), channel_id=1, source_target_pairs={{0,2},{1,3},{2,0},{3,1},{4,6},{5,7},{6,4},{7,5},{8,10},{9,11},{10,... | collective-permute-start | bytes 221192 | tf_op jit(solution)/shard_map/ppermute | solution.py:398
  35.9 4.4 %collective-permute-start.8 = (f32[144,128]{1,0:T(8,128)S(1)}, f32[144,128]{1,0:T(8,128)S(1)}, u32[]{:S(2)}, u32[]{:S(2)}) collective-permute-start(f32[144,128]{1,0:T(8,128)S(1)} %pad_maximum_fusion.1), channel_id=1, source_target_pairs={{0,1},{1,0},{2,3},{3,2},{4,5},{5,4},{6,7},{7,6},{8,9},{9,8},{10,11... | collective-permute-start | bytes 221192 | tf_op jit(solution)/shard_map/ppermute | solution.py:398
  42.3 1.6 %collective-permute-start.11 = (f32[4,128,128]{2,1,0:T(8,128)S(1)}, f32[4,128,128]{2,1,0:T(8,128)S(1)}, u32[]{:S(2)}, u32[]{:S(2)}) collective-permute-start(f32[4,128,128]{2,1,0:T(8,128)S(1)} %shard_map.90.refs_1_), channel_id=1, source_target_pairs={{0,16},{1,17},{2,18},{3,19},{4,20},{5,21},{6,22},{7,23},{8,24},{9,... | collective-permute-start | bytes 786440 | tf_op jit(solution)/shard_map/ppermute | solution.py:398

commit v3 on v2

--- a/solution.py
+++ b/solution.py
@@ -133,13 +133,14 @@
 
     def east(values):
         rolled = [pltpu.roll(x, LANES - 1, axis=1) for x in values]
-        return [
-            jnp.where(is_last, joined[t] * rolled[(t + 1) % slots], rolled[t]) for t in range(slots)
-        ]
+        return [jnp.where(is_last, rolled[(t + 1) % slots], rolled[t]) for t in range(slots)]
 
     def west(values):
         rolled = [pltpu.roll(x, 1, axis=1) for x in values]
-        return [jnp.where(is_first, joined[t - 1] * rolled[t - 1], rolled[t]) for t in range(slots)]
+        return [jnp.where(is_first, rolled[t - 1], rolled[t]) for t in range(slots)]
+
+    to_east = [jnp.where(is_last, joined[t], 1.0) for t in range(slots)]
+    to_west = [jnp.where(is_first, joined[t - 1], 1.0) for t in range(slots)]
 
     def each(f, *lists):
         return [f(*values) for values in zip(*lists, strict=True)]
@@ -166,7 +167,8 @@
     for block in range(rows // 8):
         start = PAD + 8 * block
         kxx, kxy, wet = load(pad_ref, 0, start), load(pad_ref, 2, start), flags(start)
-        wet_e, wet_w = east(wet), west(wet)
+        wet_e = each(lambda w, j: w * j, east(wet), to_east)
+        wet_w = each(lambda w, j: w * j, west(wet), to_west)
         x_gate = each(lambda w, e: w * e, wet, wet_e)
         ax = each(lambda k, e, g: 0.5 * (k + e) * g, kxx, east(kxx), x_gate)
         cx = each(lambda k, e, g: 0.125 * (k + e) * g, kxy, east(kxy), x_gate)
@@ -318,12 +320,71 @@
             seen_ref[at : at + 1, :] = seen[:, half * LANES : (half + 1) * LANES]
 
 
+def picks_kernel(sizes, cell_ref, frac_ref, column_ref, row_ref):
+    _, _, rows, tiles, _ = sizes
+    columns, count = tiles * LANES, cell_ref.shape[1]
+    cell, frac = cell_ref[...], frac_ref[...]
+    column, row = lax.rem(cell, columns), lax.rem(cell // columns, rows)
+    at = lax.broadcasted_iota(jnp.int32, (columns, count), 0) - column
+    pick = jnp.where(at == 0, 1.0 - frac[0:1, :], jnp.where(at == 1, frac[0:1, :], 0.0))
+    for number, part in enumerate(split_parts(pick)):
+        for place in ((0, 1, 2), (3, 4), (5,))[number]:
+            column_ref[place * columns : (place + 1) * columns, :] = part
+    at = lax.broadcasted_iota(jnp.int32, (rows, count), 0) - row
+    row_ref[...] = jnp.where(at == 0, 1.0 - frac[1:2, :], jnp.where(at == 1, frac[1:2, :], 0.0))
+
+
+def split_parts(values):
+    high = values.astype(jnp.bfloat16)
+    rest = values - high.astype(jnp.float32)
+    middle = rest.astype(jnp.bfloat16)
+    low = (rest - middle.astype(jnp.float32)).astype(jnp.bfloat16)
+    return high, middle, low
+
+
+def split_values(values):
+    high, middle, low = split_parts(values)
+    return jnp.concatenate([high, middle, low, high, middle, high], axis=1)
+
+
+def own_field_kernel(sizes, rank_ref, mean_ref, stepped_ref, field_hbm, field_ref, sem):
+    members, _, _, _, _ = sizes
+    core, _, _ = chunk_number()
+    write_planes(sizes, core, rank_ref, mean_ref, stepped_ref, field_hbm, field_ref, sem)
+    for member in range(members):
+        plane_copy(sizes, member, core, field_hbm, field_ref, sem).wait()
+
+
+def plane_copy(sizes, member, field, field_hbm, field_ref, sem):
+    _, fields, _, _, _ = sizes
+    return pltpu.make_async_copy(field_ref.at[member], field_hbm.at[member * fields + field], sem.at[member])
+
+
+def write_planes(sizes, field, rank_ref, mean_ref, stepped_ref, field_hbm, field_ref, sem):
+    members, fields, _, tiles, _ = sizes
+    for member in range(members):
+        for tile in range(tiles):
+            lanes = slice(tile * LANES, (tile + 1) * LANES)
+            rank = rank_ref[tile]
+
+            @pl.when(rank >= 0)
+            def _():
+                field_ref[member, :, lanes] = stepped_ref[member * fields + field, :, lanes] - mean_ref[rank]
+
+            @pl.when(rank < 0)
+            def _():
+                field_ref[member, :, lanes] = stepped_ref[member * fields + field, :, lanes]
+
+        plane_copy(sizes, member, field, field_hbm, field_ref, sem).start()
+
+
 def final_kernel(
-    sizes, ensemble, rank_ref, own_ref, other_ref, cell_ref, frac_ref, seen_ref, stepped_ref,
-    field_hbm, anomaly_ref, variance_ref, field_ref, mean_ref, sem,
+    sizes, ensemble, rank_ref, own_ref, other_ref, column_ref, row_ref, seen_ref, stepped_ref, started_hbm,
+    field_hbm, anomaly_hbm, variance_hbm, field_ref, mean_ref, anomaly_ref, variance_ref, sem,
 ):
     members, fields, rows, tiles, _ = sizes
     core, _, _ = chunk_number()
+    write_planes(sizes, 1 - core, rank_ref, other_ref, stepped_ref, field_hbm, field_ref, sem)
     for tile in range(tiles):
         lanes = slice(tile * LANES, (tile + 1) * LANES)
         rank = rank_ref[tile]
@@ -338,14 +399,9 @@
             for field in range(fields):
                 mean_ref[field, :, lanes] = jnp.zeros((rows, LANES), jnp.float32)
 
-    for member in range(members):
-        for field in range(fields):
-            plane = member * fields + field
-            field_ref[plane] = stepped_ref[plane] - mean_ref[field]
-    copy = pltpu.make_async_copy(field_ref, field_hbm, sem)
-    copy.start()
-    mean_seen = observe_planes([mean_ref[field] for field in range(fields)], cell_ref[...], frac_ref[...])
-    halves = cell_ref.shape[1] // LANES
+    values = jnp.concatenate([split_values(mean_ref[field]) for field in range(fields)], axis=0)
+    picked = jnp.dot(values, column_ref[...], preferred_element_type=jnp.float32)
+    halves = row_ref.shape[1] // LANES
     stride = members * fields * halves
     sets = seen_ref.shape[0] // stride
 
@@ -355,9 +411,10 @@
         return values[0]
 
     for field in range(fields):
+        mean_seen = jnp.sum(picked[field * rows : (field + 1) * rows] * row_ref[...], axis=0, keepdims=True)
         for half in range(halves):
             lanes = slice(half * LANES, (half + 1) * LANES)
-            mean = mean_seen[field][:, lanes]
+            mean = mean_seen[:, lanes]
             observed = []
             for part in range(sets):
                 for member in range(members):
@@ -368,7 +425,16 @@
             variance_ref[field : field + 1, lanes] = tree([value * value for value in anomaly]) / ensemble
             for member in range(members):
                 anomaly_ref[member, field : field + 1, lanes] = anomaly[member]
-    copy.wait()
+    small = (
+        pltpu.make_async_copy(anomaly_ref, anomaly_hbm, sem.at[members]),
+        pltpu.make_async_copy(variance_ref, variance_hbm, sem.at[members + 1]),
+    )
+    for copy in small:
+        copy.start()
+    for member in range(members):
+        plane_copy(sizes, member, 1 - core, field_hbm, field_ref, sem).wait()
+    for copy in small:
+        copy.wait()
 
 
 def local(temp_salt, diffusivity, wet_rank, land_rows, obs_cell, obs_frac):
@@ -400,13 +466,14 @@
     def struct(*shape):
         return jax.ShapeDtypeStruct(shape, jnp.float32)
 
-    def call(kernel, out_shape, operands, scratch=(), cycles=1000, in_specs=None, out_specs=None):
+    def call(kernel, out_shape, operands, scratch=(), cycles=1000, in_specs=None, out_specs=None, aliases={}):
         return pl.pallas_call(
             functools.partial(kernel, sizes),
             out_shape=out_shape,
             in_specs=in_specs or [SMEM if x is wet_rank else VMEM for x in operands],
             out_specs=out_specs or jax.tree.map(lambda _: VMEM, out_shape),
             scratch_shapes=list(scratch),
+            input_output_aliases=aliases,
             compiler_params=PARAMS,
             cost_estimate=pl.CostEstimate(flops=cycles * 4096, bytes_accessed=1 << 20, transcendentals=0),
         )(*operands)
@@ -472,20 +539,34 @@
 
     own_mean = call(step_mean, struct(slots, rows, LANES), (gathered, weights), [halo(1)], cycles=2000)
     other_mean = exchange(own_mean, None)
+    column_picks, row_picks = call(
+        picks_kernel,
+        (jax.ShapeDtypeStruct((6 * columns, count), jnp.bfloat16), struct(rows, count)), (cell, obs_frac),
+    )
+    plane_scratch = pltpu.VMEM((members, rows, columns), jnp.float32)
+    started = call(
+        own_field_kernel, struct(planes, rows, columns), (wet_rank, own_mean, stepped),
+        [plane_scratch, pltpu.SemaphoreType.DMA((members,))], out_specs=HBM,
+    )
 
     def last_kernel(sizes, *refs):
         final_kernel(sizes, members * member_count, *refs)
 
+    operands = (wet_rank, own_mean, other_mean, column_picks, row_picks, seen, stepped, started)
     field, anomaly, variance = call(
         last_kernel,
         (struct(planes, rows, columns), struct(members, fields, count), struct(fields, count)),
-        (wet_rank, own_mean, other_mean, cell, obs_frac, seen, stepped),
+        operands,
         [
-            pltpu.VMEM((planes, rows, columns), jnp.float32),
+            plane_scratch,
             pltpu.VMEM((fields, rows, columns), jnp.float32),
-            pltpu.SemaphoreType.DMA,
+            pltpu.VMEM((members, fields, count), jnp.float32),
+            pltpu.VMEM((fields, count), jnp.float32),
+            pltpu.SemaphoreType.DMA((members + 2,)),
         ],
-        out_specs=(HBM, VMEM, VMEM),
+        in_specs=[SMEM] + [VMEM] * 6 + [HBM],
+        out_specs=(HBM, HBM, HBM),
+        aliases={len(operands) - 1: 0},
     )
     return field.reshape(members, fields, levels, rows, columns), anomaly, variance
 

time: 47.1 us -> 47.6 us (1.011)
  Pallas kernels: 15.1 us -> 15.7 us
    pallas_call x7 -> x9, Pallas kernels: 15.1 us -> 15.7 us  [call(): pl.pallas_call(functools.partial(kernel, sizes), out_shape=out_shape, in_...]
  transfers between devices with their start and end apart: 12 -> 12, of which waited for: 10 -> 8; matrix products, arithmetic and copies ran while one was open for 0% -> 0% of each run, Pallas kernels for 0% -> 4%
where the time goes in v3:
time: 47.6 us; the launch traced here: 47.5 us
  waiting for transfers between devices  17.5 us (37%)
  Pallas kernels  15.7 us (33%)
  starting transfers between devices  13.2 us (28%)
  between operations  0.85 us (2%)
    ppermute x12, waiting for transfers between devices, exchange(): return lax.ppermute(value, ALL_AXES, pairs)  17.5 us
    pallas_call x9, Pallas kernels, call(): pl.pallas_call(functools.partial(kernel, sizes), out_shape=out_shape, in_...  15.7 us
    ppermute x12, starting transfers between devices, exchange(): return lax.ppermute(value, ALL_AXES, pairs)  13.2 us
  transfers between devices with their start and end apart: 12, of which 8 were waited for; matrix products, arithmetic and copies ran while one was open for 0% of the time, Pallas kernels for 4%

profile of v3, /device:TPU:0, one launch (start us, length us, event | category | flops | bytes accessed | tf_op | source)
XLA Modules:
  0.0 47.5 jit_solution(9014244973732126032)
XLA Ops:
  0.6 0.0 copy-start
  0.6 1.5 %shard_map.85 = (f32[4,128,128]{2,1,0:T(8,128)S(1)}, f32[4,128,128]{2,1,0:T(8,128)S(1)}, f32[4,128,512]{2,1,0:T(8,128)S(1)}, f32[3,128,512]{2,1,0:T(8,128)S(1)}, s32[4,128]{1,0:T(4,128)S(1)}) custom-call(s32[4]{0:T(128)} %refs_0_.1, f32[4,128,512]{2,1,0:T(8,128)} %bitcast.28, f32[3,128,512]{2,1,0:T(8,128)} %kappa_hbm.1, s32[4,128]{1,0:T(4,128)} %bitcast.30), custom_call_target="tpu_custom_call" | custom-call | flops 4096000 | bytes 1048576 | tf_op jit(solution)/shard_map/pallas_call | solution.py:470
  2.2 0.0 copy-done
  2.2 0.7 %shard_map.86 = f32[6,4,128,128]{3,2,1,0:T(8,128)S(1)} custom-call(s32[4]{0:T(128)S(1)} %copy-done, f32[4,128,512]{2,1,0:T(8,128)S(1)} %get-tuple-element.17.temp_ref, f32[3,128,512]{2,1,0:T(8,128)S(1)} %get-tuple-element.19.kappa_ref, s32[4,128]{1,0:T(4,128)S(1)} %get-tuple-element.18.land_ref), custom_call_target="tpu_custom_call" | custom-call | flops 4096000 | bytes 1048576 | tf_op jit(solution)/shard_map/pallas_call | solution.py:470
  2.8 0.6 %collective-permute-start.5 = (f32[6,4,128,128]{3,2,1,0:T(8,128)S(1)}, f32[6,4,128,128]{3,2,1,0:T(8,128)S(1)}, u32[]{:S(2)}, u32[]{:S(2)}) collective-permute-start(f32[6,4,128,128]{3,2,1,0:T(8,128)S(1)} %shard_map.86), channel_id=1, source_target_pairs={{0,16},{1,17},{2,18},{3,19},{4,20},{5,21},{6,22},{7,23},{8,24},{9,... | collective-permute-start | bytes 4718600 | tf_op jit(solution)/shard_map/ppermute | solution.py:464
  3.4 0.1 collective-permute-start
  3.5 3.3 %collective-permute-done = f32[4,128,128]{2,1,0:T(8,128)S(1)} collective-permute-done((f32[4,128,128]{2,1,0:T(8,128)S(1)}, f32[4,128,128]{2,1,0:T(8,128)S(1)}, u32[]{:S(2)}, u32[]{:S(2)}) %collective-permute-start) | collective-permute-done | bytes 262176 | tf_op jit(solution)/shard_map/ppermute | solution.py:464
  6.8 0.0 collective-permute-done.5.pack_ref
  6.8 2.2 %shard_map.87.weight_ref.refs_1_ = f32[9,4,128,128]{3,2,1,0:T(8,128)S(1)} custom-call(s32[4]{0:T(128)S(1)} %copy-done, f32[3,128,512]{2,1,0:T(8,128)S(1)} %get-tuple-element.19.kappa_ref, s32[4,128]{1,0:T(4,128)S(1)} %get-tuple-element.18.land_ref, f32[6,4,128,128]{3,2,1,0:T(8,128)S(1)} %collective-permute-done.5.pack_ref), custom_call_target="tpu_custom_call" | custom-call | flops 4096000 | bytes 1048576 | tf_op jit(solution)/shard_map/pallas_call | solution.py:470
  9.1 0.0 copy-start.1
  9.1 0.0 copy-start.2
  9.1 3.7 %shard_map.88.own_ref = f32[2,4,128,128]{3,2,1,0:T(8,128)S(1)} custom-call(s32[4]{0:T(128)S(1)} %copy-done, f32[4,128,512]{2,1,0:T(8,128)S(1)} %get-tuple-element.17.temp_ref, s32[4,128]{1,0:T(4,128)S(1)} %get-tuple-element.18.land_ref, f32[6,4,128,128]{3,2,1,0:T(8,128)S(1)} %collective-permute-done.5.pack_ref, ...), custom_call_target="tpu_custom_call" | custom-call | flops 16384000 | bytes 1048576 | tf_op jit(solution)/shard_map/pallas_call | solution.py:470
  12.8 0.4 collective-permute-start.6
  13.3 2.7 %collective-permute-start.1 = (f32[128,128]{1,0:T(8,128)S(1)}, f32[128,128]{1,0:T(8,128)S(1)}, u32[]{:S(2)}, u32[]{:S(2)}) collective-permute-start(f32[128,128]{1,0:T(8,128)S(1)} %get-tuple-element.32), channel_id=1, source_target_pairs={{0,1},{1,0},{2,3},{3,2},{4,5},{5,4},{6,7},{7,6},{8,9},{9,8},{10,11... | collective-permute-start | bytes 196616 | tf_op jit(solution)/shard_map/ppermute | solution.py:464
  16.0 1.6 %collective-permute-start.2 = (f32[128,128]{1,0:T(8,128)S(1)}, f32[128,128]{1,0:T(8,128)S(1)}, u32[]{:S(2)}, u32[]{:S(2)}) collective-permute-start(f32[128,128]{1,0:T(8,128)S(1)} %get-tuple-element.31), channel_id=1, source_target_pairs={{0,2},{1,3},{2,0},{3,1},{4,6},{5,7},{6,4},{7,5},{8,10},{9,11},{10,... | collective-permute-start | bytes 196616 | tf_op jit(solution)/shard_map/ppermute | solution.py:464
  17.6 0.0 collective-permute-start.3
  17.6 0.7 %collective-permute-done.1 = f32[128,128]{1,0:T(8,128)S(1)} collective-permute-done((f32[128,128]{1,0:T(8,128)S(1)}, f32[128,128]{1,0:T(8,128)S(1)}, u32[]{:S(2)}, u32[]{:S(2)}) %collective-permute-start.1) | collective-permute-done | bytes 65568 | tf_op jit(solution)/shard_map/ppermute | solution.py:464
  18.2 2.3 %collective-permute-done.2 = f32[128,128]{1,0:T(8,128)S(1)} collective-permute-done((f32[128,128]{1,0:T(8,128)S(1)}, f32[128,128]{1,0:T(8,128)S(1)}, u32[]{:S(2)}, u32[]{:S(2)}) %collective-permute-start.2) | collective-permute-done | bytes 65568 | tf_op jit(solution)/shard_map/ppermute | solution.py:464
  20.6 2.2 %collective-permute-done.3 = f32[128,128]{1,0:T(8,128)S(1)} collective-permute-done((f32[128,128]{1,0:T(8,128)S(1)}, f32[128,128]{1,0:T(8,128)S(1)}, u32[]{:S(2)}, u32[]{:S(2)}) %collective-permute-start.3) | collective-permute-done | bytes 65568 | tf_op jit(solution)/shard_map/ppermute | solution.py:464
  22.7 1.6 %collective-permute-start.4 = (f32[128,128]{1,0:T(8,128)S(1)}, f32[128,128]{1,0:T(8,128)S(1)}, u32[]{:S(2)}, u32[]{:S(2)}) collective-permute-start(f32[128,128]{1,0:T(8,128)S(1)} %fusion.1), channel_id=1, source_target_pairs={{0,8},{1,9},{2,10},{3,11},{4,12},{5,13},{6,14},{7,15},{8,0},{9,1},... | collective-permute-start | bytes 196616 | tf_op jit(solution)/shard_map/ppermute | solution.py:464
  24.3 2.8 %collective-permute-done.4 = f32[128,128]{1,0:T(8,128)S(1)} collective-permute-done((f32[128,128]{1,0:T(8,128)S(1)}, f32[128,128]{1,0:T(8,128)S(1)}, u32[]{:S(2)}, u32[]{:S(2)}) %collective-permute-start.4) | collective-permute-done | bytes 65568 | tf_op jit(solution)/shard_map/ppermute | solution.py:464
  27.1 0.0 collective-permute-done.6.other_ref
  27.1 0.0 copy-done.1
  27.1 0.0 copy-done.2
  27.1 1.9 %shard_map.89 = (f32[4,128,512]{2,1,0:T(8,128)S(1)}, f32[8,128]{1,0:T(8,128)S(1)}) custom-call(s32[4]{0:T(128)S(1)} %copy-done, f32[2,4,128,128]{3,2,1,0:T(8,128)S(1)} %shard_map.88.own_ref, f32[2,4,128,128]{3,2,1,0:T(8,128)S(1)} %collective-permute-done.6.other_ref, s32[1,256]{1,0:T(1,128)S(1)} %bitcast.25, f32[2,256]{1,0:T(2,128)S(1)} %copy-done.1), custom_call_target="tpu_custom_call" | custom-call | flops 8192000 | bytes 1048576 | tf_op jit(solution)/shard_map/pallas_call | solution.py:470
  29.0 2.7 %collective-permute-start.7 = (f32[136,128]{1,0:T(8,128)S(1)}, f32[136,128]{1,0:T(8,128)S(1)}, u32[]{:S(2)}, u32[]{:S(2)}) collective-permute-start(f32[136,128]{1,0:T(8,128)S(1)} %pad_maximum_fusion.2), channel_id=1, source_target_pairs={{0,4},{1,5},{2,6},{3,7},{4,0},{5,1},{6,2},{7,3},{8,12},{9,13},{10,... | collective-permute-start | bytes 208904 | tf_op jit(solution)/shard_map/ppermute | solution.py:464
  31.7 3.4 %collective-permute-done.7 = f32[136,128]{1,0:T(8,128)S(1)} collective-permute-done((f32[136,128]{1,0:T(8,128)S(1)}, f32[136,128]{1,0:T(8,128)S(1)}, u32[]{:S(2)}, u32[]{:S(2)}) %collective-permute-start.7) | collective-permute-done | bytes 69664 | tf_op jit(solution)/shard_map/ppermute | solution.py:464
  35.1 0.1 collective-permute-start.10
  35.2 0.3 shard_map.91
  35.4 2.0 %collective-permute-start.9 = (f32[144,128]{1,0:T(8,128)S(1)}, f32[144,128]{1,0:T(8,128)S(1)}, u32[]{:S(2)}, u32[]{:S(2)}) collective-permute-start(f32[144,128]{1,0:T(8,128)S(1)} %pad_maximum_fusion.1), channel_id=1, source_target_pairs={{0,2},{1,3},{2,0},{3,1},{4,6},{5,7},{6,4},{7,5},{8,10},{9,11},{10,... | collective-permute-start | bytes 221192 | tf_op jit(solution)/shard_map/ppermute | solution.py:464
  37.4 1.5 %collective-permute-start.8 = (f32[144,128]{1,0:T(8,128)S(1)}, f32[144,128]{1,0:T(8,128)S(1)}, u32[]{:S(2)}, u32[]{:S(2)}) collective-permute-start(f32[144,128]{1,0:T(8,128)S(1)} %pad_maximum_fusion.1), channel_id=1, source_target_pairs={{0,1},{1,0},{2,3},{3,2},{4,5},{5,4},{6,7},{7,6},{8,9},{9,8},{10,11... | collective-permute-start | bytes 221192 | tf_op jit(solution)/shard_map/ppermute | solution.py:464
  38.9 1.4 %collective-permute-done.10 = f32[144,128]{1,0:T(8,128)S(1)} collective-permute-done((f32[144,128]{1,0:T(8,128)S(1)}, f32[144,128]{1,0:T(8,128)S(1)}, u32[]{:S(2)}, u32[]{:S(2)}) %collective-permute-start.10) | collective-permute-done | bytes 73760 | tf_op jit(solution)/shard_map/ppermute | solution.py:464
  40.4 0.0 collective-permute-done.9
  40.4 1.4 %collective-permute-done.8 = f32[144,128]{1,0:T(8,128)S(1)} collective-permute-done((f32[144,128]{1,0:T(8,128)S(1)}, f32[144,128]{1,0:T(8,128)S(1)}, u32[]{:S(2)}, u32[]{:S(2)}) %collective-permute-start.8) | collective-permute-done | bytes 73760 | tf_op jit(solution)/shard_map/ppermute | solution.py:464
  41.8 2.0 %shard_map.90.mean_ref.refs_1_ = f32[4,128,128]{2,1,0:T(8,128)S(1)} custom-call(f32[4,128,128]{2,1,0:T(8,128)S(1)} %pad_maximum_fusion.refs_0_, f32[9,4,128,128]{3,2,1,0:T(8,128)S(1)} %shard_map.87.weight_ref.refs_1_), custom_call_target="tpu_custom_call" | custom-call | flops 8192000 | bytes 1048576 | tf_op jit(solution)/shard_map/pallas_call | solution.py:470
  43.8 0.1 collective-permute-start.11
  43.9 1.4 %shard_map.92.refs_7_ = f32[4,128,512]{2,1,0:T(8,128)} custom-call(s32[4]{0:T(128)S(1)} %copy-done, f32[4,128,128]{2,1,0:T(8,128)S(1)} %shard_map.90.mean_ref.refs_1_, f32[4,128,512]{2,1,0:T(8,128)S(1)} %get-tuple-element.23.stepped_ref.refs_6_), custom_call_target="tpu_custom_call" | custom-call | flops 4096000 | bytes 1048576 | tf_op jit(solution)/shard_map/pallas_call | solution.py:470
  45.4 0.0 collective-permute-done.11.refs_2_
  45.4 2.1 %shard_map.93 = (f32[4,128,512]{2,1,0:T(8,128)}, f32[2,2,256]{2,1,0:T(2,128)}, f32[2,256]{1,0:T(2,128)}) custom-call(s32[4]{0:T(128)S(1)} %copy-done, f32[4,128,128]{2,1,0:T(8,128)S(1)} %shard_map.90.mean_ref.refs_1_, f32[4,128,128]{2,1,0:T(8,128)S(1)} %collective-permute-done.11.refs_2_, ...), custom_call_target="tpu_custom_call", output_to_operand_aliasing={{0}: (7, {})} | custom-call | flops 4096000 | bytes 1048576 | tf_op jit(solution)/shard_map/pallas_call | solution.py:470
  (16 shorter events, 0.1 us)
Async XLA Ops:
  0.6 1.5 %copy-start = (s32[4]{0:T(128)S(1)}, s32[4]{0:T(128)}, u32[]{:S(2)}) copy-start(s32[4]{0:T(128)} %refs_0_.1) | copy-start | bytes 52
  2.8 4.0 %collective-permute-start.5 = (f32[6,4,128,128]{3,2,1,0:T(8,128)S(1)}, f32[6,4,128,128]{3,2,1,0:T(8,128)S(1)}, u32[]{:S(2)}, u32[]{:S(2)}) collective-permute-start(f32[6,4,128,128]{3,2,1,0:T(8,128)S(1)} %shard_map.86), channel_id=1, source_target_pairs={{0,16},{1,17},{2,18},{3,19},{4,20},{5,21},{6,22},{7,23},{8,24},{9,... | collective-permute-start | bytes 4718600 | tf_op jit(solution)/shard_map/ppermute | solution.py:464
  3.4 3.4 %collective-permute-start = (f32[4,128,128]{2,1,0:T(8,128)S(1)}, f32[4,128,128]{2,1,0:T(8,128)S(1)}, u32[]{:S(2)}, u32[]{:S(2)}) collective-permute-start(f32[4,128,128]{2,1,0:T(8,128)S(1)} %get-tuple-element.16), channel_id=1, source_target_pairs={{0,16},{1,17},{2,18},{3,19},{4,20},{5,21},{6,22},{7,23},{8,24},{9,... | collective-permute-start | bytes 786440 | tf_op jit(solution)/shard_map/ppermute | solution.py:464
  9.1 18.0 %copy-start.1 = (f32[2,256]{1,0:T(2,128)S(1)}, f32[2,256]{1,0:T(2,128)}, u32[]{:S(2)}) copy-start(f32[2,256]{1,0:T(2,128)} %frac_ref.3) | copy-start | bytes 6148
  9.1 18.0 %copy-start.2 = (s32[256]{0:T(256)S(1)}, s32[256]{0:T(256)}, u32[]{:S(2)}) copy-start(s32[256]{0:T(256)} %param.10) | copy-start | bytes 3076
  12.8 14.3 %collective-permute-start.6 = (f32[2,4,128,128]{3,2,1,0:T(8,128)S(1)}, f32[2,4,128,128]{3,2,1,0:T(8,128)S(1)}, u32[]{:S(2)}, u32[]{:S(2)}) collective-permute-start(f32[2,4,128,128]{3,2,1,0:T(8,128)S(1)} %shard_map.88.own_ref), channel_id=1, source_target_pairs={{0,16},{1,17},{2,18},{3,19},{4,20},{5,21},{6,22},{7,23},{8,24},{9,... | collective-permute-start | bytes 1572872 | tf_op jit(solution)/shard_map/ppermute | solution.py:464
  13.3 5.0 %collective-permute-start.1 = (f32[128,128]{1,0:T(8,128)S(1)}, f32[128,128]{1,0:T(8,128)S(1)}, u32[]{:S(2)}, u32[]{:S(2)}) collective-permute-start(f32[128,128]{1,0:T(8,128)S(1)} %get-tuple-element.32), channel_id=1, source_target_pairs={{0,1},{1,0},{2,3},{3,2},{4,5},{5,4},{6,7},{7,6},{8,9},{9,8},{10,11... | collective-permute-start | bytes 196616 | tf_op jit(solution)/shard_map/ppermute | solution.py:464
  16.0 4.6 %collective-permute-start.2 = (f32[128,128]{1,0:T(8,128)S(1)}, f32[128,128]{1,0:T(8,128)S(1)}, u32[]{:S(2)}, u32[]{:S(2)}) collective-permute-start(f32[128,128]{1,0:T(8,128)S(1)} %get-tuple-element.31), channel_id=1, source_target_pairs={{0,2},{1,3},{2,0},{3,1},{4,6},{5,7},{6,4},{7,5},{8,10},{9,11},{10,... | collective-permute-start | bytes 196616 | tf_op jit(solution)/shard_map/ppermute | solution.py:464
  17.6 5.2 %collective-permute-start.3 = (f32[128,128]{1,0:T(8,128)S(1)}, f32[128,128]{1,0:T(8,128)S(1)}, u32[]{:S(2)}, u32[]{:S(2)}) collective-permute-start(f32[128,128]{1,0:T(8,128)S(1)} %get-tuple-element.30), channel_id=1, source_target_pairs={{0,3},{1,2},{2,1},{3,0},{4,7},{5,6},{6,5},{7,4},{8,11},{9,10},{10,... | collective-permute-start | bytes 196616 | tf_op jit(solution)/shard_map/ppermute | solution.py:464
  22.7 4.3 %collective-permute-start.4 = (f32[128,128]{1,0:T(8,128)S(1)}, f32[128,128]{1,0:T(8,128)S(1)}, u32[]{:S(2)}, u32[]{:S(2)}) collective-permute-start(f32[128,128]{1,0:T(8,128)S(1)} %fusion.1), channel_id=1, source_target_pairs={{0,8},{1,9},{2,10},{3,11},{4,12},{5,13},{6,14},{7,15},{8,0},{9,1},... | collective-permute-start | bytes 196616 | tf_op jit(solution)/shard_map/ppermute | solution.py:464
  29.0 6.0 %collective-permute-start.7 = (f32[136,128]{1,0:T(8,128)S(1)}, f32[136,128]{1,0:T(8,128)S(1)}, u32[]{:S(2)}, u32[]{:S(2)}) collective-permute-start(f32[136,128]{1,0:T(8,128)S(1)} %pad_maximum_fusion.2), channel_id=1, source_target_pairs={{0,4},{1,5},{2,6},{3,7},{4,0},{5,1},{6,2},{7,3},{8,12},{9,13},{10,... | collective-permute-start | bytes 208904 | tf_op jit(solution)/shard_map/ppermute | solution.py:464
  35.1 5.3 %collective-permute-start.10 = (f32[144,128]{1,0:T(8,128)S(1)}, f32[144,128]{1,0:T(8,128)S(1)}, u32[]{:S(2)}, u32[]{:S(2)}) collective-permute-start(f32[144,128]{1,0:T(8,128)S(1)} %pad_maximum_fusion.1), channel_id=1, source_target_pairs={{0,3},{1,2},{2,1},{3,0},{4,7},{5,6},{6,5},{7,4},{8,11},{9,10},{10,... | collective-permute-start | bytes 221192 | tf_op jit(solution)/shard_map/ppermute | solution.py:464
  35.4 4.9 %collective-permute-start.9 = (f32[144,128]{1,0:T(8,128)S(1)}, f32[144,128]{1,0:T(8,128)S(1)}, u32[]{:S(2)}, u32[]{:S(2)}) collective-permute-start(f32[144,128]{1,0:T(8,128)S(1)} %pad_maximum_fusion.1), channel_id=1, source_target_pairs={{0,2},{1,3},{2,0},{3,1},{4,6},{5,7},{6,4},{7,5},{8,10},{9,11},{10,... | collective-permute-start | bytes 221192 | tf_op jit(solution)/shard_map/ppermute | solution.py:464
  37.4 4.4 %collective-permute-start.8 = (f32[144,128]{1,0:T(8,128)S(1)}, f32[144,128]{1,0:T(8,128)S(1)}, u32[]{:S(2)}, u32[]{:S(2)}) collective-permute-start(f32[144,128]{1,0:T(8,128)S(1)} %pad_maximum_fusion.1), channel_id=1, source_target_pairs={{0,1},{1,0},{2,3},{3,2},{4,5},{5,4},{6,7},{7,6},{8,9},{9,8},{10,11... | collective-permute-start | bytes 221192 | tf_op jit(solution)/shard_map/ppermute | solution.py:464
  43.8 1.6 %collective-permute-start.11 = (f32[4,128,128]{2,1,0:T(8,128)S(1)}, f32[4,128,128]{2,1,0:T(8,128)S(1)}, u32[]{:S(2)}, u32[]{:S(2)}) collective-permute-start(f32[4,128,128]{2,1,0:T(8,128)S(1)} %shard_map.90.mean_ref.refs_1_), channel_id=1, source_target_pairs={{0,16},{1,17},{2,18},{3,19},{4,20},{5,21},{6,22},{7,23},{8,24},{9,... | collective-permute-start | bytes 786440 | tf_op jit(solution)/shard_map/ppermute | solution.py:464

commit v4 on v3

--- a/solution.py
+++ b/solution.py
@@ -54,17 +54,17 @@
 
 
 def sums_kernel(
-    sizes, rank_hbm, temp_hbm, kappa_hbm, land_hbm, send_ref, keep_ref, temp_ref, kappa_ref, land_ref, rank_ref, sem
+    sizes, rank_hbm, temp_hbm, land_hbm, send_ref, keep_ref, temp_ref, land_ref, rank_out, rank_ref, sem
 ):
     members, fields, rows, tiles, _ = sizes
     core, mine, other = chunk_number()
-    pairs = ((rank_hbm, rank_ref), (land_hbm, land_ref), (temp_hbm, temp_ref), (kappa_hbm, kappa_ref))
+    pairs = ((rank_hbm, rank_ref), (land_hbm, land_ref), (temp_hbm, temp_ref), (rank_hbm, rank_out))
     copies = [pltpu.make_async_copy(*pair, sem.at[number]) for number, pair in enumerate(pairs)]
     for copy in copies:
         copy.start()
     send_ref[...] = jnp.zeros_like(send_ref)
     keep_ref[...] = jnp.zeros_like(keep_ref)
-    for copy in copies[:3]:
+    for copy in copies:
         copy.wait()
     for tile in range(tiles):
         lanes = slice(tile * LANES, (tile + 1) * LANES)
@@ -78,8 +78,6 @@
                 for member in range(1, members):
                     total = total + temp_ref[member * fields + field, :, lanes] * wet
                 ref[jnp.bitwise_xor(slot, rank)] = total
-
-    copies[3].wait()
 
 
 def pack_kernel(sizes, rank_ref, temp_ref, kappa_ref, land_ref, pack_ref):
@@ -347,10 +345,24 @@
     return jnp.concatenate([high, middle, low, high, middle, high], axis=1)
 
 
-def own_field_kernel(sizes, rank_ref, mean_ref, stepped_ref, field_hbm, field_ref, sem):
+def observe_mean(sizes, rank_ref, mean_ref, column_ref, row_ref, whole_ref):
+    _, _, _, tiles, _ = sizes
+    for tile in range(tiles):
+        lanes = slice(tile * LANES, (tile + 1) * LANES)
+        rank = rank_ref[tile]
+        wet = jnp.where(rank >= 0, 1.0, 0.0)
+        whole_ref[:, lanes] = mean_ref[jnp.maximum(rank, 0)] * wet
+    picked = jnp.dot(split_values(whole_ref[...]), column_ref[...], preferred_element_type=jnp.float32)
+    return jnp.sum(picked * row_ref[...], axis=0, keepdims=True)
+
+
+def own_field_kernel(
+    sizes, rank_ref, mean_ref, stepped_ref, column_ref, row_ref, field_hbm, mean_seen_ref, field_ref, whole_ref, sem
+):
     members, _, _, _, _ = sizes
     core, _, _ = chunk_number()
     write_planes(sizes, core, rank_ref, mean_ref, stepped_ref, field_hbm, field_ref, sem)
+    mean_seen_ref[...] = observe_mean(sizes, rank_ref, mean_ref, column_ref, row_ref, whole_ref)
     for member in range(members):
         plane_copy(sizes, member, core, field_hbm, field_ref, sem).wait()
 
@@ -379,28 +391,14 @@
 
 
 def final_kernel(
-    sizes, ensemble, rank_ref, own_ref, other_ref, column_ref, row_ref, seen_ref, stepped_ref, started_hbm,
-    field_hbm, anomaly_hbm, variance_hbm, field_ref, mean_ref, anomaly_ref, variance_ref, sem,
+    sizes, ensemble, rank_ref, other_ref, column_ref, row_ref, own_seen_ref, seen_ref, stepped_ref, started_hbm,
+    field_hbm, anomaly_hbm, variance_hbm, field_ref, whole_ref, anomaly_ref, variance_ref, sem,
 ):
-    members, fields, rows, tiles, _ = sizes
+    members, fields, _, _, _ = sizes
     core, _, _ = chunk_number()
     write_planes(sizes, 1 - core, rank_ref, other_ref, stepped_ref, field_hbm, field_ref, sem)
-    for tile in range(tiles):
-        lanes = slice(tile * LANES, (tile + 1) * LANES)
-        rank = rank_ref[tile]
-
-        @pl.when(rank >= 0)
-        def _():
-            mean_ref[core, :, lanes] = own_ref[rank]
-            mean_ref[1 - core, :, lanes] = other_ref[rank]
-
-        @pl.when(rank < 0)
-        def _():
-            for field in range(fields):
-                mean_ref[field, :, lanes] = jnp.zeros((rows, LANES), jnp.float32)
-
-    values = jnp.concatenate([split_values(mean_ref[field]) for field in range(fields)], axis=0)
-    picked = jnp.dot(values, column_ref[...], preferred_element_type=jnp.float32)
+    own_seen = own_seen_ref[...]
+    other_seen = observe_mean(sizes, rank_ref, other_ref, column_ref, row_ref, whole_ref)
     halves = row_ref.shape[1] // LANES
     stride = members * fields * halves
     sets = seen_ref.shape[0] // stride
@@ -411,7 +409,7 @@
         return values[0]
 
     for field in range(fields):
-        mean_seen = jnp.sum(picked[field * rows : (field + 1) * rows] * row_ref[...], axis=0, keepdims=True)
+        mean_seen = jnp.where(core == field, own_seen, other_seen)
         for half in range(halves):
             lanes = slice(half * LANES, (half + 1) * LANES)
             mean = mean_seen[:, lanes]
@@ -470,7 +468,7 @@
         return pl.pallas_call(
             functools.partial(kernel, sizes),
             out_shape=out_shape,
-            in_specs=in_specs or [SMEM if x is wet_rank else VMEM for x in operands],
+            in_specs=in_specs or [SMEM if x.shape == wet_rank.shape else VMEM for x in operands],
             out_specs=out_specs or jax.tree.map(lambda _: VMEM, out_shape),
             scratch_shapes=list(scratch),
             input_output_aliases=aliases,
@@ -486,39 +484,39 @@
     cell = obs_cell.reshape(1, count)
     masks = {1: (1, 2), 2: (2, 1), 3: (3, 3)}
 
-    inputs = tuple(pltpu.with_memory_space_constraint(x, pltpu.HBM) for x in (wet_rank, temp, diffusivity, land))
-    send, keep, temp, kappa, land = call(
+    inputs = tuple(pltpu.with_memory_space_constraint(x, pltpu.HBM) for x in (wet_rank, temp, land))
+    send, keep, temp, land, rank = call(
         sums_kernel,
         (
             struct(slots, rows, LANES),
             struct(slots, rows, LANES),
             struct(planes, rows, columns),
-            struct(*diffusivity.shape),
             jax.ShapeDtypeStruct((tiles, LANES), jnp.int32),
+            jax.ShapeDtypeStruct((tiles,), jnp.int32),
         ),
         inputs,
         scratch=[pltpu.SMEM((tiles,), jnp.int32), pltpu.SemaphoreType.DMA((4,))],
-        in_specs=[HBM] * 4,
+        in_specs=[HBM] * 3,
     )
     arrived = exchange(send, None)
-    pack = call(pack_kernel, struct(fields + 4, slots, rows, LANES), (wet_rank, temp, kappa, land))
+    pack = call(pack_kernel, struct(fields + 4, slots, rows, LANES), (rank, temp, diffusivity, land))
     packed = exchange(pack, None)
     total = keep + arrived
     got = [exchange(total[k], masks[k]) for k in (1, 2, 3)]
     total = (total[0] + got[0]) + (got[1] + got[2])
 
     weights = call(
-        weights_kernel, struct(9, slots, rows, LANES), (wet_rank, kappa, land, packed),
+        weights_kernel, struct(9, slots, rows, LANES), (rank, diffusivity, land, packed),
         [pltpu.VMEM((4, slots, rows + 2 * PAD, LANES), jnp.float32)] * 2,
     )
     own = call(
-        member_kernel, struct(fields, slots, rows, LANES), (wet_rank, temp, land, packed, weights),
+        member_kernel, struct(fields, slots, rows, LANES), (rank, temp, land, packed, weights),
         [halo(fields)], cycles=4000,
     )
     other = exchange(own, None)
     stepped, seen = call(
         observe_kernel, (struct(planes, rows, columns), struct(planes * count // LANES, LANES)),
-        (wet_rank, own, other, cell, obs_frac), cycles=2000,
+        (rank, own, other, cell, obs_frac), cycles=2000,
     )
 
     for bit in [level_bit] + list(range(2, level_bit)):
@@ -544,22 +542,24 @@
         (jax.ShapeDtypeStruct((6 * columns, count), jnp.bfloat16), struct(rows, count)), (cell, obs_frac),
     )
     plane_scratch = pltpu.VMEM((members, rows, columns), jnp.float32)
-    started = call(
-        own_field_kernel, struct(planes, rows, columns), (wet_rank, own_mean, stepped),
-        [plane_scratch, pltpu.SemaphoreType.DMA((members,))], out_specs=HBM,
+    whole_scratch = pltpu.VMEM((rows, columns), jnp.float32)
+    started, own_seen = call(
+        own_field_kernel, (struct(planes, rows, columns), struct(1, count)),
+        (rank, own_mean, stepped, column_picks, row_picks),
+        [plane_scratch, whole_scratch, pltpu.SemaphoreType.DMA((members,))], out_specs=(HBM, VMEM),
     )
 
     def last_kernel(sizes, *refs):
         final_kernel(sizes, members * member_count, *refs)
 
-    operands = (wet_rank, own_mean, other_mean, column_picks, row_picks, seen, stepped, started)
+    operands = (rank, other_mean, column_picks, row_picks, own_seen, seen, stepped, started)
     field, anomaly, variance = call(
         last_kernel,
         (struct(planes, rows, columns), struct(members, fields, count), struct(fields, count)),
         operands,
         [
             plane_scratch,
-            pltpu.VMEM((fields, rows, columns), jnp.float32),
+            whole_scratch,
             pltpu.VMEM((members, fields, count), jnp.float32),
             pltpu.VMEM((fields, count), jnp.float32),
             pltpu.SemaphoreType.DMA((members + 2,)),

time: 47.6 us -> 47 us (0.987)
  waiting for transfers between devices: 17.5 us -> 17 us
    ppermute x12, waiting for transfers between devices: 17.5 us -> 17 us  [exchange(): return lax.ppermute(value, ALL_AXES, pairs)]
where the time goes in v4:
time: 47 us; the launch traced here: 46.9 us
  waiting for transfers between devices  17 us (36%)
  Pallas kernels  15.7 us (33%)
  starting transfers between devices  13.2 us (28%)
  between operations  0.85 us (2%)
    ppermute x12, waiting for transfers between devices, exchange(): return lax.ppermute(value, ALL_AXES, pairs)  17 us
    pallas_call x9, Pallas kernels, call(): pl.pallas_call(functools.partial(kernel, sizes), out_shape=out_shape, in_...  15.7 us
    ppermute x12, starting transfers between devices, exchange(): return lax.ppermute(value, ALL_AXES, pairs)  13.2 us
  transfers between devices with their start and end apart: 12, of which 8 were waited for; matrix products, arithmetic and copies ran while one was open for 0% of the time, Pallas kernels for 4%

profile of v4, /device:TPU:0, one launch (start us, length us, event | category | flops | bytes accessed | tf_op | source)
XLA Modules:
  0.0 46.9 jit_solution(5834849878930948186)
XLA Ops:
  0.6 0.0 copy-start
  0.6 1.4 %shard_map.85 = (f32[4,128,128]{2,1,0:T(8,128)S(1)}, f32[4,128,128]{2,1,0:T(8,128)S(1)}, f32[4,128,512]{2,1,0:T(8,128)S(1)}, s32[4,128]{1,0:T(4,128)S(1)}, s32[4]{0:T(128)S(1)}) custom-call(s32[4]{0:T(128)} %rank_hbm.1, f32[4,128,512]{2,1,0:T(8,128)} %bitcast.28, s32[4,128]{1,0:T(4,128)} %bitcast.30), custom_call_target="tpu_custom_call" | custom-call | flops 4096000 | bytes 1048576 | tf_op jit(solution)/shard_map/pallas_call | solution.py:468
  2.1 0.0 copy-done
  2.1 0.7 %shard_map.86 = f32[6,4,128,128]{3,2,1,0:T(8,128)S(1)} custom-call(s32[4]{0:T(128)S(1)} %get-tuple-element.17.rank_ref.refs_0_, f32[4,128,512]{2,1,0:T(8,128)S(1)} %get-tuple-element.20.temp_ref, f32[3,128,512]{2,1,0:T(8,128)S(1)} %copy-done, s32[4,128]{1,0:T(4,128)S(1)} %get-tuple-element.21.land_ref), custom_call_target="tpu_custom_call" | custom-call | flops 4096000 | bytes 1048576 | tf_op jit(solution)/shard_map/pallas_call | solution.py:468
  2.8 0.6 %collective-permute-start.5 = (f32[6,4,128,128]{3,2,1,0:T(8,128)S(1)}, f32[6,4,128,128]{3,2,1,0:T(8,128)S(1)}, u32[]{:S(2)}, u32[]{:S(2)}) collective-permute-start(f32[6,4,128,128]{3,2,1,0:T(8,128)S(1)} %shard_map.86), channel_id=1, source_target_pairs={{0,16},{1,17},{2,18},{3,19},{4,20},{5,21},{6,22},{7,23},{8,24},{9,... | collective-permute-start | bytes 4718600 | tf_op jit(solution)/shard_map/ppermute | solution.py:462
  3.3 0.1 collective-permute-start
  3.4 3.3 %collective-permute-done = f32[4,128,128]{2,1,0:T(8,128)S(1)} collective-permute-done((f32[4,128,128]{2,1,0:T(8,128)S(1)}, f32[4,128,128]{2,1,0:T(8,128)S(1)}, u32[]{:S(2)}, u32[]{:S(2)}) %collective-permute-start) | collective-permute-done | bytes 262176 | tf_op jit(solution)/shard_map/ppermute | solution.py:462
  6.8 0.0 collective-permute-done.5.pack_ref
  6.8 2.2 %shard_map.87.weight_ref.refs_1_ = f32[9,4,128,128]{3,2,1,0:T(8,128)S(1)} custom-call(s32[4]{0:T(128)S(1)} %get-tuple-element.17.rank_ref.refs_0_, f32[3,128,512]{2,1,0:T(8,128)S(1)} %copy-done, s32[4,128]{1,0:T(4,128)S(1)} %get-tuple-element.21.land_ref, f32[6,4,128,128]{3,2,1,0:T(8,128)S(1)} %collective-permute-done.5.pack_ref), custom_call_target="tpu_custom_call" | custom-call | flops 4096000 | bytes 1048576 | tf_op jit(solution)/shard_map/pallas_call | solution.py:468
  9.0 0.0 copy-start.1
  9.0 0.0 copy-start.2
  9.0 3.7 %shard_map.88.own_ref = f32[2,4,128,128]{3,2,1,0:T(8,128)S(1)} custom-call(s32[4]{0:T(128)S(1)} %get-tuple-element.17.rank_ref.refs_0_, f32[4,128,512]{2,1,0:T(8,128)S(1)} %get-tuple-element.20.temp_ref, s32[4,128]{1,0:T(4,128)S(1)} %get-tuple-element.21.land_ref, f32[6,4,128,128]{3,2,1,0:T(8,128)S(1)} %collective-permute-done.5.pack_ref, ...), custom_call_target="tpu_custom_call" | custom-call | flops 16384000 | bytes 1048576 | tf_op jit(solution)/shard_map/pallas_call | solution.py:468
  12.8 0.4 collective-permute-start.6
  13.2 2.7 %collective-permute-start.1 = (f32[128,128]{1,0:T(8,128)S(1)}, f32[128,128]{1,0:T(8,128)S(1)}, u32[]{:S(2)}, u32[]{:S(2)}) collective-permute-start(f32[128,128]{1,0:T(8,128)S(1)} %get-tuple-element.36), channel_id=1, source_target_pairs={{0,1},{1,0},{2,3},{3,2},{4,5},{5,4},{6,7},{7,6},{8,9},{9,8},{10,11... | collective-permute-start | bytes 196616 | tf_op jit(solution)/shard_map/ppermute | solution.py:462
  15.9 1.6 %collective-permute-start.2 = (f32[128,128]{1,0:T(8,128)S(1)}, f32[128,128]{1,0:T(8,128)S(1)}, u32[]{:S(2)}, u32[]{:S(2)}) collective-permute-start(f32[128,128]{1,0:T(8,128)S(1)} %get-tuple-element.35), channel_id=1, source_target_pairs={{0,2},{1,3},{2,0},{3,1},{4,6},{5,7},{6,4},{7,5},{8,10},{9,11},{10,... | collective-permute-start | bytes 196616 | tf_op jit(solution)/shard_map/ppermute | solution.py:462
  17.5 0.0 collective-permute-start.3
  17.5 0.7 %collective-permute-done.1 = f32[128,128]{1,0:T(8,128)S(1)} collective-permute-done((f32[128,128]{1,0:T(8,128)S(1)}, f32[128,128]{1,0:T(8,128)S(1)}, u32[]{:S(2)}, u32[]{:S(2)}) %collective-permute-start.1) | collective-permute-done | bytes 65568 | tf_op jit(solution)/shard_map/ppermute | solution.py:462
  18.2 2.3 %collective-permute-done.2 = f32[128,128]{1,0:T(8,128)S(1)} collective-permute-done((f32[128,128]{1,0:T(8,128)S(1)}, f32[128,128]{1,0:T(8,128)S(1)}, u32[]{:S(2)}, u32[]{:S(2)}) %collective-permute-start.2) | collective-permute-done | bytes 65568 | tf_op jit(solution)/shard_map/ppermute | solution.py:462
  20.5 2.2 %collective-permute-done.3 = f32[128,128]{1,0:T(8,128)S(1)} collective-permute-done((f32[128,128]{1,0:T(8,128)S(1)}, f32[128,128]{1,0:T(8,128)S(1)}, u32[]{:S(2)}, u32[]{:S(2)}) %collective-permute-start.3) | collective-permute-done | bytes 65568 | tf_op jit(solution)/shard_map/ppermute | solution.py:462
  22.7 1.6 %collective-permute-start.4 = (f32[128,128]{1,0:T(8,128)S(1)}, f32[128,128]{1,0:T(8,128)S(1)}, u32[]{:S(2)}, u32[]{:S(2)}) collective-permute-start(f32[128,128]{1,0:T(8,128)S(1)} %fusion.1), channel_id=1, source_target_pairs={{0,8},{1,9},{2,10},{3,11},{4,12},{5,13},{6,14},{7,15},{8,0},{9,1},... | collective-permute-start | bytes 196616 | tf_op jit(solution)/shard_map/ppermute | solution.py:462
  24.3 2.8 %collective-permute-done.4 = f32[128,128]{1,0:T(8,128)S(1)} collective-permute-done((f32[128,128]{1,0:T(8,128)S(1)}, f32[128,128]{1,0:T(8,128)S(1)}, u32[]{:S(2)}, u32[]{:S(2)}) %collective-permute-start.4) | collective-permute-done | bytes 65568 | tf_op jit(solution)/shard_map/ppermute | solution.py:462
  27.0 0.0 collective-permute-done.6.other_ref
  27.1 0.0 copy-done.1
  27.1 0.0 copy-done.2
  27.1 1.9 %shard_map.89 = (f32[4,128,512]{2,1,0:T(8,128)S(1)}, f32[8,128]{1,0:T(8,128)S(1)}) custom-call(s32[4]{0:T(128)S(1)} %get-tuple-element.17.rank_ref.refs_0_, f32[2,4,128,128]{3,2,1,0:T(8,128)S(1)} %shard_map.88.own_ref, f32[2,4,128,128]{3,2,1,0:T(8,128)S(1)} %collective-permute-done.6.other_ref, s32[1,256]{1,0:T(1,128)S(1)} %bitcast.25, f32[2,256]{1,0:T(2,128)S(1)} %copy-done.1), custom_call_target="tpu_custom_call" | custom-call | flops 8192000 | bytes 1048576 | tf_op jit(solution)/shard_map/pallas_call | solution.py:468
  29.0 2.7 %collective-permute-start.7 = (f32[136,128]{1,0:T(8,128)S(1)}, f32[136,128]{1,0:T(8,128)S(1)}, u32[]{:S(2)}, u32[]{:S(2)}) collective-permute-start(f32[136,128]{1,0:T(8,128)S(1)} %pad_maximum_fusion.2), channel_id=1, source_target_pairs={{0,4},{1,5},{2,6},{3,7},{4,0},{5,1},{6,2},{7,3},{8,12},{9,13},{10,... | collective-permute-start | bytes 208904 | tf_op jit(solution)/shard_map/ppermute | solution.py:462
  31.6 3.4 %collective-permute-done.7 = f32[136,128]{1,0:T(8,128)S(1)} collective-permute-done((f32[136,128]{1,0:T(8,128)S(1)}, f32[136,128]{1,0:T(8,128)S(1)}, u32[]{:S(2)}, u32[]{:S(2)}) %collective-permute-start.7) | collective-permute-done | bytes 69664 | tf_op jit(solution)/shard_map/ppermute | solution.py:462
  35.0 0.1 collective-permute-start.10
  35.1 0.3 shard_map.91
  35.4 1.2 %collective-permute-start.8 = (f32[144,128]{1,0:T(8,128)S(1)}, f32[144,128]{1,0:T(8,128)S(1)}, u32[]{:S(2)}, u32[]{:S(2)}) collective-permute-start(f32[144,128]{1,0:T(8,128)S(1)} %pad_maximum_fusion.1), channel_id=1, source_target_pairs={{0,1},{1,0},{2,3},{3,2},{4,5},{5,4},{6,7},{7,6},{8,9},{9,8},{10,11... | collective-permute-start | bytes 221192 | tf_op jit(solution)/shard_map/ppermute | solution.py:462
  36.6 2.2 %collective-permute-start.9 = (f32[144,128]{1,0:T(8,128)S(1)}, f32[144,128]{1,0:T(8,128)S(1)}, u32[]{:S(2)}, u32[]{:S(2)}) collective-permute-start(f32[144,128]{1,0:T(8,128)S(1)} %pad_maximum_fusion.1), channel_id=1, source_target_pairs={{0,2},{1,3},{2,0},{3,1},{4,6},{5,7},{6,4},{7,5},{8,10},{9,11},{10,... | collective-permute-start | bytes 221192 | tf_op jit(solution)/shard_map/ppermute | solution.py:462
  38.9 1.5 %collective-permute-done.10 = f32[144,128]{1,0:T(8,128)S(1)} collective-permute-done((f32[144,128]{1,0:T(8,128)S(1)}, f32[144,128]{1,0:T(8,128)S(1)}, u32[]{:S(2)}, u32[]{:S(2)}) %collective-permute-start.10) | collective-permute-done | bytes 73760 | tf_op jit(solution)/shard_map/ppermute | solution.py:462
  40.4 0.8 %collective-permute-done.9 = f32[144,128]{1,0:T(8,128)S(1)} collective-permute-done((f32[144,128]{1,0:T(8,128)S(1)}, f32[144,128]{1,0:T(8,128)S(1)}, u32[]{:S(2)}, u32[]{:S(2)}) %collective-permute-start.9) | collective-permute-done | bytes 73760 | tf_op jit(solution)/shard_map/ppermute | solution.py:462
  41.2 0.0 collective-permute-done.8
  41.3 2.0 %shard_map.90.mean_ref = f32[4,128,128]{2,1,0:T(8,128)S(1)} custom-call(f32[4,128,128]{2,1,0:T(8,128)S(1)} %pad_maximum_fusion.refs_0_, f32[9,4,128,128]{3,2,1,0:T(8,128)S(1)} %shard_map.87.weight_ref.refs_1_), custom_call_target="tpu_custom_call" | custom-call | flops 8192000 | bytes 1048576 | tf_op jit(solution)/shard_map/pallas_call | solution.py:468
  43.3 0.1 collective-permute-start.11
  43.4 1.7 %shard_map.92 = (f32[4,128,512]{2,1,0:T(8,128)}, f32[1,256]{1,0:T(1,128)S(1)}) custom-call(s32[4]{0:T(128)S(1)} %get-tuple-element.17.rank_ref.refs_0_, f32[4,128,128]{2,1,0:T(8,128)S(1)} %shard_map.90.mean_ref, f32[4,128,512]{2,1,0:T(8,128)S(1)} %get-tuple-element.25.stepped_ref.refs_6_, bf16[3072,256]{1,0:T(8,128)(2,1)S(1)} %get-tuple-element.23.column_ref.refs_2_, ...), custom_call_target="tpu_custom_call" | custom-call | flops 4096000 | bytes 1048576 | tf_op jit(solution)/shard_map/pallas_call | solution.py:468
  45.1 0.0 collective-permute-done.11.refs_1_
  45.1 1.8 %shard_map.93 = (f32[4,128,512]{2,1,0:T(8,128)}, f32[2,2,256]{2,1,0:T(2,128)}, f32[2,256]{1,0:T(2,128)}) custom-call(s32[4]{0:T(128)S(1)} %get-tuple-element.17.rank_ref.refs_0_, f32[4,128,128]{2,1,0:T(8,128)S(1)} %collective-permute-done.11.refs_1_, bf16[3072,256]{1,0:T(8,128)(2,1)S(1)} %get-tuple-element.23.column_ref.refs_2_, ...), custom_call_target="tpu_custom_call", output_to_operand_aliasing={{0}: (7, {})} | custom-call | flops 4096000 | bytes 1048576 | tf_op jit(solution)/shard_map/pallas_call | solution.py:468
  (16 shorter events, 0.2 us)
Async XLA Ops:
  0.6 1.5 %copy-start = (f32[3,128,512]{2,1,0:T(8,128)S(1)}, f32[3,128,512]{2,1,0:T(8,128)}, u32[]{:S(2)}) copy-start(f32[3,128,512]{2,1,0:T(8,128)} %kappa_ref.3) | copy-start | bytes 2359300
  2.8 4.0 %collective-permute-start.5 = (f32[6,4,128,128]{3,2,1,0:T(8,128)S(1)}, f32[6,4,128,128]{3,2,1,0:T(8,128)S(1)}, u32[]{:S(2)}, u32[]{:S(2)}) collective-permute-start(f32[6,4,128,128]{3,2,1,0:T(8,128)S(1)} %shard_map.86), channel_id=1, source_target_pairs={{0,16},{1,17},{2,18},{3,19},{4,20},{5,21},{6,22},{7,23},{8,24},{9,... | collective-permute-start | bytes 4718600 | tf_op jit(solution)/shard_map/ppermute | solution.py:462
  3.3 3.4 %collective-permute-start = (f32[4,128,128]{2,1,0:T(8,128)S(1)}, f32[4,128,128]{2,1,0:T(8,128)S(1)}, u32[]{:S(2)}, u32[]{:S(2)}) collective-permute-start(f32[4,128,128]{2,1,0:T(8,128)S(1)} %get-tuple-element.19), channel_id=1, source_target_pairs={{0,16},{1,17},{2,18},{3,19},{4,20},{5,21},{6,22},{7,23},{8,24},{9,... | collective-permute-start | bytes 786440 | tf_op jit(solution)/shard_map/ppermute | solution.py:462
  9.0 18.0 %copy-start.1 = (f32[2,256]{1,0:T(2,128)S(1)}, f32[2,256]{1,0:T(2,128)}, u32[]{:S(2)}) copy-start(f32[2,256]{1,0:T(2,128)} %frac_ref.3) | copy-start | bytes 6148
  9.0 18.0 %copy-start.2 = (s32[256]{0:T(256)S(1)}, s32[256]{0:T(256)}, u32[]{:S(2)}) copy-start(s32[256]{0:T(256)} %param.10) | copy-start | bytes 3076
  12.8 14.3 %collective-permute-start.6 = (f32[2,4,128,128]{3,2,1,0:T(8,128)S(1)}, f32[2,4,128,128]{3,2,1,0:T(8,128)S(1)}, u32[]{:S(2)}, u32[]{:S(2)}) collective-permute-start(f32[2,4,128,128]{3,2,1,0:T(8,128)S(1)} %shard_map.88.own_ref), channel_id=1, source_target_pairs={{0,16},{1,17},{2,18},{3,19},{4,20},{5,21},{6,22},{7,23},{8,24},{9,... | collective-permute-start | bytes 1572872 | tf_op jit(solution)/shard_map/ppermute | solution.py:462
  13.2 5.0 %collective-permute-start.1 = (f32[128,128]{1,0:T(8,128)S(1)}, f32[128,128]{1,0:T(8,128)S(1)}, u32[]{:S(2)}, u32[]{:S(2)}) collective-permute-start(f32[128,128]{1,0:T(8,128)S(1)} %get-tuple-element.36), channel_id=1, source_target_pairs={{0,1},{1,0},{2,3},{3,2},{4,5},{5,4},{6,7},{7,6},{8,9},{9,8},{10,11... | collective-permute-start | bytes 196616 | tf_op jit(solution)/shard_map/ppermute | solution.py:462
  15.9 4.6 %collective-permute-start.2 = (f32[128,128]{1,0:T(8,128)S(1)}, f32[128,128]{1,0:T(8,128)S(1)}, u32[]{:S(2)}, u32[]{:S(2)}) collective-permute-start(f32[128,128]{1,0:T(8,128)S(1)} %get-tuple-element.35), channel_id=1, source_target_pairs={{0,2},{1,3},{2,0},{3,1},{4,6},{5,7},{6,4},{7,5},{8,10},{9,11},{10,... | collective-permute-start | bytes 196616 | tf_op jit(solution)/shard_map/ppermute | solution.py:462
  17.5 5.2 %collective-permute-start.3 = (f32[128,128]{1,0:T(8,128)S(1)}, f32[128,128]{1,0:T(8,128)S(1)}, u32[]{:S(2)}, u32[]{:S(2)}) collective-permute-start(f32[128,128]{1,0:T(8,128)S(1)} %get-tuple-element.34), channel_id=1, source_target_pairs={{0,3},{1,2},{2,1},{3,0},{4,7},{5,6},{6,5},{7,4},{8,11},{9,10},{10,... | collective-permute-start | bytes 196616 | tf_op jit(solution)/shard_map/ppermute | solution.py:462
  22.7 4.3 %collective-permute-start.4 = (f32[128,128]{1,0:T(8,128)S(1)}, f32[128,128]{1,0:T(8,128)S(1)}, u32[]{:S(2)}, u32[]{:S(2)}) collective-permute-start(f32[128,128]{1,0:T(8,128)S(1)} %fusion.1), channel_id=1, source_target_pairs={{0,8},{1,9},{2,10},{3,11},{4,12},{5,13},{6,14},{7,15},{8,0},{9,1},... | collective-permute-start | bytes 196616 | tf_op jit(solution)/shard_map/ppermute | solution.py:462
  29.0 6.0 %collective-permute-start.7 = (f32[136,128]{1,0:T(8,128)S(1)}, f32[136,128]{1,0:T(8,128)S(1)}, u32[]{:S(2)}, u32[]{:S(2)}) collective-permute-start(f32[136,128]{1,0:T(8,128)S(1)} %pad_maximum_fusion.2), channel_id=1, source_target_pairs={{0,4},{1,5},{2,6},{3,7},{4,0},{5,1},{6,2},{7,3},{8,12},{9,13},{10,... | collective-permute-start | bytes 208904 | tf_op jit(solution)/shard_map/ppermute | solution.py:462
  35.0 5.4 %collective-permute-start.10 = (f32[144,128]{1,0:T(8,128)S(1)}, f32[144,128]{1,0:T(8,128)S(1)}, u32[]{:S(2)}, u32[]{:S(2)}) collective-permute-start(f32[144,128]{1,0:T(8,128)S(1)} %pad_maximum_fusion.1), channel_id=1, source_target_pairs={{0,3},{1,2},{2,1},{3,0},{4,7},{5,6},{6,5},{7,4},{8,11},{9,10},{10,... | collective-permute-start | bytes 221192 | tf_op jit(solution)/shard_map/ppermute | solution.py:462
  35.4 5.8 %collective-permute-start.8 = (f32[144,128]{1,0:T(8,128)S(1)}, f32[144,128]{1,0:T(8,128)S(1)}, u32[]{:S(2)}, u32[]{:S(2)}) collective-permute-start(f32[144,128]{1,0:T(8,128)S(1)} %pad_maximum_fusion.1), channel_id=1, source_target_pairs={{0,1},{1,0},{2,3},{3,2},{4,5},{5,4},{6,7},{7,6},{8,9},{9,8},{10,11... | collective-permute-start | bytes 221192 | tf_op jit(solution)/shard_map/ppermute | solution.py:462
  36.6 4.6 %collective-permute-start.9 = (f32[144,128]{1,0:T(8,128)S(1)}, f32[144,128]{1,0:T(8,128)S(1)}, u32[]{:S(2)}, u32[]{:S(2)}) collective-permute-start(f32[144,128]{1,0:T(8,128)S(1)} %pad_maximum_fusion.1), channel_id=1, source_target_pairs={{0,2},{1,3},{2,0},{3,1},{4,6},{5,7},{6,4},{7,5},{8,10},{9,11},{10,... | collective-permute-start | bytes 221192 | tf_op jit(solution)/shard_map/ppermute | solution.py:462
  43.3 1.8 %collective-permute-start.11 = (f32[4,128,128]{2,1,0:T(8,128)S(1)}, f32[4,128,128]{2,1,0:T(8,128)S(1)}, u32[]{:S(2)}, u32[]{:S(2)}) collective-permute-start(f32[4,128,128]{2,1,0:T(8,128)S(1)} %shard_map.90.mean_ref), channel_id=1, source_target_pairs={{0,16},{1,17},{2,18},{3,19},{4,20},{5,21},{6,22},{7,23},{8,24},{9,... | collective-permute-start | bytes 786440 | tf_op jit(solution)/shard_map/ppermute | solution.py:462

commit v5 on v4

--- a/solution.py
+++ b/solution.py
@@ -519,14 +519,14 @@
         (rank, own, other, cell, obs_frac), cycles=2000,
     )
 
-    for bit in [level_bit] + list(range(2, level_bit)):
-        mask = (1 << bit, 1 << bit)
-        if bit == level_bit:
-            total = total + exchange(total, mask)
-        else:
-            got = exchange(jnp.concatenate([total, seen], axis=0), mask)
-            total = total + got[:rows]
-            seen = jnp.concatenate([seen, got[rows:]], axis=0)
+    level, member = 1 << level_bit, 1 << 2
+    total = total + exchange(total, (member, level))
+    total = total + exchange(total, (level, member))
+    seen = jnp.concatenate([seen, exchange(seen, (member, member))], axis=0)
+    for bit in range(3, level_bit):
+        got = exchange(jnp.concatenate([total, seen], axis=0), (1 << bit, 1 << bit))
+        total = total + got[:rows]
+        seen = jnp.concatenate([seen, got[rows:]], axis=0)
     payload = jnp.concatenate([total, seen], axis=0)
     got = [payload] + [exchange(payload, masks[k]) for k in (1, 2, 3)]
     gathered = jnp.stack([x[:rows] for x in got])

time: 47 us -> 52.9 us (1.13)
  waiting for transfers between devices: 17 us -> 21.9 us
  starting transfers between devices: 13.2 us -> 14.1 us
    ppermute x12 -> x13, waiting for transfers between devices: 17 us -> 21.9 us  [exchange(): return lax.ppermute(value, ALL_AXES, pairs)]
    ppermute x12 -> x13, starting transfers between devices: 13.2 us -> 14.1 us  [exchange(): return lax.ppermute(value, ALL_AXES, pairs)]
  transfers between devices with their start and end apart: 12 -> 13, of which waited for: 8 -> 8; matrix products, arithmetic and copies ran while one was open for 0% -> 0% of each run, Pallas kernels for 4% -> 4%
where the time goes in v5:
time: 52.9 us; the launch traced here: 52.7 us
  waiting for transfers between devices  21.9 us (41%)
  Pallas kernels  15.7 us (30%)
  starting transfers between devices  14.1 us (27%)
  between operations  0.83 us (2%)
    ppermute x13, waiting for transfers between devices, exchange(): return lax.ppermute(value, ALL_AXES, pairs)  21.9 us
    pallas_call x9, Pallas kernels, call(): pl.pallas_call(functools.partial(kernel, sizes), out_shape=out_shape, in_...  15.7 us
    ppermute x13, starting transfers between devices, exchange(): return lax.ppermute(value, ALL_AXES, pairs)  14.1 us
  transfers between devices with their start and end apart: 13, of which 8 were waited for; matrix products, arithmetic and copies ran while one was open for 0% of the time, Pallas kernels for 4%

profile of v5, /device:TPU:0, one launch (start us, length us, event | category | flops | bytes accessed | tf_op | source)
XLA Modules:
  0.0 52.7 jit_solution(10983158621046348418)
XLA Ops:
  0.6 0.0 copy-start
  0.6 1.4 %shard_map.85 = (f32[4,128,128]{2,1,0:T(8,128)S(1)}, f32[4,128,128]{2,1,0:T(8,128)S(1)}, f32[4,128,512]{2,1,0:T(8,128)S(1)}, s32[4,128]{1,0:T(4,128)S(1)}, s32[4]{0:T(128)S(1)}) custom-call(s32[4]{0:T(128)} %rank_hbm.1, f32[4,128,512]{2,1,0:T(8,128)} %bitcast.28, s32[4,128]{1,0:T(4,128)} %bitcast.30), custom_call_target="tpu_custom_call" | custom-call | flops 4096000 | bytes 1048576 | tf_op jit(solution)/shard_map/pallas_call | solution.py:468
  2.1 0.0 copy-done
  2.1 0.7 %shard_map.86 = f32[6,4,128,128]{3,2,1,0:T(8,128)S(1)} custom-call(s32[4]{0:T(128)S(1)} %get-tuple-element.17.rank_ref.refs_0_, f32[4,128,512]{2,1,0:T(8,128)S(1)} %get-tuple-element.20.temp_ref, f32[3,128,512]{2,1,0:T(8,128)S(1)} %copy-done, s32[4,128]{1,0:T(4,128)S(1)} %get-tuple-element.21.land_ref), custom_call_target="tpu_custom_call" | custom-call | flops 4096000 | bytes 1048576 | tf_op jit(solution)/shard_map/pallas_call | solution.py:468
  2.8 0.6 %collective-permute-start.6 = (f32[6,4,128,128]{3,2,1,0:T(8,128)S(1)}, f32[6,4,128,128]{3,2,1,0:T(8,128)S(1)}, u32[]{:S(2)}, u32[]{:S(2)}) collective-permute-start(f32[6,4,128,128]{3,2,1,0:T(8,128)S(1)} %shard_map.86), channel_id=1, source_target_pairs={{0,16},{1,17},{2,18},{3,19},{4,20},{5,21},{6,22},{7,23},{8,24},{9,... | collective-permute-start | bytes 4718600 | tf_op jit(solution)/shard_map/ppermute | solution.py:462
  3.3 0.1 collective-permute-start
  3.4 3.3 %collective-permute-done = f32[4,128,128]{2,1,0:T(8,128)S(1)} collective-permute-done((f32[4,128,128]{2,1,0:T(8,128)S(1)}, f32[4,128,128]{2,1,0:T(8,128)S(1)}, u32[]{:S(2)}, u32[]{:S(2)}) %collective-permute-start) | collective-permute-done | bytes 262176 | tf_op jit(solution)/shard_map/ppermute | solution.py:462
  6.8 0.0 collective-permute-done.6.pack_ref
  6.8 2.2 %shard_map.87.weight_ref.refs_1_ = f32[9,4,128,128]{3,2,1,0:T(8,128)S(1)} custom-call(s32[4]{0:T(128)S(1)} %get-tuple-element.17.rank_ref.refs_0_, f32[3,128,512]{2,1,0:T(8,128)S(1)} %copy-done, s32[4,128]{1,0:T(4,128)S(1)} %get-tuple-element.21.land_ref, f32[6,4,128,128]{3,2,1,0:T(8,128)S(1)} %collective-permute-done.6.pack_ref), custom_call_target="tpu_custom_call" | custom-call | flops 4096000 | bytes 1048576 | tf_op jit(solution)/shard_map/pallas_call | solution.py:468
  9.0 0.0 copy-start.1
  9.0 0.0 copy-start.2
  9.0 3.7 %shard_map.88.own_ref = f32[2,4,128,128]{3,2,1,0:T(8,128)S(1)} custom-call(s32[4]{0:T(128)S(1)} %get-tuple-element.17.rank_ref.refs_0_, f32[4,128,512]{2,1,0:T(8,128)S(1)} %get-tuple-element.20.temp_ref, s32[4,128]{1,0:T(4,128)S(1)} %get-tuple-element.21.land_ref, f32[6,4,128,128]{3,2,1,0:T(8,128)S(1)} %collective-permute-done.6.pack_ref, ...), custom_call_target="tpu_custom_call" | custom-call | flops 16384000 | bytes 1048576 | tf_op jit(solution)/shard_map/pallas_call | solution.py:468
  12.8 0.4 collective-permute-start.7
  13.2 2.7 %collective-permute-start.1 = (f32[128,128]{1,0:T(8,128)S(1)}, f32[128,128]{1,0:T(8,128)S(1)}, u32[]{:S(2)}, u32[]{:S(2)}) collective-permute-start(f32[128,128]{1,0:T(8,128)S(1)} %get-tuple-element.36), channel_id=1, source_target_pairs={{0,1},{1,0},{2,3},{3,2},{4,5},{5,4},{6,7},{7,6},{8,9},{9,8},{10,11... | collective-permute-start | bytes 196616 | tf_op jit(solution)/shard_map/ppermute | solution.py:462
  15.9 1.6 %collective-permute-start.2 = (f32[128,128]{1,0:T(8,128)S(1)}, f32[128,128]{1,0:T(8,128)S(1)}, u32[]{:S(2)}, u32[]{:S(2)}) collective-permute-start(f32[128,128]{1,0:T(8,128)S(1)} %get-tuple-element.35), channel_id=1, source_target_pairs={{0,2},{1,3},{2,0},{3,1},{4,6},{5,7},{6,4},{7,5},{8,10},{9,11},{10,... | collective-permute-start | bytes 196616 | tf_op jit(solution)/shard_map/ppermute | solution.py:462
  17.5 0.0 collective-permute-start.3
  17.5 0.7 %collective-permute-done.1 = f32[128,128]{1,0:T(8,128)S(1)} collective-permute-done((f32[128,128]{1,0:T(8,128)S(1)}, f32[128,128]{1,0:T(8,128)S(1)}, u32[]{:S(2)}, u32[]{:S(2)}) %collective-permute-start.1) | collective-permute-done | bytes 65568 | tf_op jit(solution)/shard_map/ppermute | solution.py:462
  18.2 2.3 %collective-permute-done.2 = f32[128,128]{1,0:T(8,128)S(1)} collective-permute-done((f32[128,128]{1,0:T(8,128)S(1)}, f32[128,128]{1,0:T(8,128)S(1)}, u32[]{:S(2)}, u32[]{:S(2)}) %collective-permute-start.2) | collective-permute-done | bytes 65568 | tf_op jit(solution)/shard_map/ppermute | solution.py:462
  20.5 2.2 %collective-permute-done.3 = f32[128,128]{1,0:T(8,128)S(1)} collective-permute-done((f32[128,128]{1,0:T(8,128)S(1)}, f32[128,128]{1,0:T(8,128)S(1)}, u32[]{:S(2)}, u32[]{:S(2)}) %collective-permute-start.3) | collective-permute-done | bytes 65568 | tf_op jit(solution)/shard_map/ppermute | solution.py:462
  22.7 2.7 %collective-permute-start.4 = (f32[128,128]{1,0:T(8,128)S(1)}, f32[128,128]{1,0:T(8,128)S(1)}, u32[]{:S(2)}, u32[]{:S(2)}) collective-permute-start(f32[128,128]{1,0:T(8,128)S(1)} %fusion.1), channel_id=1, source_target_pairs={{0,4},{1,5},{2,6},{3,7},{4,0},{5,1},{6,2},{7,3},{8,12},{9,13},{10,... | collective-permute-start | bytes 196616 | tf_op jit(solution)/shard_map/ppermute | solution.py:462
  25.3 4.2 %collective-permute-done.4 = f32[128,128]{1,0:T(8,128)S(1)} collective-permute-done((f32[128,128]{1,0:T(8,128)S(1)}, f32[128,128]{1,0:T(8,128)S(1)}, u32[]{:S(2)}, u32[]{:S(2)}) %collective-permute-start.4) | collective-permute-done | bytes 65568 | tf_op jit(solution)/shard_map/ppermute | solution.py:462
  29.6 1.6 %collective-permute-start.5 = (f32[128,128]{1,0:T(8,128)S(1)}, f32[128,128]{1,0:T(8,128)S(1)}, u32[]{:S(2)}, u32[]{:S(2)}) collective-permute-start(f32[128,128]{1,0:T(8,128)S(1)} %add.22), channel_id=1, source_target_pairs={{0,8},{1,9},{2,10},{3,11},{4,12},{5,13},{6,14},{7,15},{8,0},{9,1},... | collective-permute-start | bytes 196616 | tf_op jit(solution)/shard_map/ppermute | solution.py:462
  31.2 0.0 copy-done.1
  31.2 0.0 copy-done.2
  31.2 0.3 shard_map.91
  31.4 2.5 %collective-permute-done.5 = f32[128,128]{1,0:T(8,128)S(1)} collective-permute-done((f32[128,128]{1,0:T(8,128)S(1)}, f32[128,128]{1,0:T(8,128)S(1)}, u32[]{:S(2)}, u32[]{:S(2)}) %collective-permute-start.5) | collective-permute-done | bytes 65568 | tf_op jit(solution)/shard_map/ppermute | solution.py:462
  33.9 0.0 collective-permute-done.7.other_ref
  34.0 1.9 %shard_map.89 = (f32[4,128,512]{2,1,0:T(8,128)S(1)}, f32[8,128]{1,0:T(8,128)S(1)}) custom-call(s32[4]{0:T(128)S(1)} %get-tuple-element.17.rank_ref.refs_0_, f32[2,4,128,128]{3,2,1,0:T(8,128)S(1)} %shard_map.88.own_ref, f32[2,4,128,128]{3,2,1,0:T(8,128)S(1)} %collective-permute-done.7.other_ref, s32[1,256]{1,0:T(1,128)S(1)} %bitcast.26, f32[2,256]{1,0:T(2,128)S(1)} %copy-done.1), custom_call_target="tpu_custom_call" | custom-call | flops 8192000 | bytes 1048576 | tf_op jit(solution)/shard_map/pallas_call | solution.py:468
  35.8 1.0 %collective-permute-start.8 = (f32[8,128]{1,0:T(8,128)S(1)}, f32[8,128]{1,0:T(8,128)S(1)}, u32[]{:S(2)}, u32[]{:S(2)}) collective-permute-start(f32[8,128]{1,0:T(8,128)S(1)} %get-tuple-element.22), channel_id=1, source_target_pairs={{0,4},{1,5},{2,6},{3,7},{4,0},{5,1},{6,2},{7,3},{8,12},{9,13},{10,... | collective-permute-start | bytes 12296 | tf_op jit(solution)/shard_map/ppermute | solution.py:462
  36.9 3.6 %collective-permute-done.8 = f32[8,128]{1,0:T(8,128)S(1)} collective-permute-done((f32[8,128]{1,0:T(8,128)S(1)}, f32[8,128]{1,0:T(8,128)S(1)}, u32[]{:S(2)}, u32[]{:S(2)}) %collective-permute-start.8) | collective-permute-done | bytes 4128 | tf_op jit(solution)/shard_map/ppermute | solution.py:462
  40.4 0.6 %collective-permute-start.9 = (f32[144,128]{1,0:T(8,128)S(1)}, f32[144,128]{1,0:T(8,128)S(1)}, u32[]{:S(2)}, u32[]{:S(2)}) collective-permute-start(f32[144,128]{1,0:T(8,128)S(1)} %pad_maximum_fusion.1), channel_id=1, source_target_pairs={{0,1},{1,0},{2,3},{3,2},{4,5},{5,4},{6,7},{7,6},{8,9},{9,8},{10,11... | collective-permute-start | bytes 221192 | tf_op jit(solution)/shard_map/ppermute | solution.py:462
  41.1 0.0 collective-permute-start.10
  41.1 2.8 %collective-permute-start.11 = (f32[144,128]{1,0:T(8,128)S(1)}, f32[144,128]{1,0:T(8,128)S(1)}, u32[]{:S(2)}, u32[]{:S(2)}) collective-permute-start(f32[144,128]{1,0:T(8,128)S(1)} %pad_maximum_fusion.1), channel_id=1, source_target_pairs={{0,3},{1,2},{2,1},{3,0},{4,7},{5,6},{6,5},{7,4},{8,11},{9,10},{10,... | collective-permute-start | bytes 221192 | tf_op jit(solution)/shard_map/ppermute | solution.py:462
  43.9 3.1 %collective-permute-done.11 = f32[144,128]{1,0:T(8,128)S(1)} collective-permute-done((f32[144,128]{1,0:T(8,128)S(1)}, f32[144,128]{1,0:T(8,128)S(1)}, u32[]{:S(2)}, u32[]{:S(2)}) %collective-permute-start.11) | collective-permute-done | bytes 73760 | tf_op jit(solution)/shard_map/ppermute | solution.py:462
  47.0 0.0 collective-permute-done.10
  47.0 0.0 collective-permute-done.9
  47.1 2.0 %shard_map.90.mean_ref = f32[4,128,128]{2,1,0:T(8,128)S(1)} custom-call(f32[4,128,128]{2,1,0:T(8,128)S(1)} %pad_maximum_fusion.refs_0_, f32[9,4,128,128]{3,2,1,0:T(8,128)S(1)} %shard_map.87.weight_ref.refs_1_), custom_call_target="tpu_custom_call" | custom-call | flops 8192000 | bytes 1048576 | tf_op jit(solution)/shard_map/pallas_call | solution.py:468
  49.1 0.1 collective-permute-start.12
  49.2 1.7 %shard_map.92 = (f32[4,128,512]{2,1,0:T(8,128)}, f32[1,256]{1,0:T(1,128)S(1)}) custom-call(s32[4]{0:T(128)S(1)} %get-tuple-element.17.rank_ref.refs_0_, f32[4,128,128]{2,1,0:T(8,128)S(1)} %shard_map.90.mean_ref, f32[4,128,512]{2,1,0:T(8,128)S(1)} %get-tuple-element.25.stepped_ref.refs_6_, bf16[3072,256]{1,0:T(8,128)(2,1)S(1)} %get-tuple-element.23.column_ref.refs_2_, ...), custom_call_target="tpu_custom_call" | custom-call | flops 4096000 | bytes 1048576 | tf_op jit(solution)/shard_map/pallas_call | solution.py:468
  50.9 0.0 collective-permute-done.12.refs_1_
  50.9 1.8 %shard_map.93 = (f32[4,128,512]{2,1,0:T(8,128)}, f32[2,2,256]{2,1,0:T(2,128)}, f32[2,256]{1,0:T(2,128)}) custom-call(s32[4]{0:T(128)S(1)} %get-tuple-element.17.rank_ref.refs_0_, f32[4,128,128]{2,1,0:T(8,128)S(1)} %collective-permute-done.12.refs_1_, bf16[3072,256]{1,0:T(8,128)(2,1)S(1)} %get-tuple-element.23.column_ref.refs_2_, ...), custom_call_target="tpu_custom_call", output_to_operand_aliasing={{0}: (7, {})} | custom-call | flops 4096000 | bytes 1048576 | tf_op jit(solution)/shard_map/pallas_call | solution.py:468
  (15 shorter events, 0.1 us)
Async XLA Ops:
  0.6 1.5 %copy-start = (f32[3,128,512]{2,1,0:T(8,128)S(1)}, f32[3,128,512]{2,1,0:T(8,128)}, u32[]{:S(2)}) copy-start(f32[3,128,512]{2,1,0:T(8,128)} %kappa_ref.3) | copy-start | bytes 2359300
  2.8 4.0 %collective-permute-start.6 = (f32[6,4,128,128]{3,2,1,0:T(8,128)S(1)}, f32[6,4,128,128]{3,2,1,0:T(8,128)S(1)}, u32[]{:S(2)}, u32[]{:S(2)}) collective-permute-start(f32[6,4,128,128]{3,2,1,0:T(8,128)S(1)} %shard_map.86), channel_id=1, source_target_pairs={{0,16},{1,17},{2,18},{3,19},{4,20},{5,21},{6,22},{7,23},{8,24},{9,... | collective-permute-start | bytes 4718600 | tf_op jit(solution)/shard_map/ppermute | solution.py:462
  3.3 3.4 %collective-permute-start = (f32[4,128,128]{2,1,0:T(8,128)S(1)}, f32[4,128,128]{2,1,0:T(8,128)S(1)}, u32[]{:S(2)}, u32[]{:S(2)}) collective-permute-start(f32[4,128,128]{2,1,0:T(8,128)S(1)} %get-tuple-element.19), channel_id=1, source_target_pairs={{0,16},{1,17},{2,18},{3,19},{4,20},{5,21},{6,22},{7,23},{8,24},{9,... | collective-permute-start | bytes 786440 | tf_op jit(solution)/shard_map/ppermute | solution.py:462
  9.0 22.2 %copy-start.1 = (f32[2,256]{1,0:T(2,128)S(1)}, f32[2,256]{1,0:T(2,128)}, u32[]{:S(2)}) copy-start(f32[2,256]{1,0:T(2,128)} %frac_ref.3) | copy-start | bytes 6148
  9.0 22.1 %copy-start.2 = (s32[256]{0:T(256)S(1)}, s32[256]{0:T(256)}, u32[]{:S(2)}) copy-start(s32[256]{0:T(256)} %param.10) | copy-start | bytes 3076
  12.8 21.2 %collective-permute-start.7 = (f32[2,4,128,128]{3,2,1,0:T(8,128)S(1)}, f32[2,4,128,128]{3,2,1,0:T(8,128)S(1)}, u32[]{:S(2)}, u32[]{:S(2)}) collective-permute-start(f32[2,4,128,128]{3,2,1,0:T(8,128)S(1)} %shard_map.88.own_ref), channel_id=1, source_target_pairs={{0,16},{1,17},{2,18},{3,19},{4,20},{5,21},{6,22},{7,23},{8,24},{9,... | collective-permute-start | bytes 1572872 | tf_op jit(solution)/shard_map/ppermute | solution.py:462
  13.2 5.0 %collective-permute-start.1 = (f32[128,128]{1,0:T(8,128)S(1)}, f32[128,128]{1,0:T(8,128)S(1)}, u32[]{:S(2)}, u32[]{:S(2)}) collective-permute-start(f32[128,128]{1,0:T(8,128)S(1)} %get-tuple-element.36), channel_id=1, source_target_pairs={{0,1},{1,0},{2,3},{3,2},{4,5},{5,4},{6,7},{7,6},{8,9},{9,8},{10,11... | collective-permute-start | bytes 196616 | tf_op jit(solution)/shard_map/ppermute | solution.py:462
  15.9 4.6 %collective-permute-start.2 = (f32[128,128]{1,0:T(8,128)S(1)}, f32[128,128]{1,0:T(8,128)S(1)}, u32[]{:S(2)}, u32[]{:S(2)}) collective-permute-start(f32[128,128]{1,0:T(8,128)S(1)} %get-tuple-element.35), channel_id=1, source_target_pairs={{0,2},{1,3},{2,0},{3,1},{4,6},{5,7},{6,4},{7,5},{8,10},{9,11},{10,... | collective-permute-start | bytes 196616 | tf_op jit(solution)/shard_map/ppermute | solution.py:462
  17.5 5.2 %collective-permute-start.3 = (f32[128,128]{1,0:T(8,128)S(1)}, f32[128,128]{1,0:T(8,128)S(1)}, u32[]{:S(2)}, u32[]{:S(2)}) collective-permute-start(f32[128,128]{1,0:T(8,128)S(1)} %get-tuple-element.34), channel_id=1, source_target_pairs={{0,3},{1,2},{2,1},{3,0},{4,7},{5,6},{6,5},{7,4},{8,11},{9,10},{10,... | collective-permute-start | bytes 196616 | tf_op jit(solution)/shard_map/ppermute | solution.py:462
  22.7 6.9 %collective-permute-start.4 = (f32[128,128]{1,0:T(8,128)S(1)}, f32[128,128]{1,0:T(8,128)S(1)}, u32[]{:S(2)}, u32[]{:S(2)}) collective-permute-start(f32[128,128]{1,0:T(8,128)S(1)} %fusion.1), channel_id=1, source_target_pairs={{0,4},{1,5},{2,6},{3,7},{4,0},{5,1},{6,2},{7,3},{8,12},{9,13},{10,... | collective-permute-start | bytes 196616 | tf_op jit(solution)/shard_map/ppermute | solution.py:462
  29.6 4.3 %collective-permute-start.5 = (f32[128,128]{1,0:T(8,128)S(1)}, f32[128,128]{1,0:T(8,128)S(1)}, u32[]{:S(2)}, u32[]{:S(2)}) collective-permute-start(f32[128,128]{1,0:T(8,128)S(1)} %add.22), channel_id=1, source_target_pairs={{0,8},{1,9},{2,10},{3,11},{4,12},{5,13},{6,14},{7,15},{8,0},{9,1},... | collective-permute-start | bytes 196616 | tf_op jit(solution)/shard_map/ppermute | solution.py:462
  35.8 4.6 %collective-permute-start.8 = (f32[8,128]{1,0:T(8,128)S(1)}, f32[8,128]{1,0:T(8,128)S(1)}, u32[]{:S(2)}, u32[]{:S(2)}) collective-permute-start(f32[8,128]{1,0:T(8,128)S(1)} %get-tuple-element.22), channel_id=1, source_target_pairs={{0,4},{1,5},{2,6},{3,7},{4,0},{5,1},{6,2},{7,3},{8,12},{9,13},{10,... | collective-permute-start | bytes 12296 | tf_op jit(solution)/shard_map/ppermute | solution.py:462
  40.4 6.6 %collective-permute-start.9 = (f32[144,128]{1,0:T(8,128)S(1)}, f32[144,128]{1,0:T(8,128)S(1)}, u32[]{:S(2)}, u32[]{:S(2)}) collective-permute-start(f32[144,128]{1,0:T(8,128)S(1)} %pad_maximum_fusion.1), channel_id=1, source_target_pairs={{0,1},{1,0},{2,3},{3,2},{4,5},{5,4},{6,7},{7,6},{8,9},{9,8},{10,11... | collective-permute-start | bytes 221192 | tf_op jit(solution)/shard_map/ppermute | solution.py:462
  41.1 6.0 %collective-permute-start.10 = (f32[144,128]{1,0:T(8,128)S(1)}, f32[144,128]{1,0:T(8,128)S(1)}, u32[]{:S(2)}, u32[]{:S(2)}) collective-permute-start(f32[144,128]{1,0:T(8,128)S(1)} %pad_maximum_fusion.1), channel_id=1, source_target_pairs={{0,2},{1,3},{2,0},{3,1},{4,6},{5,7},{6,4},{7,5},{8,10},{9,11},{10,... | collective-permute-start | bytes 221192 | tf_op jit(solution)/shard_map/ppermute | solution.py:462
  41.1 6.0 %collective-permute-start.11 = (f32[144,128]{1,0:T(8,128)S(1)}, f32[144,128]{1,0:T(8,128)S(1)}, u32[]{:S(2)}, u32[]{:S(2)}) collective-permute-start(f32[144,128]{1,0:T(8,128)S(1)} %pad_maximum_fusion.1), channel_id=1, source_target_pairs={{0,3},{1,2},{2,1},{3,0},{4,7},{5,6},{6,5},{7,4},{8,11},{9,10},{10,... | collective-permute-start | bytes 221192 | tf_op jit(solution)/shard_map/ppermute | solution.py:462
  49.1 1.8 %collective-permute-start.12 = (f32[4,128,128]{2,1,0:T(8,128)S(1)}, f32[4,128,128]{2,1,0:T(8,128)S(1)}, u32[]{:S(2)}, u32[]{:S(2)}) collective-permute-start(f32[4,128,128]{2,1,0:T(8,128)S(1)} %shard_map.90.mean_ref), channel_id=1, source_target_pairs={{0,16},{1,17},{2,18},{3,19},{4,20},{5,21},{6,22},{7,23},{8,24},{9,... | collective-permute-start | bytes 786440 | tf_op jit(solution)/shard_map/ppermute | solution.py:462

commit v6 on v4

--- a/solution.py
+++ b/solution.py
@@ -11,6 +11,7 @@
 STEPS = 6
 LANES = 128
 PAD = 8
+COPIES = 2
 ALL_AXES = ("tile", "level", "member")
 VMEM = pl.BlockSpec(memory_space=pltpu.VMEM)
 SMEM = pl.BlockSpec(memory_space=pltpu.SMEM)
@@ -58,7 +59,11 @@
 ):
     members, fields, rows, tiles, _ = sizes
     core, mine, other = chunk_number()
-    pairs = ((rank_hbm, rank_ref), (land_hbm, land_ref), (temp_hbm, temp_ref), (rank_hbm, rank_out))
+    pairs = [(rank_hbm, rank_ref), (land_hbm, land_ref), (rank_hbm, rank_out)]
+    for plane in range(members * fields):
+        for part in range(COPIES):
+            at = pl.ds(part * rows // COPIES, rows // COPIES)
+            pairs.append((temp_hbm.at[plane, at], temp_ref.at[plane, at]))
     copies = [pltpu.make_async_copy(*pair, sem.at[number]) for number, pair in enumerate(pairs)]
     for copy in copies:
         copy.start()
@@ -97,7 +102,7 @@
             pack_ref[fields + 3, rank] = signed_number(land_ref, rank_ref, core, tile, rows, tiles)
 
 
-def weights_kernel(sizes, rank_ref, kappa_ref, land_ref, pack_ref, weight_ref, pad_ref, face_ref):
+def make_weights(sizes, rank_ref, kappa_ref, land_ref, pack_ref, weight_ref, pad_ref, face_ref):
     _, fields, rows, tiles, slots = sizes
     core, _, _ = chunk_number()
     band = float(2 * tiles)
@@ -238,9 +243,10 @@
                 u_ref[half, plane, slot, PAD + rows :, :] = zeros
 
 
-def member_kernel(sizes, rank_ref, temp_ref, land_ref, pack_ref, weight_ref, stepped_ref, u_ref):
+def member_kernel(sizes, rank_ref, kappa_ref, temp_ref, land_ref, pack_ref, weight_ref, stepped_ref, u_ref, pad_ref, face_ref):
     _, fields, rows, tiles, slots = sizes
     core, _, _ = chunk_number()
+    make_weights(sizes, rank_ref, kappa_ref, land_ref, pack_ref, weight_ref, pad_ref, face_ref)
     clear_pads(fields, rows, slots, u_ref)
     inside = slice(PAD, PAD + rows)
     for slot in range(slots):
@@ -363,13 +369,19 @@
     core, _, _ = chunk_number()
     write_planes(sizes, core, rank_ref, mean_ref, stepped_ref, field_hbm, field_ref, sem)
     mean_seen_ref[...] = observe_mean(sizes, rank_ref, mean_ref, column_ref, row_ref, whole_ref)
-    for member in range(members):
-        plane_copy(sizes, member, core, field_hbm, field_ref, sem).wait()
-
-
-def plane_copy(sizes, member, field, field_hbm, field_ref, sem):
-    _, fields, _, _, _ = sizes
-    return pltpu.make_async_copy(field_ref.at[member], field_hbm.at[member * fields + field], sem.at[member])
+    for copy in plane_copies(sizes, range(members), core, field_hbm, field_ref, sem):
+        copy.wait()
+
+
+def plane_copies(sizes, of_members, field, field_hbm, field_ref, sem):
+    _, fields, rows, _, _ = sizes
+    copies = []
+    for member in of_members:
+        for part in range(COPIES):
+            at = pl.ds(part * rows // COPIES, rows // COPIES)
+            target = field_hbm.at[member * fields + field, at]
+            copies.append(pltpu.make_async_copy(field_ref.at[member, at], target, sem.at[member * COPIES + part]))
+    return copies
 
 
 def write_planes(sizes, field, rank_ref, mean_ref, stepped_ref, field_hbm, field_ref, sem):
@@ -387,7 +399,8 @@
             def _():
                 field_ref[member, :, lanes] = stepped_ref[member * fields + field, :, lanes]
 
-        plane_copy(sizes, member, field, field_hbm, field_ref, sem).start()
+        for copy in plane_copies(sizes, [member], field, field_hbm, field_ref, sem):
+            copy.start()
 
 
 def final_kernel(
@@ -424,13 +437,13 @@
             for member in range(members):
                 anomaly_ref[member, field : field + 1, lanes] = anomaly[member]
     small = (
-        pltpu.make_async_copy(anomaly_ref, anomaly_hbm, sem.at[members]),
-        pltpu.make_async_copy(variance_ref, variance_hbm, sem.at[members + 1]),
+        pltpu.make_async_copy(anomaly_ref, anomaly_hbm, sem.at[members * COPIES]),
+        pltpu.make_async_copy(variance_ref, variance_hbm, sem.at[members * COPIES + 1]),
     )
     for copy in small:
         copy.start()
-    for member in range(members):
-        plane_copy(sizes, member, 1 - core, field_hbm, field_ref, sem).wait()
+    for copy in plane_copies(sizes, range(members), 1 - core, field_hbm, field_ref, sem):
+        copy.wait()
     for copy in small:
         copy.wait()
 
@@ -495,7 +508,7 @@
             jax.ShapeDtypeStruct((tiles,), jnp.int32),
         ),
         inputs,
-        scratch=[pltpu.SMEM((tiles,), jnp.int32), pltpu.SemaphoreType.DMA((4,))],
+        scratch=[pltpu.SMEM((tiles,), jnp.int32), pltpu.SemaphoreType.DMA((3 + planes * COPIES,))],
         in_specs=[HBM] * 3,
     )
     arrived = exchange(send, None)
@@ -505,13 +518,10 @@
     got = [exchange(total[k], masks[k]) for k in (1, 2, 3)]
     total = (total[0] + got[0]) + (got[1] + got[2])
 
-    weights = call(
-        weights_kernel, struct(9, slots, rows, LANES), (rank, diffusivity, land, packed),
-        [pltpu.VMEM((4, slots, rows + 2 * PAD, LANES), jnp.float32)] * 2,
-    )
-    own = call(
-        member_kernel, struct(fields, slots, rows, LANES), (rank, temp, land, packed, weights),
-        [halo(fields)], cycles=4000,
+    face = pltpu.VMEM((4, slots, rows + 2 * PAD, LANES), jnp.float32)
+    weights, own = call(
+        member_kernel, (struct(9, slots, rows, LANES), struct(fields, slots, rows, LANES)),
+        (rank, diffusivity, temp, land, packed), [halo(fields), face, face], cycles=6000,
     )
     other = exchange(own, None)
     stepped, seen = call(
@@ -546,7 +556,7 @@
     started, own_seen = call(
         own_field_kernel, (struct(planes, rows, columns), struct(1, count)),
         (rank, own_mean, stepped, column_picks, row_picks),
-        [plane_scratch, whole_scratch, pltpu.SemaphoreType.DMA((members,))], out_specs=(HBM, VMEM),
+        [plane_scratch, whole_scratch, pltpu.SemaphoreType.DMA((members * COPIES,))], out_specs=(HBM, VMEM),
     )
 
     def last_kernel(sizes, *refs):
@@ -562,7 +572,7 @@
             whole_scratch,
             pltpu.VMEM((members, fields, count), jnp.float32),
             pltpu.VMEM((fields, count), jnp.float32),
-            pltpu.SemaphoreType.DMA((members + 2,)),
+            pltpu.SemaphoreType.DMA((members * COPIES + 2,)),
         ],
         in_specs=[SMEM] + [VMEM] * 6 + [HBM],
         out_specs=(HBM, HBM, HBM),

time: 47 us -> 45.9 us (0.977)
  waiting for transfers between devices: 17 us -> 16.2 us
    ppermute x12, waiting for transfers between devices: 17 us -> 16.2 us  [exchange(): return lax.ppermute(value, ALL_AXES, pairs)]
    pallas_call x9 -> x8, Pallas kernels: 15.7 us -> 15.3 us  [call(): pl.pallas_call(functools.partial(kernel, sizes), out_shape=out_shape, in_...]
  transfers between devices with their start and end apart: 12 -> 12, of which waited for: 8 -> 9; matrix products, arithmetic and copies ran while one was open for 0% -> 0% of each run, Pallas kernels for 4% -> 4%
where the time goes in v6:
time: 45.9 us; the launch traced here: 45.8 us
  waiting for transfers between devices  16.2 us (35%)
  Pallas kernels  15.3 us (33%)
  starting transfers between devices  13.3 us (29%)
  between operations  0.84 us (2%)
    ppermute x12, waiting for transfers between devices, exchange(): return lax.ppermute(value, ALL_AXES, pairs)  16.2 us
    pallas_call x8, Pallas kernels, call(): pl.pallas_call(functools.partial(kernel, sizes), out_shape=out_shape, in_...  15.3 us
    ppermute x12, starting transfers between devices, exchange(): return lax.ppermute(value, ALL_AXES, pairs)  13.3 us
  transfers between devices with their start and end apart: 12, of which 9 were waited for; matrix products, arithmetic and copies ran while one was open for 0% of the time, Pallas kernels for 4%

profile of v6, /device:TPU:0, one launch (start us, length us, event | category | flops | bytes accessed | tf_op | source)
XLA Modules:
  0.0 45.8 jit_solution(1960119358037967864)
XLA Ops:
  0.6 0.0 copy-start
  0.6 1.6 %shard_map.85 = (f32[4,128,128]{2,1,0:T(8,128)S(1)}, f32[4,128,128]{2,1,0:T(8,128)S(1)}, f32[4,128,512]{2,1,0:T(8,128)S(1)}, s32[4,128]{1,0:T(4,128)S(1)}, s32[4]{0:T(128)S(1)}) custom-call(s32[4]{0:T(128)} %rank_hbm.1, f32[4,128,512]{2,1,0:T(8,128)} %bitcast.28, s32[4,128]{1,0:T(4,128)} %bitcast.30), custom_call_target="tpu_custom_call" | custom-call | flops 4096000 | bytes 1048576 | tf_op jit(solution)/shard_map/pallas_call | solution.py:481
  2.2 0.0 copy-done
  2.2 0.7 %shard_map.86 = f32[6,4,128,128]{3,2,1,0:T(8,128)S(1)} custom-call(s32[4]{0:T(128)S(1)} %get-tuple-element.19.rank_ref.refs_0_, f32[4,128,512]{2,1,0:T(8,128)S(1)} %get-tuple-element.22.temp_ref, f32[3,128,512]{2,1,0:T(8,128)S(1)} %copy-done, s32[4,128]{1,0:T(4,128)S(1)} %get-tuple-element.23.land_ref), custom_call_target="tpu_custom_call" | custom-call | flops 4096000 | bytes 1048576 | tf_op jit(solution)/shard_map/pallas_call | solution.py:481
  2.9 0.6 %collective-permute-start.5 = (f32[6,4,128,128]{3,2,1,0:T(8,128)S(1)}, f32[6,4,128,128]{3,2,1,0:T(8,128)S(1)}, u32[]{:S(2)}, u32[]{:S(2)}) collective-permute-start(f32[6,4,128,128]{3,2,1,0:T(8,128)S(1)} %shard_map.86), channel_id=1, source_target_pairs={{0,16},{1,17},{2,18},{3,19},{4,20},{5,21},{6,22},{7,23},{8,24},{9,... | collective-permute-start | bytes 4718600 | tf_op jit(solution)/shard_map/ppermute | solution.py:475
  3.4 0.1 collective-permute-start
  3.5 3.3 %collective-permute-done = f32[4,128,128]{2,1,0:T(8,128)S(1)} collective-permute-done((f32[4,128,128]{2,1,0:T(8,128)S(1)}, f32[4,128,128]{2,1,0:T(8,128)S(1)}, u32[]{:S(2)}, u32[]{:S(2)}) %collective-permute-start) | collective-permute-done | bytes 262176 | tf_op jit(solution)/shard_map/ppermute | solution.py:475
  6.9 0.0 copy-start.1
  6.9 0.0 copy-start.2
  6.9 0.0 collective-permute-done.5.pack_ref
  6.9 5.4 %shard_map.87 = (f32[9,4,128,128]{3,2,1,0:T(8,128)S(1)}, f32[2,4,128,128]{3,2,1,0:T(8,128)S(1)}) custom-call(s32[4]{0:T(128)S(1)} %get-tuple-element.19.rank_ref.refs_0_, f32[3,128,512]{2,1,0:T(8,128)S(1)} %copy-done, f32[4,128,512]{2,1,0:T(8,128)S(1)} %get-tuple-element.22.temp_ref, s32[4,128]{1,0:T(4,128)S(1)} %get-tuple-element.23.land_ref, ...), custom_call_target="tpu_custom_call" | custom-call | flops 24576000 | bytes 1048576 | tf_op jit(solution)/shard_map/pallas_call | solution.py:481
  12.3 0.4 collective-permute-start.6
  12.8 3.7 %collective-permute-start.3 = (f32[128,128]{1,0:T(8,128)S(1)}, f32[128,128]{1,0:T(8,128)S(1)}, u32[]{:S(2)}, u32[]{:S(2)}) collective-permute-start(f32[128,128]{1,0:T(8,128)S(1)} %get-tuple-element.38), channel_id=1, source_target_pairs={{0,3},{1,2},{2,1},{3,0},{4,7},{5,6},{6,5},{7,4},{8,11},{9,10},{10,... | collective-permute-start | bytes 196616 | tf_op jit(solution)/shard_map/ppermute | solution.py:475
  16.5 0.4 collective-permute-start.2
  17.0 0.2 collective-permute-start.1
  17.1 2.0 %collective-permute-done.3 = f32[128,128]{1,0:T(8,128)S(1)} collective-permute-done((f32[128,128]{1,0:T(8,128)S(1)}, f32[128,128]{1,0:T(8,128)S(1)}, u32[]{:S(2)}, u32[]{:S(2)}) %collective-permute-start.3) | collective-permute-done | bytes 65568 | tf_op jit(solution)/shard_map/ppermute | solution.py:475
  19.1 1.7 %collective-permute-done.2 = f32[128,128]{1,0:T(8,128)S(1)} collective-permute-done((f32[128,128]{1,0:T(8,128)S(1)}, f32[128,128]{1,0:T(8,128)S(1)}, u32[]{:S(2)}, u32[]{:S(2)}) %collective-permute-start.2) | collective-permute-done | bytes 65568 | tf_op jit(solution)/shard_map/ppermute | solution.py:475
  20.8 0.4 collective-permute-done.1
  21.2 1.6 %collective-permute-start.4 = (f32[128,128]{1,0:T(8,128)S(1)}, f32[128,128]{1,0:T(8,128)S(1)}, u32[]{:S(2)}, u32[]{:S(2)}) collective-permute-start(f32[128,128]{1,0:T(8,128)S(1)} %fusion.1), channel_id=1, source_target_pairs={{0,8},{1,9},{2,10},{3,11},{4,12},{5,13},{6,14},{7,15},{8,0},{9,1},... | collective-permute-start | bytes 196616 | tf_op jit(solution)/shard_map/ppermute | solution.py:475
  22.8 2.8 %collective-permute-done.4 = f32[128,128]{1,0:T(8,128)S(1)} collective-permute-done((f32[128,128]{1,0:T(8,128)S(1)}, f32[128,128]{1,0:T(8,128)S(1)}, u32[]{:S(2)}, u32[]{:S(2)}) %collective-permute-start.4) | collective-permute-done | bytes 65568 | tf_op jit(solution)/shard_map/ppermute | solution.py:475
  25.6 0.0 collective-permute-done.6.other_ref
  25.6 0.0 copy-done.1
  25.6 0.0 copy-done.2
  25.6 1.9 %shard_map.88 = (f32[4,128,512]{2,1,0:T(8,128)S(1)}, f32[8,128]{1,0:T(8,128)S(1)}) custom-call(s32[4]{0:T(128)S(1)} %get-tuple-element.19.rank_ref.refs_0_, f32[2,4,128,128]{3,2,1,0:T(8,128)S(1)} %get-tuple-element.24.own_ref, f32[2,4,128,128]{3,2,1,0:T(8,128)S(1)} %collective-permute-done.6.other_ref, s32[1,256]{1,0:T(1,128)S(1)} %bitcast.25, ...), custom_call_target="tpu_custom_call" | custom-call | flops 8192000 | bytes 1048576 | tf_op jit(solution)/shard_map/pallas_call | solution.py:481
  27.5 2.7 %collective-permute-start.7 = (f32[136,128]{1,0:T(8,128)S(1)}, f32[136,128]{1,0:T(8,128)S(1)}, u32[]{:S(2)}, u32[]{:S(2)}) collective-permute-start(f32[136,128]{1,0:T(8,128)S(1)} %pad_maximum_fusion.2), channel_id=1, source_target_pairs={{0,4},{1,5},{2,6},{3,7},{4,0},{5,1},{6,2},{7,3},{8,12},{9,13},{10,... | collective-permute-start | bytes 208904 | tf_op jit(solution)/shard_map/ppermute | solution.py:475
  30.2 2.6 %collective-permute-done.7 = f32[136,128]{1,0:T(8,128)S(1)} collective-permute-done((f32[136,128]{1,0:T(8,128)S(1)}, f32[136,128]{1,0:T(8,128)S(1)}, u32[]{:S(2)}, u32[]{:S(2)}) %collective-permute-start.7) | collective-permute-done | bytes 69664 | tf_op jit(solution)/shard_map/ppermute | solution.py:475
  32.8 1.8 %collective-permute-start.10 = (f32[144,128]{1,0:T(8,128)S(1)}, f32[144,128]{1,0:T(8,128)S(1)}, u32[]{:S(2)}, u32[]{:S(2)}) collective-permute-start(f32[144,128]{1,0:T(8,128)S(1)} %pad_maximum_fusion.1), channel_id=1, source_target_pairs={{0,3},{1,2},{2,1},{3,0},{4,7},{5,6},{6,5},{7,4},{8,11},{9,10},{10,... | collective-permute-start | bytes 221192 | tf_op jit(solution)/shard_map/ppermute | solution.py:475
  34.6 0.3 shard_map.90
  34.8 0.9 %collective-permute-start.9 = (f32[144,128]{1,0:T(8,128)S(1)}, f32[144,128]{1,0:T(8,128)S(1)}, u32[]{:S(2)}, u32[]{:S(2)}) collective-permute-start(f32[144,128]{1,0:T(8,128)S(1)} %pad_maximum_fusion.1), channel_id=1, source_target_pairs={{0,2},{1,3},{2,0},{3,1},{4,6},{5,7},{6,4},{7,5},{8,10},{9,11},{10,... | collective-permute-start | bytes 221192 | tf_op jit(solution)/shard_map/ppermute | solution.py:475
  35.7 1.0 %collective-permute-start.8 = (f32[144,128]{1,0:T(8,128)S(1)}, f32[144,128]{1,0:T(8,128)S(1)}, u32[]{:S(2)}, u32[]{:S(2)}) collective-permute-start(f32[144,128]{1,0:T(8,128)S(1)} %pad_maximum_fusion.1), channel_id=1, source_target_pairs={{0,1},{1,0},{2,3},{3,2},{4,5},{5,4},{6,7},{7,6},{8,9},{9,8},{10,11... | collective-permute-start | bytes 221192 | tf_op jit(solution)/shard_map/ppermute | solution.py:475
  36.7 1.4 %collective-permute-done.10 = f32[144,128]{1,0:T(8,128)S(1)} collective-permute-done((f32[144,128]{1,0:T(8,128)S(1)}, f32[144,128]{1,0:T(8,128)S(1)}, u32[]{:S(2)}, u32[]{:S(2)}) %collective-permute-start.10) | collective-permute-done | bytes 73760 | tf_op jit(solution)/shard_map/ppermute | solution.py:475
  38.1 1.1 %collective-permute-done.9 = f32[144,128]{1,0:T(8,128)S(1)} collective-permute-done((f32[144,128]{1,0:T(8,128)S(1)}, f32[144,128]{1,0:T(8,128)S(1)}, u32[]{:S(2)}, u32[]{:S(2)}) %collective-permute-start.9) | collective-permute-done | bytes 73760 | tf_op jit(solution)/shard_map/ppermute | solution.py:475
  39.3 0.8 %collective-permute-done.8 = f32[144,128]{1,0:T(8,128)S(1)} collective-permute-done((f32[144,128]{1,0:T(8,128)S(1)}, f32[144,128]{1,0:T(8,128)S(1)}, u32[]{:S(2)}, u32[]{:S(2)}) %collective-permute-start.8) | collective-permute-done | bytes 73760 | tf_op jit(solution)/shard_map/ppermute | solution.py:475
  40.1 2.0 %shard_map.89.mean_ref = f32[4,128,128]{2,1,0:T(8,128)S(1)} custom-call(f32[4,128,128]{2,1,0:T(8,128)S(1)} %pad_maximum_fusion.refs_0_, f32[9,4,128,128]{3,2,1,0:T(8,128)S(1)} %get-tuple-element.26.refs_1_), custom_call_target="tpu_custom_call" | custom-call | flops 8192000 | bytes 1048576 | tf_op jit(solution)/shard_map/pallas_call | solution.py:481
  42.1 0.1 collective-permute-start.11
  42.2 1.7 %shard_map.91 = (f32[4,128,512]{2,1,0:T(8,128)}, f32[1,256]{1,0:T(1,128)S(1)}) custom-call(s32[4]{0:T(128)S(1)} %get-tuple-element.19.rank_ref.refs_0_, f32[4,128,128]{2,1,0:T(8,128)S(1)} %shard_map.89.mean_ref, f32[4,128,512]{2,1,0:T(8,128)S(1)} %get-tuple-element.29.stepped_ref.refs_6_, bf16[3072,256]{1,0:T(8,128)(2,1)S(1)} %get-tuple-element.27.column_ref.refs_2_, ...), custom_call_target="tpu_custom_call" | custom-call | flops 4096000 | bytes 1048576 | tf_op jit(solution)/shard_map/pallas_call | solution.py:481
  44.0 0.0 collective-permute-done.11.refs_1_
  44.0 1.8 %shard_map.92 = (f32[4,128,512]{2,1,0:T(8,128)}, f32[2,2,256]{2,1,0:T(2,128)}, f32[2,256]{1,0:T(2,128)}) custom-call(s32[4]{0:T(128)S(1)} %get-tuple-element.19.rank_ref.refs_0_, f32[4,128,128]{2,1,0:T(8,128)S(1)} %collective-permute-done.11.refs_1_, bf16[3072,256]{1,0:T(8,128)(2,1)S(1)} %get-tuple-element.27.column_ref.refs_2_, ...), custom_call_target="tpu_custom_call", output_to_operand_aliasing={{0}: (7, {})} | custom-call | flops 4096000 | bytes 1048576 | tf_op jit(solution)/shard_map/pallas_call | solution.py:481
  (16 shorter events, 0.1 us)
Async XLA Ops:
  0.6 1.6 %copy-start = (f32[3,128,512]{2,1,0:T(8,128)S(1)}, f32[3,128,512]{2,1,0:T(8,128)}, u32[]{:S(2)}) copy-start(f32[3,128,512]{2,1,0:T(8,128)} %kappa_ref.3) | copy-start | bytes 2359300
  2.9 4.0 %collective-permute-start.5 = (f32[6,4,128,128]{3,2,1,0:T(8,128)S(1)}, f32[6,4,128,128]{3,2,1,0:T(8,128)S(1)}, u32[]{:S(2)}, u32[]{:S(2)}) collective-permute-start(f32[6,4,128,128]{3,2,1,0:T(8,128)S(1)} %shard_map.86), channel_id=1, source_target_pairs={{0,16},{1,17},{2,18},{3,19},{4,20},{5,21},{6,22},{7,23},{8,24},{9,... | collective-permute-start | bytes 4718600 | tf_op jit(solution)/shard_map/ppermute | solution.py:475
  3.4 3.4 %collective-permute-start = (f32[4,128,128]{2,1,0:T(8,128)S(1)}, f32[4,128,128]{2,1,0:T(8,128)S(1)}, u32[]{:S(2)}, u32[]{:S(2)}) collective-permute-start(f32[4,128,128]{2,1,0:T(8,128)S(1)} %get-tuple-element.21), channel_id=1, source_target_pairs={{0,16},{1,17},{2,18},{3,19},{4,20},{5,21},{6,22},{7,23},{8,24},{9,... | collective-permute-start | bytes 786440 | tf_op jit(solution)/shard_map/ppermute | solution.py:475
  6.9 18.7 %copy-start.1 = (f32[2,256]{1,0:T(2,128)S(1)}, f32[2,256]{1,0:T(2,128)}, u32[]{:S(2)}) copy-start(f32[2,256]{1,0:T(2,128)} %frac_ref.3) | copy-start | bytes 6148
  6.9 18.7 %copy-start.2 = (s32[256]{0:T(256)S(1)}, s32[256]{0:T(256)}, u32[]{:S(2)}) copy-start(s32[256]{0:T(256)} %param.10) | copy-start | bytes 3076
  12.3 13.2 %collective-permute-start.6 = (f32[2,4,128,128]{3,2,1,0:T(8,128)S(1)}, f32[2,4,128,128]{3,2,1,0:T(8,128)S(1)}, u32[]{:S(2)}, u32[]{:S(2)}) collective-permute-start(f32[2,4,128,128]{3,2,1,0:T(8,128)S(1)} %get-tuple-element.24.own_ref), channel_id=1, source_target_pairs={{0,16},{1,17},{2,18},{3,19},{4,20},{5,21},{6,22},{7,23},{8,24},{9,... | collective-permute-start | bytes 1572872 | tf_op jit(solution)/shard_map/ppermute | solution.py:475
  12.8 6.4 %collective-permute-start.3 = (f32[128,128]{1,0:T(8,128)S(1)}, f32[128,128]{1,0:T(8,128)S(1)}, u32[]{:S(2)}, u32[]{:S(2)}) collective-permute-start(f32[128,128]{1,0:T(8,128)S(1)} %get-tuple-element.38), channel_id=1, source_target_pairs={{0,3},{1,2},{2,1},{3,0},{4,7},{5,6},{6,5},{7,4},{8,11},{9,10},{10,... | collective-permute-start | bytes 196616 | tf_op jit(solution)/shard_map/ppermute | solution.py:475
  16.5 4.3 %collective-permute-start.2 = (f32[128,128]{1,0:T(8,128)S(1)}, f32[128,128]{1,0:T(8,128)S(1)}, u32[]{:S(2)}, u32[]{:S(2)}) collective-permute-start(f32[128,128]{1,0:T(8,128)S(1)} %get-tuple-element.39), channel_id=1, source_target_pairs={{0,2},{1,3},{2,0},{3,1},{4,6},{5,7},{6,4},{7,5},{8,10},{9,11},{10,... | collective-permute-start | bytes 196616 | tf_op jit(solution)/shard_map/ppermute | solution.py:475
  17.0 4.3 %collective-permute-start.1 = (f32[128,128]{1,0:T(8,128)S(1)}, f32[128,128]{1,0:T(8,128)S(1)}, u32[]{:S(2)}, u32[]{:S(2)}) collective-permute-start(f32[128,128]{1,0:T(8,128)S(1)} %get-tuple-element.40), channel_id=1, source_target_pairs={{0,1},{1,0},{2,3},{3,2},{4,5},{5,4},{6,7},{7,6},{8,9},{9,8},{10,11... | collective-permute-start | bytes 196616 | tf_op jit(solution)/shard_map/ppermute | solution.py:475
  21.2 4.3 %collective-permute-start.4 = (f32[128,128]{1,0:T(8,128)S(1)}, f32[128,128]{1,0:T(8,128)S(1)}, u32[]{:S(2)}, u32[]{:S(2)}) collective-permute-start(f32[128,128]{1,0:T(8,128)S(1)} %fusion.1), channel_id=1, source_target_pairs={{0,8},{1,9},{2,10},{3,11},{4,12},{5,13},{6,14},{7,15},{8,0},{9,1},... | collective-permute-start | bytes 196616 | tf_op jit(solution)/shard_map/ppermute | solution.py:475
  27.5 5.3 %collective-permute-start.7 = (f32[136,128]{1,0:T(8,128)S(1)}, f32[136,128]{1,0:T(8,128)S(1)}, u32[]{:S(2)}, u32[]{:S(2)}) collective-permute-start(f32[136,128]{1,0:T(8,128)S(1)} %pad_maximum_fusion.2), channel_id=1, source_target_pairs={{0,4},{1,5},{2,6},{3,7},{4,0},{5,1},{6,2},{7,3},{8,12},{9,13},{10,... | collective-permute-start | bytes 208904 | tf_op jit(solution)/shard_map/ppermute | solution.py:475
  32.8 5.3 %collective-permute-start.10 = (f32[144,128]{1,0:T(8,128)S(1)}, f32[144,128]{1,0:T(8,128)S(1)}, u32[]{:S(2)}, u32[]{:S(2)}) collective-permute-start(f32[144,128]{1,0:T(8,128)S(1)} %pad_maximum_fusion.1), channel_id=1, source_target_pairs={{0,3},{1,2},{2,1},{3,0},{4,7},{5,6},{6,5},{7,4},{8,11},{9,10},{10,... | collective-permute-start | bytes 221192 | tf_op jit(solution)/shard_map/ppermute | solution.py:475
  34.8 4.4 %collective-permute-start.9 = (f32[144,128]{1,0:T(8,128)S(1)}, f32[144,128]{1,0:T(8,128)S(1)}, u32[]{:S(2)}, u32[]{:S(2)}) collective-permute-start(f32[144,128]{1,0:T(8,128)S(1)} %pad_maximum_fusion.1), channel_id=1, source_target_pairs={{0,2},{1,3},{2,0},{3,1},{4,6},{5,7},{6,4},{7,5},{8,10},{9,11},{10,... | collective-permute-start | bytes 221192 | tf_op jit(solution)/shard_map/ppermute | solution.py:475
  35.7 4.4 %collective-permute-start.8 = (f32[144,128]{1,0:T(8,128)S(1)}, f32[144,128]{1,0:T(8,128)S(1)}, u32[]{:S(2)}, u32[]{:S(2)}) collective-permute-start(f32[144,128]{1,0:T(8,128)S(1)} %pad_maximum_fusion.1), channel_id=1, source_target_pairs={{0,1},{1,0},{2,3},{3,2},{4,5},{5,4},{6,7},{7,6},{8,9},{9,8},{10,11... | collective-permute-start | bytes 221192 | tf_op jit(solution)/shard_map/ppermute | solution.py:475
  42.1 1.8 %collective-permute-start.11 = (f32[4,128,128]{2,1,0:T(8,128)S(1)}, f32[4,128,128]{2,1,0:T(8,128)S(1)}, u32[]{:S(2)}, u32[]{:S(2)}) collective-permute-start(f32[4,128,128]{2,1,0:T(8,128)S(1)} %shard_map.89.mean_ref), channel_id=1, source_target_pairs={{0,16},{1,17},{2,18},{3,19},{4,20},{5,21},{6,22},{7,23},{8,24},{9,... | collective-permute-start | bytes 786440 | tf_op jit(solution)/shard_map/ppermute | solution.py:475

commit v7 on v6

--- a/solution.py
+++ b/solution.py
@@ -11,7 +11,7 @@
 STEPS = 6
 LANES = 128
 PAD = 8
-COPIES = 2
+COPIES = 1
 ALL_AXES = ("tile", "level", "member")
 VMEM = pl.BlockSpec(memory_space=pltpu.VMEM)
 SMEM = pl.BlockSpec(memory_space=pltpu.SMEM)
@@ -54,40 +54,44 @@
     return (2.0 * wet_mask(land_ref, rank_ref, tile, rows) - 1.0) * number
 
 
-def sums_kernel(
-    sizes, rank_hbm, temp_hbm, land_hbm, send_ref, keep_ref, temp_ref, land_ref, rank_out, rank_ref, sem
-):
-    members, fields, rows, tiles, _ = sizes
-    core, mine, other = chunk_number()
+def slot_sums(sizes, rank_ref, land_ref, load, slot, total_ref):
+    members, _, rows, tiles, _ = sizes
+    for tile in range(tiles):
+        lanes = slice(tile * LANES, (tile + 1) * LANES)
+
+        @pl.when(rank_ref[tile] >= 0)
+        def _():
+            rank = rank_ref[tile]
+            wet = wet_mask(land_ref, rank_ref, tile, rows)
+            total = load(0, lanes) * wet
+            for member in range(1, members):
+                total = total + load(member, lanes) * wet
+            total_ref[jnp.bitwise_xor(slot, rank)] = total
+
+
+def sums_kernel(sizes, rank_hbm, temp_hbm, land_hbm, send_ref, land_ref, rank_out, rank_ref, temp_ref, sem):
+    members, fields, _, _, _ = sizes
+    core, _, other = chunk_number()
     pairs = [(rank_hbm, rank_ref), (land_hbm, land_ref), (rank_hbm, rank_out)]
-    for plane in range(members * fields):
-        for part in range(COPIES):
-            at = pl.ds(part * rows // COPIES, rows // COPIES)
-            pairs.append((temp_hbm.at[plane, at], temp_ref.at[plane, at]))
+    pairs += [(temp_hbm.at[member * fields + 1 - core], temp_ref.at[member]) for member in range(members)]
     copies = [pltpu.make_async_copy(*pair, sem.at[number]) for number, pair in enumerate(pairs)]
     for copy in copies:
         copy.start()
     send_ref[...] = jnp.zeros_like(send_ref)
-    keep_ref[...] = jnp.zeros_like(keep_ref)
     for copy in copies:
         copy.wait()
-    for tile in range(tiles):
-        lanes = slice(tile * LANES, (tile + 1) * LANES)
-
-        @pl.when(rank_ref[tile] >= 0)
-        def _():
-            rank = rank_ref[tile]
-            wet = wet_mask(land_ref, rank_ref, tile, rows)
-            for ref, slot, field in ((send_ref, other, 1 - core), (keep_ref, mine, core)):
-                total = temp_ref[field, :, lanes] * wet
-                for member in range(1, members):
-                    total = total + temp_ref[member * fields + field, :, lanes] * wet
-                ref[jnp.bitwise_xor(slot, rank)] = total
-
-
-def pack_kernel(sizes, rank_ref, temp_ref, kappa_ref, land_ref, pack_ref):
+    slot_sums(sizes, rank_ref, land_ref, lambda member, lanes: temp_ref[member, :, lanes], other, send_ref)
+
+
+def pack_kernel(sizes, rank_ref, temp_ref, kappa_hbm, land_ref, pack_ref, keep_ref, kappa_ref, sem):
     _, fields, rows, tiles, _ = sizes
-    core, _, _ = chunk_number()
+    core, mine, _ = chunk_number()
+    copy = pltpu.make_async_copy(kappa_hbm, kappa_ref, sem)
+    copy.start()
+    keep_ref[...] = jnp.zeros_like(keep_ref)
+    slot_sums(
+        sizes, rank_ref, land_ref, lambda member, lanes: temp_ref[member * fields + core, :, lanes], mine, keep_ref
+    )
     for tile in range(tiles):
         lanes = slice(tile * LANES, (tile + 1) * LANES)
 
@@ -97,9 +101,16 @@
             wet = wet_mask(land_ref, rank_ref, tile, rows)
             for field in range(fields):
                 pack_ref[field, rank] = temp_ref[(1 - core) * fields + field, :, lanes] * wet
+            pack_ref[fields + 3, rank] = signed_number(land_ref, rank_ref, core, tile, rows, tiles)
+
+    copy.wait()
+    for tile in range(tiles):
+        lanes = slice(tile * LANES, (tile + 1) * LANES)
+
+        @pl.when(rank_ref[tile] >= 0)
+        def _():
             for part in range(3):
-                pack_ref[fields + part, rank] = kappa_ref[part, :, lanes]
-            pack_ref[fields + 3, rank] = signed_number(land_ref, rank_ref, core, tile, rows, tiles)
+                pack_ref[fields + part, rank_ref[tile]] = kappa_ref[part, :, lanes]
 
 
 def make_weights(sizes, rank_ref, kappa_ref, land_ref, pack_ref, weight_ref, pad_ref, face_ref):
@@ -498,21 +509,29 @@
     masks = {1: (1, 2), 2: (2, 1), 3: (3, 3)}
 
     inputs = tuple(pltpu.with_memory_space_constraint(x, pltpu.HBM) for x in (wet_rank, temp, land))
-    send, keep, temp, land, rank = call(
+    send, land, rank = call(
         sums_kernel,
         (
             struct(slots, rows, LANES),
-            struct(slots, rows, LANES),
-            struct(planes, rows, columns),
             jax.ShapeDtypeStruct((tiles, LANES), jnp.int32),
             jax.ShapeDtypeStruct((tiles,), jnp.int32),
         ),
         inputs,
-        scratch=[pltpu.SMEM((tiles,), jnp.int32), pltpu.SemaphoreType.DMA((3 + planes * COPIES,))],
+        scratch=[
+            pltpu.SMEM((tiles,), jnp.int32),
+            pltpu.VMEM((members, rows, columns), jnp.float32),
+            pltpu.SemaphoreType.DMA((3 + members,)),
+        ],
         in_specs=[HBM] * 3,
     )
     arrived = exchange(send, None)
-    pack = call(pack_kernel, struct(fields + 4, slots, rows, LANES), (rank, temp, diffusivity, land))
+    pack, keep, kappa = call(
+        pack_kernel,
+        (struct(fields + 4, slots, rows, LANES), struct(slots, rows, LANES), struct(*diffusivity.shape)),
+        (rank, temp, pltpu.with_memory_space_constraint(diffusivity, pltpu.HBM), land),
+        scratch=[pltpu.SemaphoreType.DMA],
+        in_specs=[SMEM, VMEM, HBM, VMEM],
+    )
     packed = exchange(pack, None)
     total = keep + arrived
     got = [exchange(total[k], masks[k]) for k in (1, 2, 3)]
@@ -521,7 +540,7 @@
     face = pltpu.VMEM((4, slots, rows + 2 * PAD, LANES), jnp.float32)
     weights, own = call(
         member_kernel, (struct(9, slots, rows, LANES), struct(fields, slots, rows, LANES)),
-        (rank, diffusivity, temp, land, packed), [halo(fields), face, face], cycles=6000,
+        (rank, kappa, temp, land, packed), [halo(fields), face, face], cycles=6000,
     )
     other = exchange(own, None)
     stepped, seen = call(

time: 45.9 us -> 47.5 us (1.035)
  waiting for transfers between devices: 16.2 us -> 17 us
  Pallas kernels: 15.3 us -> 16 us
    ppermute x12, waiting for transfers between devices: 16.2 us -> 17 us  [exchange(): return lax.ppermute(value, ALL_AXES, pairs)]
    pallas_call x8, Pallas kernels: 15.3 us -> 16 us  [call(): pl.pallas_call(functools.partial(kernel, sizes), out_shape=out_shape, in_...]
  transfers between devices with their start and end apart: 12 -> 12, of which waited for: 9 -> 8; matrix products, arithmetic and copies ran while one was open for 0% -> 0% of each run, Pallas kernels for 4% -> 4%
where the time goes in v7:
time: 47.5 us; the launch traced here: 47.4 us
  waiting for transfers between devices  17 us (36%)
  Pallas kernels  16 us (34%)
  starting transfers between devices  13.2 us (28%)
  between operations  0.84 us (2%)
    ppermute x12, waiting for transfers between devices, exchange(): return lax.ppermute(value, ALL_AXES, pairs)  17 us
    pallas_call x8, Pallas kernels, call(): pl.pallas_call(functools.partial(kernel, sizes), out_shape=out_shape, in_...  16 us
    ppermute x12, starting transfers between devices, exchange(): return lax.ppermute(value, ALL_AXES, pairs)  13.2 us
  transfers between devices with their start and end apart: 12, of which 8 were waited for; matrix products, arithmetic and copies ran while one was open for 0% of the time, Pallas kernels for 4%

profile of v7, /device:TPU:0, one launch (start us, length us, event | category | flops | bytes accessed | tf_op | source)
XLA Modules:
  0.0 47.4 jit_solution(4463656966624834923)
XLA Ops:
  0.6 0.0 copy-start
  0.6 1.3 %shard_map.85 = (f32[4,128,128]{2,1,0:T(8,128)S(1)}, s32[4,128]{1,0:T(4,128)S(1)}, s32[4]{0:T(128)S(1)}) custom-call(s32[4]{0:T(128)} %rank_hbm.1, f32[4,128,512]{2,1,0:T(8,128)} %bitcast.25, s32[4,128]{1,0:T(4,128)} %bitcast.32), custom_call_target="tpu_custom_call" | custom-call | flops 4096000 | bytes 1048576 | tf_op jit(solution)/shard_map/pallas_call | solution.py:492
  1.9 0.1 copy-done
  2.0 1.7 %shard_map.86 = (f32[6,4,128,128]{3,2,1,0:T(8,128)S(1)}, f32[4,128,128]{2,1,0:T(8,128)S(1)}, f32[3,128,512]{2,1,0:T(8,128)S(1)}) custom-call(s32[4]{0:T(128)S(1)} %get-tuple-element.20.rank_ref.refs_0_, f32[4,128,512]{2,1,0:T(8,128)S(1)} %bitcast.26, f32[3,128,512]{2,1,0:T(8,128)} %kappa_hbm.1, s32[4,128]{1,0:T(4,128)S(1)} %get-tuple-element.21.land_ref), custom_call_target="tpu_custom_call" | custom-call | flops 4096000 | bytes 1048576 | tf_op jit(solution)/shard_map/pallas_call | solution.py:492
  3.8 0.6 %collective-permute-start.5 = (f32[6,4,128,128]{3,2,1,0:T(8,128)S(1)}, f32[6,4,128,128]{3,2,1,0:T(8,128)S(1)}, u32[]{:S(2)}, u32[]{:S(2)}) collective-permute-start(f32[6,4,128,128]{3,2,1,0:T(8,128)S(1)} %get-tuple-element.25), channel_id=1, source_target_pairs={{0,16},{1,17},{2,18},{3,19},{4,20},{5,21},{6,22},{7,23},{8,24},{9,... | collective-permute-start | bytes 4718600 | tf_op jit(solution)/shard_map/ppermute | solution.py:486
  4.4 0.1 collective-permute-start
  4.4 3.3 %collective-permute-done = f32[4,128,128]{2,1,0:T(8,128)S(1)} collective-permute-done((f32[4,128,128]{2,1,0:T(8,128)S(1)}, f32[4,128,128]{2,1,0:T(8,128)S(1)}, u32[]{:S(2)}, u32[]{:S(2)}) %collective-permute-start) | collective-permute-done | bytes 262176 | tf_op jit(solution)/shard_map/ppermute | solution.py:486
  7.8 0.0 collective-permute-done.5.pack_ref
  7.8 0.0 copy-start.1
  7.8 0.0 copy-start.2
  7.8 5.4 %shard_map.87 = (f32[9,4,128,128]{3,2,1,0:T(8,128)S(1)}, f32[2,4,128,128]{3,2,1,0:T(8,128)S(1)}) custom-call(s32[4]{0:T(128)S(1)} %get-tuple-element.20.rank_ref.refs_0_, f32[3,128,512]{2,1,0:T(8,128)S(1)} %get-tuple-element.24.kappa_ref, f32[4,128,512]{2,1,0:T(8,128)S(1)} %bitcast.27, s32[4,128]{1,0:T(4,128)S(1)} %get-tuple-element.21.land_ref, ...), custom_call_target="tpu_custom_call" | custom-call | flops 24576000 | bytes 1048576 | tf_op jit(solution)/shard_map/pallas_call | solution.py:492
  13.2 0.4 collective-permute-start.6
  13.7 2.7 %collective-permute-start.1 = (f32[128,128]{1,0:T(8,128)S(1)}, f32[128,128]{1,0:T(8,128)S(1)}, u32[]{:S(2)}, u32[]{:S(2)}) collective-permute-start(f32[128,128]{1,0:T(8,128)S(1)} %get-tuple-element.42), channel_id=1, source_target_pairs={{0,1},{1,0},{2,3},{3,2},{4,5},{5,4},{6,7},{7,6},{8,9},{9,8},{10,11... | collective-permute-start | bytes 196616 | tf_op jit(solution)/shard_map/ppermute | solution.py:486
  16.4 1.6 %collective-permute-start.2 = (f32[128,128]{1,0:T(8,128)S(1)}, f32[128,128]{1,0:T(8,128)S(1)}, u32[]{:S(2)}, u32[]{:S(2)}) collective-permute-start(f32[128,128]{1,0:T(8,128)S(1)} %get-tuple-element.41), channel_id=1, source_target_pairs={{0,2},{1,3},{2,0},{3,1},{4,6},{5,7},{6,4},{7,5},{8,10},{9,11},{10,... | collective-permute-start | bytes 196616 | tf_op jit(solution)/shard_map/ppermute | solution.py:486
  18.0 0.0 collective-permute-start.3
  18.0 0.7 %collective-permute-done.1 = f32[128,128]{1,0:T(8,128)S(1)} collective-permute-done((f32[128,128]{1,0:T(8,128)S(1)}, f32[128,128]{1,0:T(8,128)S(1)}, u32[]{:S(2)}, u32[]{:S(2)}) %collective-permute-start.1) | collective-permute-done | bytes 65568 | tf_op jit(solution)/shard_map/ppermute | solution.py:486
  18.6 2.3 %collective-permute-done.2 = f32[128,128]{1,0:T(8,128)S(1)} collective-permute-done((f32[128,128]{1,0:T(8,128)S(1)}, f32[128,128]{1,0:T(8,128)S(1)}, u32[]{:S(2)}, u32[]{:S(2)}) %collective-permute-start.2) | collective-permute-done | bytes 65568 | tf_op jit(solution)/shard_map/ppermute | solution.py:486
  21.0 2.2 %collective-permute-done.3 = f32[128,128]{1,0:T(8,128)S(1)} collective-permute-done((f32[128,128]{1,0:T(8,128)S(1)}, f32[128,128]{1,0:T(8,128)S(1)}, u32[]{:S(2)}, u32[]{:S(2)}) %collective-permute-start.3) | collective-permute-done | bytes 65568 | tf_op jit(solution)/shard_map/ppermute | solution.py:486
  23.2 1.6 %collective-permute-start.4 = (f32[128,128]{1,0:T(8,128)S(1)}, f32[128,128]{1,0:T(8,128)S(1)}, u32[]{:S(2)}, u32[]{:S(2)}) collective-permute-start(f32[128,128]{1,0:T(8,128)S(1)} %fusion.1), channel_id=1, source_target_pairs={{0,8},{1,9},{2,10},{3,11},{4,12},{5,13},{6,14},{7,15},{8,0},{9,1},... | collective-permute-start | bytes 196616 | tf_op jit(solution)/shard_map/ppermute | solution.py:486
  24.7 2.8 %collective-permute-done.4 = f32[128,128]{1,0:T(8,128)S(1)} collective-permute-done((f32[128,128]{1,0:T(8,128)S(1)}, f32[128,128]{1,0:T(8,128)S(1)}, u32[]{:S(2)}, u32[]{:S(2)}) %collective-permute-start.4) | collective-permute-done | bytes 65568 | tf_op jit(solution)/shard_map/ppermute | solution.py:486
  27.5 0.0 collective-permute-done.6.other_ref
  27.5 0.0 copy-done.1
  27.5 0.0 copy-done.2
  27.5 1.9 %shard_map.88 = (f32[4,128,512]{2,1,0:T(8,128)S(1)}, f32[8,128]{1,0:T(8,128)S(1)}) custom-call(s32[4]{0:T(128)S(1)} %get-tuple-element.20.rank_ref.refs_0_, f32[2,4,128,128]{3,2,1,0:T(8,128)S(1)} %get-tuple-element.26.own_ref, f32[2,4,128,128]{3,2,1,0:T(8,128)S(1)} %collective-permute-done.6.other_ref, s32[1,256]{1,0:T(1,128)S(1)} %bitcast.28, ...), custom_call_target="tpu_custom_call" | custom-call | flops 8192000 | bytes 1048576 | tf_op jit(solution)/shard_map/pallas_call | solution.py:492
  29.4 2.7 %collective-permute-start.7 = (f32[136,128]{1,0:T(8,128)S(1)}, f32[136,128]{1,0:T(8,128)S(1)}, u32[]{:S(2)}, u32[]{:S(2)}) collective-permute-start(f32[136,128]{1,0:T(8,128)S(1)} %pad_maximum_fusion.2), channel_id=1, source_target_pairs={{0,4},{1,5},{2,6},{3,7},{4,0},{5,1},{6,2},{7,3},{8,12},{9,13},{10,... | collective-permute-start | bytes 208904 | tf_op jit(solution)/shard_map/ppermute | solution.py:486
  32.1 3.4 %collective-permute-done.7 = f32[136,128]{1,0:T(8,128)S(1)} collective-permute-done((f32[136,128]{1,0:T(8,128)S(1)}, f32[136,128]{1,0:T(8,128)S(1)}, u32[]{:S(2)}, u32[]{:S(2)}) %collective-permute-start.7) | collective-permute-done | bytes 69664 | tf_op jit(solution)/shard_map/ppermute | solution.py:486
  35.5 0.1 collective-permute-start.10
  35.6 0.3 shard_map.90
  35.9 1.2 %collective-permute-start.8 = (f32[144,128]{1,0:T(8,128)S(1)}, f32[144,128]{1,0:T(8,128)S(1)}, u32[]{:S(2)}, u32[]{:S(2)}) collective-permute-start(f32[144,128]{1,0:T(8,128)S(1)} %pad_maximum_fusion.1), channel_id=1, source_target_pairs={{0,1},{1,0},{2,3},{3,2},{4,5},{5,4},{6,7},{7,6},{8,9},{9,8},{10,11... | collective-permute-start | bytes 221192 | tf_op jit(solution)/shard_map/ppermute | solution.py:486
  37.1 2.2 %collective-permute-start.9 = (f32[144,128]{1,0:T(8,128)S(1)}, f32[144,128]{1,0:T(8,128)S(1)}, u32[]{:S(2)}, u32[]{:S(2)}) collective-permute-start(f32[144,128]{1,0:T(8,128)S(1)} %pad_maximum_fusion.1), channel_id=1, source_target_pairs={{0,2},{1,3},{2,0},{3,1},{4,6},{5,7},{6,4},{7,5},{8,10},{9,11},{10,... | collective-permute-start | bytes 221192 | tf_op jit(solution)/shard_map/ppermute | solution.py:486
  39.4 1.5 %collective-permute-done.10 = f32[144,128]{1,0:T(8,128)S(1)} collective-permute-done((f32[144,128]{1,0:T(8,128)S(1)}, f32[144,128]{1,0:T(8,128)S(1)}, u32[]{:S(2)}, u32[]{:S(2)}) %collective-permute-start.10) | collective-permute-done | bytes 73760 | tf_op jit(solution)/shard_map/ppermute | solution.py:486
  40.9 0.8 %collective-permute-done.9 = f32[144,128]{1,0:T(8,128)S(1)} collective-permute-done((f32[144,128]{1,0:T(8,128)S(1)}, f32[144,128]{1,0:T(8,128)S(1)}, u32[]{:S(2)}, u32[]{:S(2)}) %collective-permute-start.9) | collective-permute-done | bytes 73760 | tf_op jit(solution)/shard_map/ppermute | solution.py:486
  41.7 0.0 collective-permute-done.8
  41.7 2.0 %shard_map.89.mean_ref = f32[4,128,128]{2,1,0:T(8,128)S(1)} custom-call(f32[4,128,128]{2,1,0:T(8,128)S(1)} %pad_maximum_fusion.refs_0_, f32[9,4,128,128]{3,2,1,0:T(8,128)S(1)} %get-tuple-element.28.refs_1_), custom_call_target="tpu_custom_call" | custom-call | flops 8192000 | bytes 1048576 | tf_op jit(solution)/shard_map/pallas_call | solution.py:492
  43.8 0.1 collective-permute-start.11
  43.9 1.7 %shard_map.91 = (f32[4,128,512]{2,1,0:T(8,128)}, f32[1,256]{1,0:T(1,128)S(1)}) custom-call(s32[4]{0:T(128)S(1)} %get-tuple-element.20.rank_ref.refs_0_, f32[4,128,128]{2,1,0:T(8,128)S(1)} %shard_map.89.mean_ref, f32[4,128,512]{2,1,0:T(8,128)S(1)} %get-tuple-element.31.stepped_ref.refs_6_, bf16[3072,256]{1,0:T(8,128)(2,1)S(1)} %get-tuple-element.29.column_ref.refs_2_, ...), custom_call_target="tpu_custom_call" | custom-call | flops 4096000 | bytes 1048576 | tf_op jit(solution)/shard_map/pallas_call | solution.py:492
  45.6 0.0 collective-permute-done.11.refs_1_
  45.6 1.8 %shard_map.92 = (f32[4,128,512]{2,1,0:T(8,128)}, f32[2,2,256]{2,1,0:T(2,128)}, f32[2,256]{1,0:T(2,128)}) custom-call(s32[4]{0:T(128)S(1)} %get-tuple-element.20.rank_ref.refs_0_, f32[4,128,128]{2,1,0:T(8,128)S(1)} %collective-permute-done.11.refs_1_, bf16[3072,256]{1,0:T(8,128)(2,1)S(1)} %get-tuple-element.29.column_ref.refs_2_, ...), custom_call_target="tpu_custom_call", output_to_operand_aliasing={{0}: (7, {})} | custom-call | flops 4096000 | bytes 1048576 | tf_op jit(solution)/shard_map/pallas_call | solution.py:492
  (16 shorter events, 0.1 us)
Async XLA Ops:
  0.6 1.4 %copy-start = (f32[2,2,1,128,512]{4,3,2,1,0:T(8,128)S(1)}, f32[2,2,1,128,512]{4,3,2,1,0:T(8,128)}, u32[]{:S(2)}) copy-start(f32[2,2,1,128,512]{4,3,2,1,0:T(8,128)} %param.6) | copy-start | bytes 3145732
  3.8 4.0 %collective-permute-start.5 = (f32[6,4,128,128]{3,2,1,0:T(8,128)S(1)}, f32[6,4,128,128]{3,2,1,0:T(8,128)S(1)}, u32[]{:S(2)}, u32[]{:S(2)}) collective-permute-start(f32[6,4,128,128]{3,2,1,0:T(8,128)S(1)} %get-tuple-element.25), channel_id=1, source_target_pairs={{0,16},{1,17},{2,18},{3,19},{4,20},{5,21},{6,22},{7,23},{8,24},{9,... | collective-permute-start | bytes 4718600 | tf_op jit(solution)/shard_map/ppermute | solution.py:486
  4.4 3.4 %collective-permute-start = (f32[4,128,128]{2,1,0:T(8,128)S(1)}, f32[4,128,128]{2,1,0:T(8,128)S(1)}, u32[]{:S(2)}, u32[]{:S(2)}) collective-permute-start(f32[4,128,128]{2,1,0:T(8,128)S(1)} %get-tuple-element.23), channel_id=1, source_target_pairs={{0,16},{1,17},{2,18},{3,19},{4,20},{5,21},{6,22},{7,23},{8,24},{9,... | collective-permute-start | bytes 786440 | tf_op jit(solution)/shard_map/ppermute | solution.py:486
  7.8 19.7 %copy-start.1 = (f32[2,256]{1,0:T(2,128)S(1)}, f32[2,256]{1,0:T(2,128)}, u32[]{:S(2)}) copy-start(f32[2,256]{1,0:T(2,128)} %frac_ref.3) | copy-start | bytes 6148
  7.8 19.7 %copy-start.2 = (s32[256]{0:T(256)S(1)}, s32[256]{0:T(256)}, u32[]{:S(2)}) copy-start(s32[256]{0:T(256)} %param.10) | copy-start | bytes 3076
  13.2 14.3 %collective-permute-start.6 = (f32[2,4,128,128]{3,2,1,0:T(8,128)S(1)}, f32[2,4,128,128]{3,2,1,0:T(8,128)S(1)}, u32[]{:S(2)}, u32[]{:S(2)}) collective-permute-start(f32[2,4,128,128]{3,2,1,0:T(8,128)S(1)} %get-tuple-element.26.own_ref), channel_id=1, source_target_pairs={{0,16},{1,17},{2,18},{3,19},{4,20},{5,21},{6,22},{7,23},{8,24},{9,... | collective-permute-start | bytes 1572872 | tf_op jit(solution)/shard_map/ppermute | solution.py:486
  13.7 5.0 %collective-permute-start.1 = (f32[128,128]{1,0:T(8,128)S(1)}, f32[128,128]{1,0:T(8,128)S(1)}, u32[]{:S(2)}, u32[]{:S(2)}) collective-permute-start(f32[128,128]{1,0:T(8,128)S(1)} %get-tuple-element.42), channel_id=1, source_target_pairs={{0,1},{1,0},{2,3},{3,2},{4,5},{5,4},{6,7},{7,6},{8,9},{9,8},{10,11... | collective-permute-start | bytes 196616 | tf_op jit(solution)/shard_map/ppermute | solution.py:486
  16.4 4.6 %collective-permute-start.2 = (f32[128,128]{1,0:T(8,128)S(1)}, f32[128,128]{1,0:T(8,128)S(1)}, u32[]{:S(2)}, u32[]{:S(2)}) collective-permute-start(f32[128,128]{1,0:T(8,128)S(1)} %get-tuple-element.41), channel_id=1, source_target_pairs={{0,2},{1,3},{2,0},{3,1},{4,6},{5,7},{6,4},{7,5},{8,10},{9,11},{10,... | collective-permute-start | bytes 196616 | tf_op jit(solution)/shard_map/ppermute | solution.py:486
  18.0 5.2 %collective-permute-start.3 = (f32[128,128]{1,0:T(8,128)S(1)}, f32[128,128]{1,0:T(8,128)S(1)}, u32[]{:S(2)}, u32[]{:S(2)}) collective-permute-start(f32[128,128]{1,0:T(8,128)S(1)} %get-tuple-element.40), channel_id=1, source_target_pairs={{0,3},{1,2},{2,1},{3,0},{4,7},{5,6},{6,5},{7,4},{8,11},{9,10},{10,... | collective-permute-start | bytes 196616 | tf_op jit(solution)/shard_map/ppermute | solution.py:486
  23.2 4.3 %collective-permute-start.4 = (f32[128,128]{1,0:T(8,128)S(1)}, f32[128,128]{1,0:T(8,128)S(1)}, u32[]{:S(2)}, u32[]{:S(2)}) collective-permute-start(f32[128,128]{1,0:T(8,128)S(1)} %fusion.1), channel_id=1, source_target_pairs={{0,8},{1,9},{2,10},{3,11},{4,12},{5,13},{6,14},{7,15},{8,0},{9,1},... | collective-permute-start | bytes 196616 | tf_op jit(solution)/shard_map/ppermute | solution.py:486
  29.4 6.0 %collective-permute-start.7 = (f32[136,128]{1,0:T(8,128)S(1)}, f32[136,128]{1,0:T(8,128)S(1)}, u32[]{:S(2)}, u32[]{:S(2)}) collective-permute-start(f32[136,128]{1,0:T(8,128)S(1)} %pad_maximum_fusion.2), channel_id=1, source_target_pairs={{0,4},{1,5},{2,6},{3,7},{4,0},{5,1},{6,2},{7,3},{8,12},{9,13},{10,... | collective-permute-start | bytes 208904 | tf_op jit(solution)/shard_map/ppermute | solution.py:486
  35.5 5.4 %collective-permute-start.10 = (f32[144,128]{1,0:T(8,128)S(1)}, f32[144,128]{1,0:T(8,128)S(1)}, u32[]{:S(2)}, u32[]{:S(2)}) collective-permute-start(f32[144,128]{1,0:T(8,128)S(1)} %pad_maximum_fusion.1), channel_id=1, source_target_pairs={{0,3},{1,2},{2,1},{3,0},{4,7},{5,6},{6,5},{7,4},{8,11},{9,10},{10,... | collective-permute-start | bytes 221192 | tf_op jit(solution)/shard_map/ppermute | solution.py:486
  35.9 5.8 %collective-permute-start.8 = (f32[144,128]{1,0:T(8,128)S(1)}, f32[144,128]{1,0:T(8,128)S(1)}, u32[]{:S(2)}, u32[]{:S(2)}) collective-permute-start(f32[144,128]{1,0:T(8,128)S(1)} %pad_maximum_fusion.1), channel_id=1, source_target_pairs={{0,1},{1,0},{2,3},{3,2},{4,5},{5,4},{6,7},{7,6},{8,9},{9,8},{10,11... | collective-permute-start | bytes 221192 | tf_op jit(solution)/shard_map/ppermute | solution.py:486
  37.1 4.6 %collective-permute-start.9 = (f32[144,128]{1,0:T(8,128)S(1)}, f32[144,128]{1,0:T(8,128)S(1)}, u32[]{:S(2)}, u32[]{:S(2)}) collective-permute-start(f32[144,128]{1,0:T(8,128)S(1)} %pad_maximum_fusion.1), channel_id=1, source_target_pairs={{0,2},{1,3},{2,0},{3,1},{4,6},{5,7},{6,4},{7,5},{8,10},{9,11},{10,... | collective-permute-start | bytes 221192 | tf_op jit(solution)/shard_map/ppermute | solution.py:486
  43.8 1.8 %collective-permute-start.11 = (f32[4,128,128]{2,1,0:T(8,128)S(1)}, f32[4,128,128]{2,1,0:T(8,128)S(1)}, u32[]{:S(2)}, u32[]{:S(2)}) collective-permute-start(f32[4,128,128]{2,1,0:T(8,128)S(1)} %shard_map.89.mean_ref), channel_id=1, source_target_pairs={{0,16},{1,17},{2,18},{3,19},{4,20},{5,21},{6,22},{7,23},{8,24},{9,... | collective-permute-start | bytes 786440 | tf_op jit(solution)/shard_map/ppermute | solution.py:486

commit v8 on v6

--- a/solution.py
+++ b/solution.py
@@ -11,7 +11,7 @@
 STEPS = 6
 LANES = 128
 PAD = 8
-COPIES = 2
+COPIES = 1
 ALL_AXES = ("tile", "level", "member")
 VMEM = pl.BlockSpec(memory_space=pltpu.VMEM)
 SMEM = pl.BlockSpec(memory_space=pltpu.SMEM)
@@ -60,10 +60,7 @@
     members, fields, rows, tiles, _ = sizes
     core, mine, other = chunk_number()
     pairs = [(rank_hbm, rank_ref), (land_hbm, land_ref), (rank_hbm, rank_out)]
-    for plane in range(members * fields):
-        for part in range(COPIES):
-            at = pl.ds(part * rows // COPIES, rows // COPIES)
-            pairs.append((temp_hbm.at[plane, at], temp_ref.at[plane, at]))
+    pairs.append((temp_hbm, temp_ref))
     copies = [pltpu.make_async_copy(*pair, sem.at[number]) for number, pair in enumerate(pairs)]
     for copy in copies:
         copy.start()
@@ -508,7 +505,7 @@
             jax.ShapeDtypeStruct((tiles,), jnp.int32),
         ),
         inputs,
-        scratch=[pltpu.SMEM((tiles,), jnp.int32), pltpu.SemaphoreType.DMA((3 + planes * COPIES,))],
+        scratch=[pltpu.SMEM((tiles,), jnp.int32), pltpu.SemaphoreType.DMA((4,))],
         in_specs=[HBM] * 3,
     )
     arrived = exchange(send, None)

time: 45.9 us -> 45.8 us (level)
  no operation moved by 1% of the time
where the time goes in v8:
time: 45.8 us; the launch traced here: 45.6 us
  waiting for transfers between devices  16.2 us (35%)
  Pallas kernels  15.1 us (33%)
  starting transfers between devices  13.3 us (29%)
  between operations  0.83 us (2%)
    ppermute x12, waiting for transfers between devices, exchange(): return lax.ppermute(value, ALL_AXES, pairs)  16.2 us
    pallas_call x8, Pallas kernels, call(): pl.pallas_call(functools.partial(kernel, sizes), out_shape=out_shape, in_...  15.1 us
    ppermute x12, starting transfers between devices, exchange(): return lax.ppermute(value, ALL_AXES, pairs)  13.3 us
  transfers between devices with their start and end apart: 12, of which 9 were waited for; matrix products, arithmetic and copies ran while one was open for 0% of the time, Pallas kernels for 4%

profile of v8, /device:TPU:0, one launch (start us, length us, event | category | flops | bytes accessed | tf_op | source)
XLA Modules:
  0.0 45.6 jit_solution(2993088994270313435)
XLA Ops:
  0.6 0.0 copy-start
  0.6 1.5 %shard_map.85 = (f32[4,128,128]{2,1,0:T(8,128)S(1)}, f32[4,128,128]{2,1,0:T(8,128)S(1)}, f32[4,128,512]{2,1,0:T(8,128)S(1)}, s32[4,128]{1,0:T(4,128)S(1)}, s32[4]{0:T(128)S(1)}) custom-call(s32[4]{0:T(128)} %rank_hbm.1, f32[4,128,512]{2,1,0:T(8,128)} %bitcast.28, s32[4,128]{1,0:T(4,128)} %bitcast.30), custom_call_target="tpu_custom_call" | custom-call | flops 4096000 | bytes 1048576 | tf_op jit(solution)/shard_map/pallas_call | solution.py:478
  2.1 0.0 copy-done
  2.1 0.7 %shard_map.86 = f32[6,4,128,128]{3,2,1,0:T(8,128)S(1)} custom-call(s32[4]{0:T(128)S(1)} %get-tuple-element.19.rank_ref.refs_0_, f32[4,128,512]{2,1,0:T(8,128)S(1)} %get-tuple-element.22.temp_ref, f32[3,128,512]{2,1,0:T(8,128)S(1)} %copy-done, s32[4,128]{1,0:T(4,128)S(1)} %get-tuple-element.23.land_ref), custom_call_target="tpu_custom_call" | custom-call | flops 4096000 | bytes 1048576 | tf_op jit(solution)/shard_map/pallas_call | solution.py:478
  2.8 0.6 %collective-permute-start.5 = (f32[6,4,128,128]{3,2,1,0:T(8,128)S(1)}, f32[6,4,128,128]{3,2,1,0:T(8,128)S(1)}, u32[]{:S(2)}, u32[]{:S(2)}) collective-permute-start(f32[6,4,128,128]{3,2,1,0:T(8,128)S(1)} %shard_map.86), channel_id=1, source_target_pairs={{0,16},{1,17},{2,18},{3,19},{4,20},{5,21},{6,22},{7,23},{8,24},{9,... | collective-permute-start | bytes 4718600 | tf_op jit(solution)/shard_map/ppermute | solution.py:472
  3.3 0.1 collective-permute-start
  3.4 3.3 %collective-permute-done = f32[4,128,128]{2,1,0:T(8,128)S(1)} collective-permute-done((f32[4,128,128]{2,1,0:T(8,128)S(1)}, f32[4,128,128]{2,1,0:T(8,128)S(1)}, u32[]{:S(2)}, u32[]{:S(2)}) %collective-permute-start) | collective-permute-done | bytes 262176 | tf_op jit(solution)/shard_map/ppermute | solution.py:472
  6.8 0.0 copy-start.1
  6.8 0.0 copy-start.2
  6.8 0.0 collective-permute-done.5.pack_ref
  6.8 5.4 %shard_map.87 = (f32[9,4,128,128]{3,2,1,0:T(8,128)S(1)}, f32[2,4,128,128]{3,2,1,0:T(8,128)S(1)}) custom-call(s32[4]{0:T(128)S(1)} %get-tuple-element.19.rank_ref.refs_0_, f32[3,128,512]{2,1,0:T(8,128)S(1)} %copy-done, f32[4,128,512]{2,1,0:T(8,128)S(1)} %get-tuple-element.22.temp_ref, s32[4,128]{1,0:T(4,128)S(1)} %get-tuple-element.23.land_ref, ...), custom_call_target="tpu_custom_call" | custom-call | flops 24576000 | bytes 1048576 | tf_op jit(solution)/shard_map/pallas_call | solution.py:478
  12.2 0.4 collective-permute-start.6
  12.7 3.7 %collective-permute-start.3 = (f32[128,128]{1,0:T(8,128)S(1)}, f32[128,128]{1,0:T(8,128)S(1)}, u32[]{:S(2)}, u32[]{:S(2)}) collective-permute-start(f32[128,128]{1,0:T(8,128)S(1)} %get-tuple-element.38), channel_id=1, source_target_pairs={{0,3},{1,2},{2,1},{3,0},{4,7},{5,6},{6,5},{7,4},{8,11},{9,10},{10,... | collective-permute-start | bytes 196616 | tf_op jit(solution)/shard_map/ppermute | solution.py:472
  16.4 0.4 collective-permute-start.2
  16.8 0.2 collective-permute-start.1
  17.0 2.0 %collective-permute-done.3 = f32[128,128]{1,0:T(8,128)S(1)} collective-permute-done((f32[128,128]{1,0:T(8,128)S(1)}, f32[128,128]{1,0:T(8,128)S(1)}, u32[]{:S(2)}, u32[]{:S(2)}) %collective-permute-start.3) | collective-permute-done | bytes 65568 | tf_op jit(solution)/shard_map/ppermute | solution.py:472
  19.0 1.7 %collective-permute-done.2 = f32[128,128]{1,0:T(8,128)S(1)} collective-permute-done((f32[128,128]{1,0:T(8,128)S(1)}, f32[128,128]{1,0:T(8,128)S(1)}, u32[]{:S(2)}, u32[]{:S(2)}) %collective-permute-start.2) | collective-permute-done | bytes 65568 | tf_op jit(solution)/shard_map/ppermute | solution.py:472
  20.7 0.4 collective-permute-done.1
  21.1 1.6 %collective-permute-start.4 = (f32[128,128]{1,0:T(8,128)S(1)}, f32[128,128]{1,0:T(8,128)S(1)}, u32[]{:S(2)}, u32[]{:S(2)}) collective-permute-start(f32[128,128]{1,0:T(8,128)S(1)} %fusion.1), channel_id=1, source_target_pairs={{0,8},{1,9},{2,10},{3,11},{4,12},{5,13},{6,14},{7,15},{8,0},{9,1},... | collective-permute-start | bytes 196616 | tf_op jit(solution)/shard_map/ppermute | solution.py:472
  22.7 2.8 %collective-permute-done.4 = f32[128,128]{1,0:T(8,128)S(1)} collective-permute-done((f32[128,128]{1,0:T(8,128)S(1)}, f32[128,128]{1,0:T(8,128)S(1)}, u32[]{:S(2)}, u32[]{:S(2)}) %collective-permute-start.4) | collective-permute-done | bytes 65568 | tf_op jit(solution)/shard_map/ppermute | solution.py:472
  25.5 0.0 collective-permute-done.6.other_ref
  25.5 0.0 copy-done.1
  25.5 0.0 copy-done.2
  25.5 1.9 %shard_map.88 = (f32[4,128,512]{2,1,0:T(8,128)S(1)}, f32[8,128]{1,0:T(8,128)S(1)}) custom-call(s32[4]{0:T(128)S(1)} %get-tuple-element.19.rank_ref.refs_0_, f32[2,4,128,128]{3,2,1,0:T(8,128)S(1)} %get-tuple-element.24.own_ref, f32[2,4,128,128]{3,2,1,0:T(8,128)S(1)} %collective-permute-done.6.other_ref, s32[1,256]{1,0:T(1,128)S(1)} %bitcast.25, ...), custom_call_target="tpu_custom_call" | custom-call | flops 8192000 | bytes 1048576 | tf_op jit(solution)/shard_map/pallas_call | solution.py:478
  27.4 2.7 %collective-permute-start.7 = (f32[136,128]{1,0:T(8,128)S(1)}, f32[136,128]{1,0:T(8,128)S(1)}, u32[]{:S(2)}, u32[]{:S(2)}) collective-permute-start(f32[136,128]{1,0:T(8,128)S(1)} %pad_maximum_fusion.2), channel_id=1, source_target_pairs={{0,4},{1,5},{2,6},{3,7},{4,0},{5,1},{6,2},{7,3},{8,12},{9,13},{10,... | collective-permute-start | bytes 208904 | tf_op jit(solution)/shard_map/ppermute | solution.py:472
  30.0 2.6 %collective-permute-done.7 = f32[136,128]{1,0:T(8,128)S(1)} collective-permute-done((f32[136,128]{1,0:T(8,128)S(1)}, f32[136,128]{1,0:T(8,128)S(1)}, u32[]{:S(2)}, u32[]{:S(2)}) %collective-permute-start.7) | collective-permute-done | bytes 69664 | tf_op jit(solution)/shard_map/ppermute | solution.py:472
  32.7 1.8 %collective-permute-start.10 = (f32[144,128]{1,0:T(8,128)S(1)}, f32[144,128]{1,0:T(8,128)S(1)}, u32[]{:S(2)}, u32[]{:S(2)}) collective-permute-start(f32[144,128]{1,0:T(8,128)S(1)} %pad_maximum_fusion.1), channel_id=1, source_target_pairs={{0,3},{1,2},{2,1},{3,0},{4,7},{5,6},{6,5},{7,4},{8,11},{9,10},{10,... | collective-permute-start | bytes 221192 | tf_op jit(solution)/shard_map/ppermute | solution.py:472
  34.5 0.3 shard_map.90
  34.7 0.9 %collective-permute-start.9 = (f32[144,128]{1,0:T(8,128)S(1)}, f32[144,128]{1,0:T(8,128)S(1)}, u32[]{:S(2)}, u32[]{:S(2)}) collective-permute-start(f32[144,128]{1,0:T(8,128)S(1)} %pad_maximum_fusion.1), channel_id=1, source_target_pairs={{0,2},{1,3},{2,0},{3,1},{4,6},{5,7},{6,4},{7,5},{8,10},{9,11},{10,... | collective-permute-start | bytes 221192 | tf_op jit(solution)/shard_map/ppermute | solution.py:472
  35.6 1.0 %collective-permute-start.8 = (f32[144,128]{1,0:T(8,128)S(1)}, f32[144,128]{1,0:T(8,128)S(1)}, u32[]{:S(2)}, u32[]{:S(2)}) collective-permute-start(f32[144,128]{1,0:T(8,128)S(1)} %pad_maximum_fusion.1), channel_id=1, source_target_pairs={{0,1},{1,0},{2,3},{3,2},{4,5},{5,4},{6,7},{7,6},{8,9},{9,8},{10,11... | collective-permute-start | bytes 221192 | tf_op jit(solution)/shard_map/ppermute | solution.py:472
  36.6 1.4 %collective-permute-done.10 = f32[144,128]{1,0:T(8,128)S(1)} collective-permute-done((f32[144,128]{1,0:T(8,128)S(1)}, f32[144,128]{1,0:T(8,128)S(1)}, u32[]{:S(2)}, u32[]{:S(2)}) %collective-permute-start.10) | collective-permute-done | bytes 73760 | tf_op jit(solution)/shard_map/ppermute | solution.py:472
  38.0 1.1 %collective-permute-done.9 = f32[144,128]{1,0:T(8,128)S(1)} collective-permute-done((f32[144,128]{1,0:T(8,128)S(1)}, f32[144,128]{1,0:T(8,128)S(1)}, u32[]{:S(2)}, u32[]{:S(2)}) %collective-permute-start.9) | collective-permute-done | bytes 73760 | tf_op jit(solution)/shard_map/ppermute | solution.py:472
  39.2 0.8 %collective-permute-done.8 = f32[144,128]{1,0:T(8,128)S(1)} collective-permute-done((f32[144,128]{1,0:T(8,128)S(1)}, f32[144,128]{1,0:T(8,128)S(1)}, u32[]{:S(2)}, u32[]{:S(2)}) %collective-permute-start.8) | collective-permute-done | bytes 73760 | tf_op jit(solution)/shard_map/ppermute | solution.py:472
  40.0 2.0 %shard_map.89.mean_ref = f32[4,128,128]{2,1,0:T(8,128)S(1)} custom-call(f32[4,128,128]{2,1,0:T(8,128)S(1)} %pad_maximum_fusion.refs_0_, f32[9,4,128,128]{3,2,1,0:T(8,128)S(1)} %get-tuple-element.26.refs_1_), custom_call_target="tpu_custom_call" | custom-call | flops 8192000 | bytes 1048576 | tf_op jit(solution)/shard_map/pallas_call | solution.py:478
  42.0 0.1 collective-permute-start.11
  42.1 1.7 %shard_map.91 = (f32[4,128,512]{2,1,0:T(8,128)}, f32[1,256]{1,0:T(1,128)S(1)}) custom-call(s32[4]{0:T(128)S(1)} %get-tuple-element.19.rank_ref.refs_0_, f32[4,128,128]{2,1,0:T(8,128)S(1)} %shard_map.89.mean_ref, f32[4,128,512]{2,1,0:T(8,128)S(1)} %get-tuple-element.29.stepped_ref.refs_6_, bf16[3072,256]{1,0:T(8,128)(2,1)S(1)} %get-tuple-element.27.column_ref.refs_2_, ...), custom_call_target="tpu_custom_call" | custom-call | flops 4096000 | bytes 1048576 | tf_op jit(solution)/shard_map/pallas_call | solution.py:478
  43.8 0.0 collective-permute-done.11.refs_1_
  43.8 1.8 %shard_map.92 = (f32[4,128,512]{2,1,0:T(8,128)}, f32[2,2,256]{2,1,0:T(2,128)}, f32[2,256]{1,0:T(2,128)}) custom-call(s32[4]{0:T(128)S(1)} %get-tuple-element.19.rank_ref.refs_0_, f32[4,128,128]{2,1,0:T(8,128)S(1)} %collective-permute-done.11.refs_1_, bf16[3072,256]{1,0:T(8,128)(2,1)S(1)} %get-tuple-element.27.column_ref.refs_2_, ...), custom_call_target="tpu_custom_call", output_to_operand_aliasing={{0}: (7, {})} | custom-call | flops 4096000 | bytes 1048576 | tf_op jit(solution)/shard_map/pallas_call | solution.py:478
  (16 shorter events, 0.1 us)
Async XLA Ops:
  0.6 1.5 %copy-start = (f32[3,128,512]{2,1,0:T(8,128)S(1)}, f32[3,128,512]{2,1,0:T(8,128)}, u32[]{:S(2)}) copy-start(f32[3,128,512]{2,1,0:T(8,128)} %kappa_ref.3) | copy-start | bytes 2359300
  2.8 4.0 %collective-permute-start.5 = (f32[6,4,128,128]{3,2,1,0:T(8,128)S(1)}, f32[6,4,128,128]{3,2,1,0:T(8,128)S(1)}, u32[]{:S(2)}, u32[]{:S(2)}) collective-permute-start(f32[6,4,128,128]{3,2,1,0:T(8,128)S(1)} %shard_map.86), channel_id=1, source_target_pairs={{0,16},{1,17},{2,18},{3,19},{4,20},{5,21},{6,22},{7,23},{8,24},{9,... | collective-permute-start | bytes 4718600 | tf_op jit(solution)/shard_map/ppermute | solution.py:472
  3.3 3.4 %collective-permute-start = (f32[4,128,128]{2,1,0:T(8,128)S(1)}, f32[4,128,128]{2,1,0:T(8,128)S(1)}, u32[]{:S(2)}, u32[]{:S(2)}) collective-permute-start(f32[4,128,128]{2,1,0:T(8,128)S(1)} %get-tuple-element.21), channel_id=1, source_target_pairs={{0,16},{1,17},{2,18},{3,19},{4,20},{5,21},{6,22},{7,23},{8,24},{9,... | collective-permute-start | bytes 786440 | tf_op jit(solution)/shard_map/ppermute | solution.py:472
  6.8 18.7 %copy-start.1 = (f32[2,256]{1,0:T(2,128)S(1)}, f32[2,256]{1,0:T(2,128)}, u32[]{:S(2)}) copy-start(f32[2,256]{1,0:T(2,128)} %frac_ref.3) | copy-start | bytes 6148
  6.8 18.7 %copy-start.2 = (s32[256]{0:T(256)S(1)}, s32[256]{0:T(256)}, u32[]{:S(2)}) copy-start(s32[256]{0:T(256)} %param.10) | copy-start | bytes 3076
  12.2 13.2 %collective-permute-start.6 = (f32[2,4,128,128]{3,2,1,0:T(8,128)S(1)}, f32[2,4,128,128]{3,2,1,0:T(8,128)S(1)}, u32[]{:S(2)}, u32[]{:S(2)}) collective-permute-start(f32[2,4,128,128]{3,2,1,0:T(8,128)S(1)} %get-tuple-element.24.own_ref), channel_id=1, source_target_pairs={{0,16},{1,17},{2,18},{3,19},{4,20},{5,21},{6,22},{7,23},{8,24},{9,... | collective-permute-start | bytes 1572872 | tf_op jit(solution)/shard_map/ppermute | solution.py:472
  12.7 6.4 %collective-permute-start.3 = (f32[128,128]{1,0:T(8,128)S(1)}, f32[128,128]{1,0:T(8,128)S(1)}, u32[]{:S(2)}, u32[]{:S(2)}) collective-permute-start(f32[128,128]{1,0:T(8,128)S(1)} %get-tuple-element.38), channel_id=1, source_target_pairs={{0,3},{1,2},{2,1},{3,0},{4,7},{5,6},{6,5},{7,4},{8,11},{9,10},{10,... | collective-permute-start | bytes 196616 | tf_op jit(solution)/shard_map/ppermute | solution.py:472
  16.4 4.3 %collective-permute-start.2 = (f32[128,128]{1,0:T(8,128)S(1)}, f32[128,128]{1,0:T(8,128)S(1)}, u32[]{:S(2)}, u32[]{:S(2)}) collective-permute-start(f32[128,128]{1,0:T(8,128)S(1)} %get-tuple-element.39), channel_id=1, source_target_pairs={{0,2},{1,3},{2,0},{3,1},{4,6},{5,7},{6,4},{7,5},{8,10},{9,11},{10,... | collective-permute-start | bytes 196616 | tf_op jit(solution)/shard_map/ppermute | solution.py:472
  16.8 4.3 %collective-permute-start.1 = (f32[128,128]{1,0:T(8,128)S(1)}, f32[128,128]{1,0:T(8,128)S(1)}, u32[]{:S(2)}, u32[]{:S(2)}) collective-permute-start(f32[128,128]{1,0:T(8,128)S(1)} %get-tuple-element.40), channel_id=1, source_target_pairs={{0,1},{1,0},{2,3},{3,2},{4,5},{5,4},{6,7},{7,6},{8,9},{9,8},{10,11... | collective-permute-start | bytes 196616 | tf_op jit(solution)/shard_map/ppermute | solution.py:472
  21.1 4.3 %collective-permute-start.4 = (f32[128,128]{1,0:T(8,128)S(1)}, f32[128,128]{1,0:T(8,128)S(1)}, u32[]{:S(2)}, u32[]{:S(2)}) collective-permute-start(f32[128,128]{1,0:T(8,128)S(1)} %fusion.1), channel_id=1, source_target_pairs={{0,8},{1,9},{2,10},{3,11},{4,12},{5,13},{6,14},{7,15},{8,0},{9,1},... | collective-permute-start | bytes 196616 | tf_op jit(solution)/shard_map/ppermute | solution.py:472
  27.4 5.3 %collective-permute-start.7 = (f32[136,128]{1,0:T(8,128)S(1)}, f32[136,128]{1,0:T(8,128)S(1)}, u32[]{:S(2)}, u32[]{:S(2)}) collective-permute-start(f32[136,128]{1,0:T(8,128)S(1)} %pad_maximum_fusion.2), channel_id=1, source_target_pairs={{0,4},{1,5},{2,6},{3,7},{4,0},{5,1},{6,2},{7,3},{8,12},{9,13},{10,... | collective-permute-start | bytes 208904 | tf_op jit(solution)/shard_map/ppermute | solution.py:472
  32.7 5.3 %collective-permute-start.10 = (f32[144,128]{1,0:T(8,128)S(1)}, f32[144,128]{1,0:T(8,128)S(1)}, u32[]{:S(2)}, u32[]{:S(2)}) collective-permute-start(f32[144,128]{1,0:T(8,128)S(1)} %pad_maximum_fusion.1), channel_id=1, source_target_pairs={{0,3},{1,2},{2,1},{3,0},{4,7},{5,6},{6,5},{7,4},{8,11},{9,10},{10,... | collective-permute-start | bytes 221192 | tf_op jit(solution)/shard_map/ppermute | solution.py:472
  34.7 4.4 %collective-permute-start.9 = (f32[144,128]{1,0:T(8,128)S(1)}, f32[144,128]{1,0:T(8,128)S(1)}, u32[]{:S(2)}, u32[]{:S(2)}) collective-permute-start(f32[144,128]{1,0:T(8,128)S(1)} %pad_maximum_fusion.1), channel_id=1, source_target_pairs={{0,2},{1,3},{2,0},{3,1},{4,6},{5,7},{6,4},{7,5},{8,10},{9,11},{10,... | collective-permute-start | bytes 221192 | tf_op jit(solution)/shard_map/ppermute | solution.py:472
  35.6 4.4 %collective-permute-start.8 = (f32[144,128]{1,0:T(8,128)S(1)}, f32[144,128]{1,0:T(8,128)S(1)}, u32[]{:S(2)}, u32[]{:S(2)}) collective-permute-start(f32[144,128]{1,0:T(8,128)S(1)} %pad_maximum_fusion.1), channel_id=1, source_target_pairs={{0,1},{1,0},{2,3},{3,2},{4,5},{5,4},{6,7},{7,6},{8,9},{9,8},{10,11... | collective-permute-start | bytes 221192 | tf_op jit(solution)/shard_map/ppermute | solution.py:472
  42.0 1.8 %collective-permute-start.11 = (f32[4,128,128]{2,1,0:T(8,128)S(1)}, f32[4,128,128]{2,1,0:T(8,128)S(1)}, u32[]{:S(2)}, u32[]{:S(2)}) collective-permute-start(f32[4,128,128]{2,1,0:T(8,128)S(1)} %shard_map.89.mean_ref), channel_id=1, source_target_pairs={{0,16},{1,17},{2,18},{3,19},{4,20},{5,21},{6,22},{7,23},{8,24},{9,... | collective-permute-start | bytes 786440 | tf_op jit(solution)/shard_map/ppermute | solution.py:472

commit v9 on v8

--- a/solution.py
+++ b/solution.py
@@ -18,6 +18,7 @@
 HBM = pl.BlockSpec(memory_space=pltpu.HBM)
 HIGHEST = lax.Precision.HIGHEST
 PARAMS = pltpu.CompilerParams(vmem_limit_bytes=20 << 20)
+STEP_PARAMS = pltpu.CompilerParams(vmem_limit_bytes=20 << 20)
 
 
 def chunk_number():
@@ -474,7 +475,7 @@
     def struct(*shape):
         return jax.ShapeDtypeStruct(shape, jnp.float32)
 
-    def call(kernel, out_shape, operands, scratch=(), cycles=1000, in_specs=None, out_specs=None, aliases={}):
+    def call(name, kernel, out_shape, operands, scratch=(), cycles=1000, in_specs=None, out_specs=None, aliases={}):
         return pl.pallas_call(
             functools.partial(kernel, sizes),
             out_shape=out_shape,
@@ -482,7 +483,7 @@
             out_specs=out_specs or jax.tree.map(lambda _: VMEM, out_shape),
             scratch_shapes=list(scratch),
             input_output_aliases=aliases,
-            compiler_params=PARAMS,
+            compiler_params=STEP_PARAMS if name == "steps" else PARAMS,
             cost_estimate=pl.CostEstimate(flops=cycles * 4096, bytes_accessed=1 << 20, transcendentals=0),
         )(*operands)
 
@@ -496,7 +497,7 @@
 
     inputs = tuple(pltpu.with_memory_space_constraint(x, pltpu.HBM) for x in (wet_rank, temp, land))
     send, keep, temp, land, rank = call(
-        sums_kernel,
+        "sums", sums_kernel,
         (
             struct(slots, rows, LANES),
             struct(slots, rows, LANES),
@@ -509,7 +510,7 @@
         in_specs=[HBM] * 3,
     )
     arrived = exchange(send, None)
-    pack = call(pack_kernel, struct(fields + 4, slots, rows, LANES), (rank, temp, diffusivity, land))
+    pack = call("pack", pack_kernel, struct(fields + 4, slots, rows, LANES), (rank, temp, diffusivity, land))
     packed = exchange(pack, None)
     total = keep + arrived
     got = [exchange(total[k], masks[k]) for k in (1, 2, 3)]
@@ -517,12 +518,12 @@
 
     face = pltpu.VMEM((4, slots, rows + 2 * PAD, LANES), jnp.float32)
     weights, own = call(
-        member_kernel, (struct(9, slots, rows, LANES), struct(fields, slots, rows, LANES)),
+        "steps", member_kernel, (struct(9, slots, rows, LANES), struct(fields, slots, rows, LANES)),
         (rank, diffusivity, temp, land, packed), [halo(fields), face, face], cycles=6000,
     )
     other = exchange(own, None)
     stepped, seen = call(
-        observe_kernel, (struct(planes, rows, columns), struct(planes * count // LANES, LANES)),
+        "observe", observe_kernel, (struct(planes, rows, columns), struct(planes * count // LANES, LANES)),
         (rank, own, other, cell, obs_frac), cycles=2000,
     )
 
@@ -542,16 +543,16 @@
     def step_mean(sizes, *refs):
         mean_kernel(sizes, samples, *refs)
 
-    own_mean = call(step_mean, struct(slots, rows, LANES), (gathered, weights), [halo(1)], cycles=2000)
+    own_mean = call("mean", step_mean, struct(slots, rows, LANES), (gathered, weights), [halo(1)], cycles=2000)
     other_mean = exchange(own_mean, None)
     column_picks, row_picks = call(
-        picks_kernel,
+        "picks", picks_kernel,
         (jax.ShapeDtypeStruct((6 * columns, count), jnp.bfloat16), struct(rows, count)), (cell, obs_frac),
     )
     plane_scratch = pltpu.VMEM((members, rows, columns), jnp.float32)
     whole_scratch = pltpu.VMEM((rows, columns), jnp.float32)
     started, own_seen = call(
-        own_field_kernel, (struct(planes, rows, columns), struct(1, count)),
+        "own_field", own_field_kernel, (struct(planes, rows, columns), struct(1, count)),
         (rank, own_mean, stepped, column_picks, row_picks),
         [plane_scratch, whole_scratch, pltpu.SemaphoreType.DMA((members * COPIES,))], out_specs=(HBM, VMEM),
     )
@@ -561,7 +562,7 @@
 
     operands = (rank, other_mean, column_picks, row_picks, own_seen, seen, stepped, started)
     field, anomaly, variance = call(
-        last_kernel,
+        "recentre", last_kernel,
         (struct(planes, rows, columns), struct(members, fields, count), struct(fields, count)),
         operands,
         [

time: 45.8 us -> 45.8 us (level)
  no operation moved by 1% of the time
where the time goes in v9:
time: 45.8 us; the launch traced here: 45.6 us
  waiting for transfers between devices  16.2 us (35%)
  Pallas kernels  15.1 us (33%)
  starting transfers between devices  13.3 us (29%)
  between operations  0.83 us (2%)
    ppermute x12, waiting for transfers between devices, exchange(): return lax.ppermute(value, ALL_AXES, pairs)  16.2 us
    pallas_call x8, Pallas kernels, call(): pl.pallas_call(functools.partial(kernel, sizes), out_shape=out_shape, in_...  15.1 us
    ppermute x12, starting transfers between devices, exchange(): return lax.ppermute(value, ALL_AXES, pairs)  13.3 us
  transfers between devices with their start and end apart: 12, of which 9 were waited for; matrix products, arithmetic and copies ran while one was open for 0% of the time, Pallas kernels for 4%

profile of v9, /device:TPU:0, one launch (start us, length us, event | category | flops | bytes accessed | tf_op | source)
XLA Modules:
  0.0 45.6 jit_solution(2993088994270313435)
XLA Ops:
  0.6 0.0 copy-start
  0.6 1.5 %shard_map.85 = (f32[4,128,128]{2,1,0:T(8,128)S(1)}, f32[4,128,128]{2,1,0:T(8,128)S(1)}, f32[4,128,512]{2,1,0:T(8,128)S(1)}, s32[4,128]{1,0:T(4,128)S(1)}, s32[4]{0:T(128)S(1)}) custom-call(s32[4]{0:T(128)} %rank_hbm.1, f32[4,128,512]{2,1,0:T(8,128)} %bitcast.28, s32[4,128]{1,0:T(4,128)} %bitcast.30), custom_call_target="tpu_custom_call" | custom-call | flops 4096000 | bytes 1048576 | tf_op jit(solution)/shard_map/pallas_call | solution.py:479
  2.1 0.0 copy-done
  2.1 0.7 %shard_map.86 = f32[6,4,128,128]{3,2,1,0:T(8,128)S(1)} custom-call(s32[4]{0:T(128)S(1)} %get-tuple-element.19.rank_ref.refs_0_, f32[4,128,512]{2,1,0:T(8,128)S(1)} %get-tuple-element.22.temp_ref, f32[3,128,512]{2,1,0:T(8,128)S(1)} %copy-done, s32[4,128]{1,0:T(4,128)S(1)} %get-tuple-element.23.land_ref), custom_call_target="tpu_custom_call" | custom-call | flops 4096000 | bytes 1048576 | tf_op jit(solution)/shard_map/pallas_call | solution.py:479
  2.8 0.6 %collective-permute-start.5 = (f32[6,4,128,128]{3,2,1,0:T(8,128)S(1)}, f32[6,4,128,128]{3,2,1,0:T(8,128)S(1)}, u32[]{:S(2)}, u32[]{:S(2)}) collective-permute-start(f32[6,4,128,128]{3,2,1,0:T(8,128)S(1)} %shard_map.86), channel_id=1, source_target_pairs={{0,16},{1,17},{2,18},{3,19},{4,20},{5,21},{6,22},{7,23},{8,24},{9,... | collective-permute-start | bytes 4718600 | tf_op jit(solution)/shard_map/ppermute | solution.py:473
  3.3 0.1 collective-permute-start
  3.4 3.3 %collective-permute-done = f32[4,128,128]{2,1,0:T(8,128)S(1)} collective-permute-done((f32[4,128,128]{2,1,0:T(8,128)S(1)}, f32[4,128,128]{2,1,0:T(8,128)S(1)}, u32[]{:S(2)}, u32[]{:S(2)}) %collective-permute-start) | collective-permute-done | bytes 262176 | tf_op jit(solution)/shard_map/ppermute | solution.py:473
  6.8 0.0 copy-start.1
  6.8 0.0 copy-start.2
  6.8 0.0 collective-permute-done.5.pack_ref
  6.8 5.4 %shard_map.87 = (f32[9,4,128,128]{3,2,1,0:T(8,128)S(1)}, f32[2,4,128,128]{3,2,1,0:T(8,128)S(1)}) custom-call(s32[4]{0:T(128)S(1)} %get-tuple-element.19.rank_ref.refs_0_, f32[3,128,512]{2,1,0:T(8,128)S(1)} %copy-done, f32[4,128,512]{2,1,0:T(8,128)S(1)} %get-tuple-element.22.temp_ref, s32[4,128]{1,0:T(4,128)S(1)} %get-tuple-element.23.land_ref, ...), custom_call_target="tpu_custom_call" | custom-call | flops 24576000 | bytes 1048576 | tf_op jit(solution)/shard_map/pallas_call | solution.py:479
  12.2 0.4 collective-permute-start.6
  12.7 3.7 %collective-permute-start.3 = (f32[128,128]{1,0:T(8,128)S(1)}, f32[128,128]{1,0:T(8,128)S(1)}, u32[]{:S(2)}, u32[]{:S(2)}) collective-permute-start(f32[128,128]{1,0:T(8,128)S(1)} %get-tuple-element.38), channel_id=1, source_target_pairs={{0,3},{1,2},{2,1},{3,0},{4,7},{5,6},{6,5},{7,4},{8,11},{9,10},{10,... | collective-permute-start | bytes 196616 | tf_op jit(solution)/shard_map/ppermute | solution.py:473
  16.4 0.4 collective-permute-start.2
  16.8 0.2 collective-permute-start.1
  17.0 2.0 %collective-permute-done.3 = f32[128,128]{1,0:T(8,128)S(1)} collective-permute-done((f32[128,128]{1,0:T(8,128)S(1)}, f32[128,128]{1,0:T(8,128)S(1)}, u32[]{:S(2)}, u32[]{:S(2)}) %collective-permute-start.3) | collective-permute-done | bytes 65568 | tf_op jit(solution)/shard_map/ppermute | solution.py:473
  19.0 1.7 %collective-permute-done.2 = f32[128,128]{1,0:T(8,128)S(1)} collective-permute-done((f32[128,128]{1,0:T(8,128)S(1)}, f32[128,128]{1,0:T(8,128)S(1)}, u32[]{:S(2)}, u32[]{:S(2)}) %collective-permute-start.2) | collective-permute-done | bytes 65568 | tf_op jit(solution)/shard_map/ppermute | solution.py:473
  20.7 0.4 collective-permute-done.1
  21.1 1.6 %collective-permute-start.4 = (f32[128,128]{1,0:T(8,128)S(1)}, f32[128,128]{1,0:T(8,128)S(1)}, u32[]{:S(2)}, u32[]{:S(2)}) collective-permute-start(f32[128,128]{1,0:T(8,128)S(1)} %fusion.1), channel_id=1, source_target_pairs={{0,8},{1,9},{2,10},{3,11},{4,12},{5,13},{6,14},{7,15},{8,0},{9,1},... | collective-permute-start | bytes 196616 | tf_op jit(solution)/shard_map/ppermute | solution.py:473
  22.7 2.8 %collective-permute-done.4 = f32[128,128]{1,0:T(8,128)S(1)} collective-permute-done((f32[128,128]{1,0:T(8,128)S(1)}, f32[128,128]{1,0:T(8,128)S(1)}, u32[]{:S(2)}, u32[]{:S(2)}) %collective-permute-start.4) | collective-permute-done | bytes 65568 | tf_op jit(solution)/shard_map/ppermute | solution.py:473
  25.5 0.0 collective-permute-done.6.other_ref
  25.5 0.0 copy-done.1
  25.5 0.0 copy-done.2
  25.5 1.9 %shard_map.88 = (f32[4,128,512]{2,1,0:T(8,128)S(1)}, f32[8,128]{1,0:T(8,128)S(1)}) custom-call(s32[4]{0:T(128)S(1)} %get-tuple-element.19.rank_ref.refs_0_, f32[2,4,128,128]{3,2,1,0:T(8,128)S(1)} %get-tuple-element.24.own_ref, f32[2,4,128,128]{3,2,1,0:T(8,128)S(1)} %collective-permute-done.6.other_ref, s32[1,256]{1,0:T(1,128)S(1)} %bitcast.25, ...), custom_call_target="tpu_custom_call" | custom-call | flops 8192000 | bytes 1048576 | tf_op jit(solution)/shard_map/pallas_call | solution.py:479
  27.4 2.7 %collective-permute-start.7 = (f32[136,128]{1,0:T(8,128)S(1)}, f32[136,128]{1,0:T(8,128)S(1)}, u32[]{:S(2)}, u32[]{:S(2)}) collective-permute-start(f32[136,128]{1,0:T(8,128)S(1)} %pad_maximum_fusion.2), channel_id=1, source_target_pairs={{0,4},{1,5},{2,6},{3,7},{4,0},{5,1},{6,2},{7,3},{8,12},{9,13},{10,... | collective-permute-start | bytes 208904 | tf_op jit(solution)/shard_map/ppermute | solution.py:473
  30.0 2.6 %collective-permute-done.7 = f32[136,128]{1,0:T(8,128)S(1)} collective-permute-done((f32[136,128]{1,0:T(8,128)S(1)}, f32[136,128]{1,0:T(8,128)S(1)}, u32[]{:S(2)}, u32[]{:S(2)}) %collective-permute-start.7) | collective-permute-done | bytes 69664 | tf_op jit(solution)/shard_map/ppermute | solution.py:473
  32.7 1.8 %collective-permute-start.10 = (f32[144,128]{1,0:T(8,128)S(1)}, f32[144,128]{1,0:T(8,128)S(1)}, u32[]{:S(2)}, u32[]{:S(2)}) collective-permute-start(f32[144,128]{1,0:T(8,128)S(1)} %pad_maximum_fusion.1), channel_id=1, source_target_pairs={{0,3},{1,2},{2,1},{3,0},{4,7},{5,6},{6,5},{7,4},{8,11},{9,10},{10,... | collective-permute-start | bytes 221192 | tf_op jit(solution)/shard_map/ppermute | solution.py:473
  34.5 0.3 shard_map.90
  34.7 0.9 %collective-permute-start.9 = (f32[144,128]{1,0:T(8,128)S(1)}, f32[144,128]{1,0:T(8,128)S(1)}, u32[]{:S(2)}, u32[]{:S(2)}) collective-permute-start(f32[144,128]{1,0:T(8,128)S(1)} %pad_maximum_fusion.1), channel_id=1, source_target_pairs={{0,2},{1,3},{2,0},{3,1},{4,6},{5,7},{6,4},{7,5},{8,10},{9,11},{10,... | collective-permute-start | bytes 221192 | tf_op jit(solution)/shard_map/ppermute | solution.py:473
  35.6 1.0 %collective-permute-start.8 = (f32[144,128]{1,0:T(8,128)S(1)}, f32[144,128]{1,0:T(8,128)S(1)}, u32[]{:S(2)}, u32[]{:S(2)}) collective-permute-start(f32[144,128]{1,0:T(8,128)S(1)} %pad_maximum_fusion.1), channel_id=1, source_target_pairs={{0,1},{1,0},{2,3},{3,2},{4,5},{5,4},{6,7},{7,6},{8,9},{9,8},{10,11... | collective-permute-start | bytes 221192 | tf_op jit(solution)/shard_map/ppermute | solution.py:473
  36.6 1.4 %collective-permute-done.10 = f32[144,128]{1,0:T(8,128)S(1)} collective-permute-done((f32[144,128]{1,0:T(8,128)S(1)}, f32[144,128]{1,0:T(8,128)S(1)}, u32[]{:S(2)}, u32[]{:S(2)}) %collective-permute-start.10) | collective-permute-done | bytes 73760 | tf_op jit(solution)/shard_map/ppermute | solution.py:473
  38.0 1.1 %collective-permute-done.9 = f32[144,128]{1,0:T(8,128)S(1)} collective-permute-done((f32[144,128]{1,0:T(8,128)S(1)}, f32[144,128]{1,0:T(8,128)S(1)}, u32[]{:S(2)}, u32[]{:S(2)}) %collective-permute-start.9) | collective-permute-done | bytes 73760 | tf_op jit(solution)/shard_map/ppermute | solution.py:473
  39.2 0.8 %collective-permute-done.8 = f32[144,128]{1,0:T(8,128)S(1)} collective-permute-done((f32[144,128]{1,0:T(8,128)S(1)}, f32[144,128]{1,0:T(8,128)S(1)}, u32[]{:S(2)}, u32[]{:S(2)}) %collective-permute-start.8) | collective-permute-done | bytes 73760 | tf_op jit(solution)/shard_map/ppermute | solution.py:473
  40.0 2.0 %shard_map.89.mean_ref = f32[4,128,128]{2,1,0:T(8,128)S(1)} custom-call(f32[4,128,128]{2,1,0:T(8,128)S(1)} %pad_maximum_fusion.refs_0_, f32[9,4,128,128]{3,2,1,0:T(8,128)S(1)} %get-tuple-element.26.refs_1_), custom_call_target="tpu_custom_call" | custom-call | flops 8192000 | bytes 1048576 | tf_op jit(solution)/shard_map/pallas_call | solution.py:479
  42.0 0.1 collective-permute-start.11
  42.1 1.7 %shard_map.91 = (f32[4,128,512]{2,1,0:T(8,128)}, f32[1,256]{1,0:T(1,128)S(1)}) custom-call(s32[4]{0:T(128)S(1)} %get-tuple-element.19.rank_ref.refs_0_, f32[4,128,128]{2,1,0:T(8,128)S(1)} %shard_map.89.mean_ref, f32[4,128,512]{2,1,0:T(8,128)S(1)} %get-tuple-element.29.stepped_ref.refs_6_, bf16[3072,256]{1,0:T(8,128)(2,1)S(1)} %get-tuple-element.27.column_ref.refs_2_, ...), custom_call_target="tpu_custom_call" | custom-call | flops 4096000 | bytes 1048576 | tf_op jit(solution)/shard_map/pallas_call | solution.py:479
  43.8 0.0 collective-permute-done.11.refs_1_
  43.8 1.8 %shard_map.92 = (f32[4,128,512]{2,1,0:T(8,128)}, f32[2,2,256]{2,1,0:T(2,128)}, f32[2,256]{1,0:T(2,128)}) custom-call(s32[4]{0:T(128)S(1)} %get-tuple-element.19.rank_ref.refs_0_, f32[4,128,128]{2,1,0:T(8,128)S(1)} %collective-permute-done.11.refs_1_, bf16[3072,256]{1,0:T(8,128)(2,1)S(1)} %get-tuple-element.27.column_ref.refs_2_, ...), custom_call_target="tpu_custom_call", output_to_operand_aliasing={{0}: (7, {})} | custom-call | flops 4096000 | bytes 1048576 | tf_op jit(solution)/shard_map/pallas_call | solution.py:479
  (16 shorter events, 0.1 us)
Async XLA Ops:
  0.6 1.5 %copy-start = (f32[3,128,512]{2,1,0:T(8,128)S(1)}, f32[3,128,512]{2,1,0:T(8,128)}, u32[]{:S(2)}) copy-start(f32[3,128,512]{2,1,0:T(8,128)} %kappa_ref.3) | copy-start | bytes 2359300
  2.8 4.0 %collective-permute-start.5 = (f32[6,4,128,128]{3,2,1,0:T(8,128)S(1)}, f32[6,4,128,128]{3,2,1,0:T(8,128)S(1)}, u32[]{:S(2)}, u32[]{:S(2)}) collective-permute-start(f32[6,4,128,128]{3,2,1,0:T(8,128)S(1)} %shard_map.86), channel_id=1, source_target_pairs={{0,16},{1,17},{2,18},{3,19},{4,20},{5,21},{6,22},{7,23},{8,24},{9,... | collective-permute-start | bytes 4718600 | tf_op jit(solution)/shard_map/ppermute | solution.py:473
  3.3 3.4 %collective-permute-start = (f32[4,128,128]{2,1,0:T(8,128)S(1)}, f32[4,128,128]{2,1,0:T(8,128)S(1)}, u32[]{:S(2)}, u32[]{:S(2)}) collective-permute-start(f32[4,128,128]{2,1,0:T(8,128)S(1)} %get-tuple-element.21), channel_id=1, source_target_pairs={{0,16},{1,17},{2,18},{3,19},{4,20},{5,21},{6,22},{7,23},{8,24},{9,... | collective-permute-start | bytes 786440 | tf_op jit(solution)/shard_map/ppermute | solution.py:473
  6.8 18.7 %copy-start.1 = (f32[2,256]{1,0:T(2,128)S(1)}, f32[2,256]{1,0:T(2,128)}, u32[]{:S(2)}) copy-start(f32[2,256]{1,0:T(2,128)} %frac_ref.3) | copy-start | bytes 6148
  6.8 18.7 %copy-start.2 = (s32[256]{0:T(256)S(1)}, s32[256]{0:T(256)}, u32[]{:S(2)}) copy-start(s32[256]{0:T(256)} %param.10) | copy-start | bytes 3076
  12.2 13.2 %collective-permute-start.6 = (f32[2,4,128,128]{3,2,1,0:T(8,128)S(1)}, f32[2,4,128,128]{3,2,1,0:T(8,128)S(1)}, u32[]{:S(2)}, u32[]{:S(2)}) collective-permute-start(f32[2,4,128,128]{3,2,1,0:T(8,128)S(1)} %get-tuple-element.24.own_ref), channel_id=1, source_target_pairs={{0,16},{1,17},{2,18},{3,19},{4,20},{5,21},{6,22},{7,23},{8,24},{9,... | collective-permute-start | bytes 1572872 | tf_op jit(solution)/shard_map/ppermute | solution.py:473
  12.7 6.4 %collective-permute-start.3 = (f32[128,128]{1,0:T(8,128)S(1)}, f32[128,128]{1,0:T(8,128)S(1)}, u32[]{:S(2)}, u32[]{:S(2)}) collective-permute-start(f32[128,128]{1,0:T(8,128)S(1)} %get-tuple-element.38), channel_id=1, source_target_pairs={{0,3},{1,2},{2,1},{3,0},{4,7},{5,6},{6,5},{7,4},{8,11},{9,10},{10,... | collective-permute-start | bytes 196616 | tf_op jit(solution)/shard_map/ppermute | solution.py:473
  16.4 4.3 %collective-permute-start.2 = (f32[128,128]{1,0:T(8,128)S(1)}, f32[128,128]{1,0:T(8,128)S(1)}, u32[]{:S(2)}, u32[]{:S(2)}) collective-permute-start(f32[128,128]{1,0:T(8,128)S(1)} %get-tuple-element.39), channel_id=1, source_target_pairs={{0,2},{1,3},{2,0},{3,1},{4,6},{5,7},{6,4},{7,5},{8,10},{9,11},{10,... | collective-permute-start | bytes 196616 | tf_op jit(solution)/shard_map/ppermute | solution.py:473
  16.8 4.3 %collective-permute-start.1 = (f32[128,128]{1,0:T(8,128)S(1)}, f32[128,128]{1,0:T(8,128)S(1)}, u32[]{:S(2)}, u32[]{:S(2)}) collective-permute-start(f32[128,128]{1,0:T(8,128)S(1)} %get-tuple-element.40), channel_id=1, source_target_pairs={{0,1},{1,0},{2,3},{3,2},{4,5},{5,4},{6,7},{7,6},{8,9},{9,8},{10,11... | collective-permute-start | bytes 196616 | tf_op jit(solution)/shard_map/ppermute | solution.py:473
  21.1 4.3 %collective-permute-start.4 = (f32[128,128]{1,0:T(8,128)S(1)}, f32[128,128]{1,0:T(8,128)S(1)}, u32[]{:S(2)}, u32[]{:S(2)}) collective-permute-start(f32[128,128]{1,0:T(8,128)S(1)} %fusion.1), channel_id=1, source_target_pairs={{0,8},{1,9},{2,10},{3,11},{4,12},{5,13},{6,14},{7,15},{8,0},{9,1},... | collective-permute-start | bytes 196616 | tf_op jit(solution)/shard_map/ppermute | solution.py:473
  27.4 5.3 %collective-permute-start.7 = (f32[136,128]{1,0:T(8,128)S(1)}, f32[136,128]{1,0:T(8,128)S(1)}, u32[]{:S(2)}, u32[]{:S(2)}) collective-permute-start(f32[136,128]{1,0:T(8,128)S(1)} %pad_maximum_fusion.2), channel_id=1, source_target_pairs={{0,4},{1,5},{2,6},{3,7},{4,0},{5,1},{6,2},{7,3},{8,12},{9,13},{10,... | collective-permute-start | bytes 208904 | tf_op jit(solution)/shard_map/ppermute | solution.py:473
  32.7 5.3 %collective-permute-start.10 = (f32[144,128]{1,0:T(8,128)S(1)}, f32[144,128]{1,0:T(8,128)S(1)}, u32[]{:S(2)}, u32[]{:S(2)}) collective-permute-start(f32[144,128]{1,0:T(8,128)S(1)} %pad_maximum_fusion.1), channel_id=1, source_target_pairs={{0,3},{1,2},{2,1},{3,0},{4,7},{5,6},{6,5},{7,4},{8,11},{9,10},{10,... | collective-permute-start | bytes 221192 | tf_op jit(solution)/shard_map/ppermute | solution.py:473
  34.7 4.4 %collective-permute-start.9 = (f32[144,128]{1,0:T(8,128)S(1)}, f32[144,128]{1,0:T(8,128)S(1)}, u32[]{:S(2)}, u32[]{:S(2)}) collective-permute-start(f32[144,128]{1,0:T(8,128)S(1)} %pad_maximum_fusion.1), channel_id=1, source_target_pairs={{0,2},{1,3},{2,0},{3,1},{4,6},{5,7},{6,4},{7,5},{8,10},{9,11},{10,... | collective-permute-start | bytes 221192 | tf_op jit(solution)/shard_map/ppermute | solution.py:473
  35.6 4.4 %collective-permute-start.8 = (f32[144,128]{1,0:T(8,128)S(1)}, f32[144,128]{1,0:T(8,128)S(1)}, u32[]{:S(2)}, u32[]{:S(2)}) collective-permute-start(f32[144,128]{1,0:T(8,128)S(1)} %pad_maximum_fusion.1), channel_id=1, source_target_pairs={{0,1},{1,0},{2,3},{3,2},{4,5},{5,4},{6,7},{7,6},{8,9},{9,8},{10,11... | collective-permute-start | bytes 221192 | tf_op jit(solution)/shard_map/ppermute | solution.py:473
  42.0 1.8 %collective-permute-start.11 = (f32[4,128,128]{2,1,0:T(8,128)S(1)}, f32[4,128,128]{2,1,0:T(8,128)S(1)}, u32[]{:S(2)}, u32[]{:S(2)}) collective-permute-start(f32[4,128,128]{2,1,0:T(8,128)S(1)} %shard_map.89.mean_ref), channel_id=1, source_target_pairs={{0,16},{1,17},{2,18},{3,19},{4,20},{5,21},{6,22},{7,23},{8,24},{9,... | collective-permute-start | bytes 786440 | tf_op jit(solution)/shard_map/ppermute | solution.py:473
